TPU v7x, 32 devices: a whole 2x2x4 slice. The times are simulated.
32 devices in a mesh: dp: 8 (over z, y), fsdp: 4 (over x, core).
Axes of the slice: x: 2, y: 2, z: 4, core: 2. Of those that a mesh axis runs over, the one named last changes fastest.
Arguments:
- tokens: bfloat16 [32, 1024, 1024], P(('dp', 'fsdp')), may hold values from -6 to 6
- key_len: int32 [32], P(('dp', 'fsdp')), may hold values from 256 to 1024, as said below
- section: int32 [32], P(('dp', 'fsdp')), may hold values from 1 to 7
- params: float32 [12611584], P(('dp', 'fsdp'))
- first_moment: float32 [12611584], P(('dp', 'fsdp')), may hold values from -6 to 6
- second_moment: float32 [12611584], P(('dp', 'fsdp')), may hold values from 327 to 32768
- cotangent: bfloat16 [32, 1024, 1024], P(('dp', 'fsdp')), may hold values from -6 to 6
Outputs:
- block_out: bfloat16 [32, 1024, 1024], P(('dp', 'fsdp'))
- input_grad: bfloat16 [32, 1024, 1024], P(('dp', 'fsdp'))
- param_grad: float32 [12611584], P(('dp', 'fsdp'))
- new_params: float32 [12611584], P(('dp', 'fsdp'))
- new_first: float32 [12611584], P(('dp', 'fsdp'))
- new_second: float32 [12611584], P(('dp', 'fsdp'))
- section_grad: float32 [7, 4096], replicated
Inputs may be any that keep to these rules, and one draw needn't show every extreme that they name: Each item's keys are its first key_len frames; some item has exactly 1024.
All inputs are finite; a program needn't handle non-finite values.
Results may differ from a plain program's by a relative error of at most 0.014.
The roundings to bfloat16 on the way count: a program that leaves them out, or rounds other values in their place, can miss the bound.
Values may be sent and summed in bfloat16 or wider, within the bound.
No kernel may reach another device: no remote copies, remote signals or barrier semaphores. Data moves between devices by JAX's collectives and lax.ppermute only.
A program may use at most 384 MiB of HBM per device.

v0:
```python
import jax
import jax.numpy as jnp
from jax import lax
from jax.sharding import PartitionSpec as P

D = 1024
HEADS = 16
FF = 4096
SECTIONS = 7


beta_one = 0.9
beta_two = 0.95
adam_eps = 1e-08
learn_rate = 0.05
bias_one = 1.0 - 0.9**10
bias_two = 1.0 - 0.95**10


def adanorm(field, gain_rows, shift_rows):
    average = jnp.mean(field, -1, keepdims=True)
    centred = field - average
    spread = jnp.mean(centred * centred, -1, keepdims=True)
    return centred * lax.rsqrt(spread + 1e-05) * gain_rows + shift_rows


def unpack(flat):
    first = 3 * D * D
    second = first + D * D
    third = second + D * FF
    fourth = third + FF * D
    return (
        flat[:first].reshape(D, 3 * D),
        flat[first:second].reshape(D, D),
        flat[second:third].reshape(D, FF),
        flat[third:fourth].reshape(FF, D),
        flat[fourth:].reshape(SECTIONS, 4 * D),
    )


def dot_trans(left, right):
    return lax.dot_general(
        left, right, (((1,), (1,)), ((), ())), preferred_element_type=jnp.float32
    )


def dot_inner(left, right):
    return lax.dot_general(
        left, right, (((0,), (0,)), ((), ())), preferred_element_type=jnp.float32
    )


def masked_scores(query_block, keys_all, key_valid, score_scale):
    scores = (
        jnp.einsum("qhd,khd->hqk", query_block, keys_all, preferred_element_type=jnp.float32)
        * score_scale
    )
    return jnp.where(key_valid, scores, -1e30)


def attend_forward(operands):
    queries, keys_all, values, valid_count = operands
    frames = queries.shape[0]
    block_rows = min(512, frames)
    score_scale = queries.shape[2] ** (-0.5)
    key_valid = (jnp.arange(frames) < valid_count)[None, None, :]
    outputs = []
    totals = []
    for offset in range(0, frames, block_rows):
        scores = masked_scores(
            queries[offset : offset + block_rows], keys_all, key_valid, score_scale
        )
        row_max = jnp.max(scores, -1, keepdims=True)
        log_total = row_max + jnp.log(jnp.sum(jnp.exp(scores - row_max), -1, keepdims=True))
        softmax_w = jnp.exp(scores - log_total).astype(jnp.bfloat16)
        outputs.append(
            jnp.einsum(
                "hqk,khd->qhd", softmax_w, values, preferred_element_type=jnp.float32
            ).astype(jnp.bfloat16)
        )
        totals.append(log_total[..., 0])
    return (jnp.concatenate(outputs, 0), jnp.concatenate(totals, 1))


def attend_backward(operands):
    queries, keys_all, values, valid_count, log_totals, grad_mix = operands
    frames = queries.shape[0]
    block_rows = min(512, frames)
    score_scale = queries.shape[2] ** (-0.5)
    key_valid = (jnp.arange(frames) < valid_count)[None, None, :]
    grad_keys = jnp.zeros(keys_all.shape, jnp.float32)
    grad_values = jnp.zeros(values.shape, jnp.float32)
    grad_queries = []
    for offset in range(0, frames, block_rows):
        query_block = queries[offset : offset + block_rows]
        grad_block = grad_mix[offset : offset + block_rows]
        scores = masked_scores(query_block, keys_all, key_valid, score_scale)
        softmax_w = jnp.exp(scores - log_totals[:, offset : offset + block_rows, None])
        grad_probs = jnp.einsum(
            "qhd,khd->hqk", grad_block, values, preferred_element_type=jnp.float32
        )
        grad_values = grad_values + jnp.einsum(
            "hqk,qhd->khd",
            softmax_w.astype(jnp.bfloat16),
            grad_block,
            preferred_element_type=jnp.float32,
        )
        grad_scores = (
            softmax_w * (grad_probs - jnp.sum(softmax_w * grad_probs, -1, keepdims=True))
        ).astype(jnp.bfloat16)
        grad_queries.append(
            jnp.einsum("hqk,khd->qhd", grad_scores, keys_all, preferred_element_type=jnp.float32)
            * score_scale
        )
        grad_keys = (
            grad_keys
            + jnp.einsum(
                "hqk,qhd->khd", grad_scores, query_block, preferred_element_type=jnp.float32
            )
            * score_scale
        )
    return jnp.stack([jnp.concatenate(grad_queries, 0), grad_keys, grad_values], 1).astype(
        jnp.bfloat16
    )


def per_device(tokens, key_len, section, params, first_moment, second_moment, cotangent):
    item_count, frames, features = tokens.shape
    row_count = item_count * frames
    head_size = features // HEADS
    low_params = params.astype(jnp.bfloat16)
    gathered = lax.all_gather(low_params, ("dp", "fsdp"), axis=0, tiled=True)
    w_qkv, w_out, w_up, w_down, table = unpack(gathered)
    picker = (section[:, None] - 1 == jnp.arange(SECTIONS)[None, :]).astype(jnp.float32)
    modulation = jnp.dot(picker, table.astype(jnp.float32), precision=lax.Precision.HIGHEST)
    gain_one = modulation[:, None, 0:features]
    shift_one = modulation[:, None, features : 2 * features]
    gain_two = modulation[:, None, 2 * features : 3 * features]
    shift_two = modulation[:, None, 3 * features : 4 * features]
    inputs = tokens.astype(jnp.float32)
    normed_one, norm_one_back = jax.vjp(adanorm, inputs, gain_one, shift_one)
    low_one = normed_one.astype(jnp.bfloat16).reshape(row_count, features)
    qkv = jnp.dot(low_one, w_qkv, preferred_element_type=jnp.float32).astype(jnp.bfloat16)
    qkv = qkv.reshape(item_count, frames, 3, HEADS, head_size)
    queries = qkv[:, :, 0]
    keys_all = qkv[:, :, 1]
    values = qkv[:, :, 2]
    mixture, log_totals = lax.map(attend_forward, (queries, keys_all, values, key_len))
    mixture = mixture.reshape(row_count, features)
    attended = jnp.dot(mixture, w_out, preferred_element_type=jnp.float32)
    middle = inputs + attended.reshape(item_count, frames, features)
    normed_two, norm_two_back = jax.vjp(adanorm, middle, gain_two, shift_two)
    low_two = normed_two.astype(jnp.bfloat16).reshape(row_count, features)
    projected = jnp.dot(low_two, w_up, preferred_element_type=jnp.float32)
    activated, gelu_back = jax.vjp(jax.nn.gelu, projected)
    low_act = activated.astype(jnp.bfloat16)
    branch = jnp.dot(low_act, w_down, preferred_element_type=jnp.float32)
    block_out = (middle + branch.reshape(item_count, frames, features)).astype(jnp.bfloat16)
    regathered = lax.all_gather(low_params, ("dp", "fsdp"), axis=0, tiled=True)
    w_qkv, w_out, w_up, w_down, table = unpack(regathered)
    grad_y = cotangent.astype(jnp.float32)
    low_gy = cotangent.reshape(row_count, features)
    grad_down = dot_inner(low_act, low_gy)
    grad_act = dot_trans(low_gy, w_down)
    (grad_proj,) = gelu_back(grad_act)
    low_gp = grad_proj.astype(jnp.bfloat16)
    grad_up = dot_inner(low_two, low_gp)
    grad_norm_two = dot_trans(low_gp, w_up).reshape(item_count, frames, features)
    grad_mid_part, grad_gain_two, grad_shift_two = norm_two_back(grad_norm_two)
    grad_mid = grad_y + grad_mid_part
    low_gm = grad_mid.astype(jnp.bfloat16).reshape(row_count, features)
    grad_out_w = dot_inner(mixture, low_gm)
    grad_mix = (
        dot_trans(low_gm, w_out).astype(jnp.bfloat16).reshape(item_count, frames, HEADS, head_size)
    )
    grad_qkv = lax.map(attend_backward, (queries, keys_all, values, key_len, log_totals, grad_mix))
    grad_qkv = grad_qkv.reshape(row_count, 3 * features)
    grad_qkv_w = dot_inner(low_one, grad_qkv)
    grad_norm_one = dot_trans(grad_qkv, w_qkv).reshape(item_count, frames, features)
    grad_in_part, grad_gain_one, grad_shift_one = norm_one_back(grad_norm_one)
    input_grad = (grad_mid + grad_in_part).astype(jnp.bfloat16)
    per_item = jnp.concatenate(
        [grad_gain_one[:, 0], grad_shift_one[:, 0], grad_gain_two[:, 0], grad_shift_two[:, 0]], 1
    )
    grad_table = jnp.einsum("is,ic->sc", picker, per_item, precision=lax.Precision.HIGHEST)
    table_flat = grad_table.ravel()
    table_size = table_flat.shape[0]
    flat_grads = jnp.concatenate(
        [
            grad_qkv_w.ravel(),
            grad_out_w.ravel(),
            grad_up.ravel(),
            grad_down.ravel(),
            jnp.zeros((table_size,), jnp.float32),
        ]
    )
    table_start = flat_grads.shape[0] - table_size
    shard_size = params.shape[0]
    weight_part = lax.psum_scatter(
        lax.slice_in_dim(flat_grads, 0, lax.axis_size(("dp", "fsdp")) * shard_size, axis=0),
        ("dp", "fsdp"),
        scatter_dimension=0,
        tiled=True,
    )
    section_total = lax.psum(table_flat, ("dp", "fsdp"))
    padded = jnp.concatenate(
        [
            jnp.zeros((shard_size,), jnp.float32),
            section_total,
            jnp.zeros((shard_size,), jnp.float32),
        ]
    )
    slice_start = jnp.clip(
        lax.axis_index(("dp", "fsdp")) * shard_size - table_start + shard_size,
        0,
        table_size + shard_size,
    ).astype(jnp.int32)
    param_grad = weight_part + lax.dynamic_slice_in_dim(padded, slice_start, shard_size)
    section_grad = section_total.reshape(SECTIONS, 4 * features)
    new_first = beta_one * first_moment + (1.0 - beta_one) * param_grad
    new_second = beta_two * second_moment + (1.0 - beta_two) * param_grad * param_grad
    new_params = params - learn_rate * (new_first / bias_one) / (
        jnp.sqrt(new_second / bias_two) + adam_eps
    )
    return (block_out, input_grad, param_grad, new_params, new_first, new_second, section_grad)


def solution(mesh):
    in_specs = (
        P(("dp", "fsdp"), None, None),
        P(("dp", "fsdp")),
        P(("dp", "fsdp")),
        P(("dp", "fsdp")),
        P(("dp", "fsdp")),
        P(("dp", "fsdp")),
        P(("dp", "fsdp"), None, None),
    )
    out_specs = (
        P(("dp", "fsdp"), None, None),
        P(("dp", "fsdp"), None, None),
        P(("dp", "fsdp")),
        P(("dp", "fsdp")),
        P(("dp", "fsdp")),
        P(("dp", "fsdp")),
        P(),
    )
    return jax.shard_map(
        per_device, mesh=mesh, in_specs=in_specs, out_specs=out_specs, check_vma=False
    )
```

profile of v0, /device:TPU:1, one launch (start us, length us, event | category | flops | bytes accessed | tf_op | source)
XLA Modules:
  0.0 1802.5 jit_solution(13227924802509628226)
XLA Ops:
  28.2 268.3 %all-gather.3.cloned.1.call-done = bf16[32,1,394112]{2,1,0:T(2,128)(2,1)} async-done(((bf16[1,1,394112]{2,1,0:T(2,128)(2,1)}), bf16[32,1,394112]{2,1,0:T(2,128)(2,1)}) %all-gather.3.cloned.1.call-update) | async-done | bytes 25223184 | tf_op jit(solution)/shard_map/all_gather | solution.py:132
  296.5 138.9 %reduce.14 = bf16[32,394112]{1,0:T(8,128)(2,1)} reduce(bf16[32,1,394112]{2,1,0:T(2,128)(2,1)} %all-gather.3.cloned.1.call-done, bf16[]{:T(256)} %constant.127), dimensions={1}, to_apply=%all-gather.reduce_sub_computation | reduce | bytes 50446336 | tf_op jit(solution)/shard_map/all_gather | solution.py:132
  435.4 59.6 %reshape.334 = bf16[12611584]{0:T(1024)(128)(2,1)} reshape(bf16[32,394112]{1,0:T(8,128)(2,1)} %reduce.14) | data formatting | bytes 50446336
  501.5 11.3 fusion.79
  512.8 10.3 reshape.314
  523.4 12.2 convolution_convert_fusion
  544.2 15.4 fusion
  559.6 25.3 %exponential_reduce_fusion.1 = (f32[16,512]{1,0:T(8,128)S(1)}, f32[16,512]{1,0:T(8,128)S(1)}, f32[16,512,1024]{2,1,0:T(8,128)}) fusion(f32[16,512,1024]{2,1,0:T(8,128)} %get-tuple-element.100, f32[16,512]{1,0:T(8,128)S(1)} %get-tuple-element.99, pred[1024]{0:T(1024)(128)(4,1)S(1)} %iota_compare_fusion, bf16[1,1024,3,16,64]{1,4,3,2,0:T(8,128)(2,1)S(1)} %bitcast.161), kind=kOutput, calls=%fused_computation.8 | convolution fusion | flops 1132445696 | bytes 70353920 | tf_op jit(solution)/shard_map/while/body/eval_jaxpr/qhd,khd->hqk/dot_general | solution.py:55
  584.8 14.6 exponential_reduce_fusion
  599.5 14.9 fusion.43
  614.4 15.8 fusion.42
  632.5 13.3 slice.134
  645.8 13.5 slice.132
  668.0 13.2 fusion.74
  681.2 22.8 %fusion.10 = bf16[1024,4096]{1,0:T(8,128)(2,1)} fusion(f32[1024,4096]{1,0:T(8,128)} %fusion.74, bf16[4096,1024]{1,0:T(8,128)(2,1)} %slice.134, bf16[1,1024,1024]{2,1,0:T(8,128)(2,1)S(1)} %copy-done.15), kind=kOutput, calls=%fused_computation.22 | convolution fusion | flops 8673820672 | bytes 35651584 | tf_op jit(solution)/shard_map/dot_general | solution.py:42
  704.1 15.7 fusion.83
  739.4 16.6 fusion.52
  756.1 14.5 fusion.45
  770.6 44.2 %multiply_reduce_fusion = (f32[16,512]{1,0:T(8,128)S(1)}, f32[16,512]{1,0:T(8,128)S(1)}, f32[16,512,1024]{2,1,0:T(8,128)}) fusion(f32[16,512,1024]{2,1,0:T(8,128)} %get-tuple-element.101, f32[16,512]{1,0:T(8,128)S(1)} %get-tuple-element.109, pred[1024]{0:T(1024)(128)(4,1)S(1)} %iota_compare_fusion, f32[16,512,1024]{2,1,0:T(8,128)} %fusion.45, ...), kind=kOutput, calls=%fused_computation.1 | convolution fusion | flops 1157611520 | bytes 137495552 | tf_op jit(solution)/shard_map/while/body/eval_jaxpr/qhd,khd->hqk/dot_general | solution.py:99
  814.7 54.0 %multiply_convert_fusion = (bf16[16,512,1024]{2,1,0:T(8,128)(2,1)}, bf16[16,512,1024]{2,1,0:T(8,128)(2,1)}) fusion(f32[16,512,1024]{2,1,0:T(8,128)} %get-tuple-element.104, f32[16,512,1024]{2,1,0:T(8,128)} %get-tuple-element.101, f32[16,512]{1,0:T(8,128)S(1)} %get-tuple-element.77, f32[16,512]{1,0:T(8,128)S(1)} %get-tuple-element.109, ...), kind=kLoop, calls=%fused_computation | loop fusion | flops 100663296 | bytes 167904256 | tf_op jit(solution)/shard_map/while/body/eval_jaxpr/convert_element_type | solution.py:110
  868.8 10.9 fusion.48
  879.7 11.7 fusion.40
  891.4 17.1 fusion.35
  908.4 11.6 fusion.41
  920.0 10.4 fusion.34
  931.5 10.6 fusion.84
  955.9 15.1 convolution_bitcast_fusion.1
  971.0 18.7 %convolution_bitcast_fusion = f32[512,8,8,128]{3,2,1,0:T(8,128)} fusion(bf16[1,1024,1024]{2,1,0:T(8,128)(2,1)S(1)} %copy-done.16, f32[1024,4096]{1,0:T(8,128)} %fusion.74), kind=kOutput, calls=%fused_computation.24 | convolution fusion | flops 8627683328 | bytes 35651584 | tf_op jit(solution)/shard_map/dot_general | solution.py:48
  1001.5 12.1 copy.48
  1013.6 11.4 constant_dynamic-update-slice_fusion.3
  1060.7 18.1 %fusion.24 = bf16[1,1024,1024]{1,2,0:T(8,128)(2,1)} fusion(f32[1,1024,1024]{1,2,0:T(8,128)} %copy-done.5, bf16[4096,1024]{1,0:T(8,128)(2,1)} %slice.134, f32[1024,4096]{1,0:T(8,128)} %fusion.74), kind=kOutput, calls=%fused_computation.50 | convolution fusion | flops 8629780480 | bytes 31457280 | tf_op jit(solution)/shard_map/dot_general | solution.py:157
  1093.6 692.0 %all-reduce.4.cloned.1.call-done = (f32[28672]{0:T(1024)}, f32[12611584]{0:T(1024)}) async-done(((f32[28672]{0:T(1024)}, f32[12611584]{0:T(1024)}), (f32[28672]{0:T(1024)}, f32[12611584]{0:T(1024)})) %all-reduce.4.cloned.1.call-update) | async-done | bytes 50561040 | tf_op jit(solution)/shard_map/psum | solution.py:205
  (176 shorter events, 151.9 us)
Async XLA Ops:
  7.2 289.3 %all-gather.3.cloned.1.call-start = ((), (), s32[]{:S(2)}) async-start(), calls=%async_computation | async-start | bytes 52022784 | tf_op jit(solution)/shard_map/all_gather | solution.py:132
  18.5 1767.1 %all-reduce.4.cloned.1.call-start = ((), (), s32[]{:S(2)}) async-start(), calls=%async_computation.1 | async-start | bytes 101122048 | tf_op jit(solution)/shard_map/psum | solution.py:205
  21.4 502.0 %copy-start.1 = (bf16[1,1024,1024]{1,2,0:T(8,128)(2,1)}, bf16[1,1024,1024]{1,2,0:T(8,128)(2,1)S(1)}, u32[]{:S(2)}) copy-start(bf16[1,1024,1024]{1,2,0:T(8,128)(2,1)S(1)} %copy.37) | copy-start | bytes 6291460
  27.6 495.8 %copy-start.24 = (f32[1024]{0:T(1024)}, f32[1024]{0:T(1024)S(1)}, u32[]{:S(2)}) copy-start(f32[1024]{0:T(1024)S(1)} %broadcast_multiply_fusion.2) | copy-start | bytes 12292
  28.2 407.2 %copy-start.36 = (f32[1024]{0:T(1024)}, f32[1024]{0:T(1024)S(1)}, u32[]{:S(2)}) copy-start(f32[1024]{0:T(1024)S(1)} %fusion.20) | copy-start | bytes 12292
  28.2 495.2 %copy-start.28 = (f32[1024]{0:T(1024)}, f32[1024]{0:T(1024)S(1)}, u32[]{:S(2)}) copy-start(f32[1024]{0:T(1024)S(1)} %fusion.55) | copy-start | bytes 12292
  523.3 12.2 copy-start.30
  523.3 12.2 copy-start.43
  523.3 143.2 %copy-start.41 = (f32[1,1024]{1,0:T(1,128)}, f32[1,1024]{1,0:T(1,128)S(1)}, u32[]{:S(2)}) copy-start(f32[1,1024]{1,0:T(1,128)S(1)} %get-tuple-element.96) | copy-start | bytes 12292
  523.3 207.4 %copy-start.34 = (f32[1,1024]{1,0:T(1,128)}, f32[1,1024]{1,0:T(1,128)S(1)}, u32[]{:S(2)}) copy-start(f32[1,1024]{1,0:T(1,128)S(1)} %get-tuple-element.93) | copy-start | bytes 12292
  544.2 15.4 copy-start
  614.4 15.9 slice-start.1
  645.8 15.1 copy-start.2
  666.1 64.7 %copy-start.26 = (f32[1024]{0:T(1024)}, f32[1024]{0:T(1024)S(1)}, u32[]{:S(2)}) copy-start(f32[1024]{0:T(1024)S(1)} %broadcast_multiply_fusion.1) | copy-start | bytes 12292
  666.6 64.2 %copy-start.32 = (f32[1024]{0:T(1024)}, f32[1024]{0:T(1024)S(1)}, u32[]{:S(2)}) copy-start(f32[1024]{0:T(1024)S(1)} %fusion.56) | copy-start | bytes 12292
  668.0 13.2 copy-start.15
  735.6 20.5 %slice-start.2 = ((s8[6291456]{0:T(1024)(128)(4,1)}), s8[4194304]{0:T(1024)(128)(4,1)S(1)}, s32[]{:S(2)}) async-start(s8[6291456]{0:T(1024)(128)(4,1)} %bitcast.162), calls=%async_computation.4 | async-start | bytes 8388608
  739.4 16.6 slice-start.3
  756.1 14.5 copy-start.12
  879.7 11.7 copy-start.13
  920.0 10.7 copy-start.22
  931.4 10.7 copy-start.3
  931.5 10.7 copy-start.25
  931.5 10.7 copy-start.29
  955.9 15.1 copy-start.16
  1013.6 11.4 copy-start.14
  1013.6 14.6 slice-start.4
  1013.6 14.6 slice-start.5
  1013.6 14.9 slice-start.6
  1060.7 22.1 %copy-start.39 = (f32[1024]{0:T(1024)S(1)}, f32[1024]{0:T(1024)}, u32[]{:S(2)}) copy-start(f32[1024]{0:T(1024)} %copy-done.38) | copy-start | bytes 12292
  1089.2 698.1 %copy-start.11 = (f32[394112]{0:T(1024)S(1)}, f32[394112]{0:T(1024)}, u32[]{:S(2)}) copy-start(f32[394112]{0:T(1024)} %param.10) | copy-start | bytes 4729348
  1089.2 698.1 %copy-start.23 = (f32[394112]{0:T(1024)S(1)}, f32[394112]{0:T(1024)}, u32[]{:S(2)}) copy-start(f32[394112]{0:T(1024)} %param.11) | copy-start | bytes 4729348
  (27 other events, 158.9 us)
Sparse Core Ops, SparseCore 0:
  18.6 277.8 all-gather.2
  1060.8 724.7 all-reduce.3
where the time goes:
time: 1810 us; the launch traced here: 1800 us
  waiting for transfers between devices  960 us (53%)
  matrix products  356 us (20%)
  other arithmetic  240 us (13%)
  local copies, waits for them, and re-layouts  229 us (13%)
    psum x1, waiting for transfers between devices, per_device(): section_total = lax.psum(table_flat, ('dp', 'fsdp'))  692 us
    all_gather x1, waiting for transfers between devices, per_device(): gathered = lax.all_gather(low_params, ('dp', 'fsdp'), axis=0, tiled=True)  268 us
    unnamed x124, local copies, waits for them, and re-layouts  148 us
    all_gather x1, other arithmetic, per_device(): gathered = lax.all_gather(low_params, ('dp', 'fsdp'), axis=0, tiled=True)  139 us
    dot_general x2, matrix products, attend_backward(): jnp.einsum('qhd,khd->hqk', grad_block, values, preferred_element_type=jnp...  58.6 us
    convert_element_type x1, other arithmetic, attend_backward(): grad_scores = (softmax_w * (grad_probs - jnp.sum(softmax_w * grad_probs,...  54 us
    dot_general x4, matrix products, dot_trans(): lax.dot_general(left, right, (((1,), (1,)), ((), ())), preferred_element_...  51.5 us
    dot_general x4, matrix products, dot_inner(): lax.dot_general(left, right, (((0,), (0,)), ((), ())), preferred_element_...  47.5 us
  transfers between devices with their start and end apart: 2, of which 2 were waited for; matrix products, arithmetic and copies ran while one was open for 2% of the time, Pallas kernels for 0%

commit v1 on v0

--- a/solution.py
+++ b/solution.py
@@ -1,6 +1,8 @@
 import jax
 import jax.numpy as jnp
 from jax import lax
+from jax.experimental import pallas as pl
+from jax.experimental.pallas import tpu as pltpu
 from jax.sharding import PartitionSpec as P
 
 D = 1024
@@ -225,6 +227,600 @@
     return (block_out, input_grad, param_grad, new_params, new_first, new_second, section_grad)
 
 
+LANES = 128
+TILE = 16
+EPS = 1e-05
+VMEM_LIMIT = 62 * 1024 * 1024
+GELU_C = 0.7978845608028654
+GELU_A = 0.044715
+BF = jnp.bfloat16
+F32 = jnp.float32
+
+
+def params_of(*semantics):
+    return pltpu.CompilerParams(
+        dimension_semantics=semantics or None, vmem_limit_bytes=VMEM_LIMIT
+    )
+
+
+def cost(flops, moved, transcendentals=0):
+    return pl.CostEstimate(
+        flops=int(flops), bytes_accessed=int(moved), transcendentals=int(transcendentals)
+    )
+
+
+def dot_nn(left, right):
+    return lax.dot_general(left, right, (((1,), (0,)), ((), ())), preferred_element_type=F32)
+
+
+def dot_nt(left, right):
+    return lax.dot_general(left, right, (((1,), (1,)), ((), ())), preferred_element_type=F32)
+
+
+def dot_tn(left, right):
+    return lax.dot_general(left, right, (((0,), (0,)), ((), ())), preferred_element_type=F32)
+
+
+def from_tiles(ref, first, count):
+    rows = ref.shape[0] * TILE
+    parts = [ref[:, first + c].reshape(rows, LANES) for c in range(count)]
+    return parts[0] if count == 1 else jnp.concatenate(parts, 1)
+
+
+def to_tiles(ref, first, value):
+    rows, columns = value.shape
+    for c in range(columns // LANES):
+        part = value[:, c * LANES : (c + 1) * LANES].astype(BF)
+        ref[:, first + c] = part.reshape(rows // TILE, TILE, LANES)
+
+
+def row_chunks(kind):
+    return {0: 3 * D // LANES, 1: D // LANES, 2: FF // LANES}[kind]
+
+
+def each_tile(kinds, body):
+    def span(kind, start, rows):
+        step = row_chunks(kind)
+        block = TILE * step
+
+        def one(index, carry):
+            base = start + index * block
+            for c in range(step):
+                body(base // TILE + c, base + c, step)
+            return carry
+
+        lax.fori_loop(0, rows // block, one, 0)
+
+    @pl.when(kinds[0] == 0)
+    def _():
+        span(0, 0, 3072)
+
+    for part in range(3):
+        for kind in (1, 2):
+
+            @pl.when(kinds[part] == kind)
+            def _():
+                span(kind, part * 1024, 1024)
+
+
+def pack_kernel(kinds, flat_ref, tiles_ref):
+    def body(tile, row, step):
+        tiles_ref[tile] = flat_ref[pl.ds(row, TILE, stride=step), :].astype(BF)
+
+    each_tile(kinds, body)
+
+
+def unpack_kernel(kinds, tiles_ref, flat_ref):
+    def body(tile, row, step):
+        flat_ref[pl.ds(row, TILE, stride=step), :] = tiles_ref[tile].astype(F32)
+
+    each_tile(kinds, body)
+
+
+def shard_kinds(index):
+    start = index * 3072 + jnp.arange(3, dtype=jnp.int32) * 1024
+    qkv_end = 3 * D * D // LANES
+    out_end = qkv_end + D * D // LANES
+    up_end = out_end + D * FF // LANES
+    return jnp.where(
+        start < qkv_end, 0, jnp.where((start < out_end) | (start >= up_end), 1, 2)
+    ).astype(jnp.int32)
+
+
+def pack_shard(kinds, flat):
+    return pl.pallas_call(
+        pack_kernel,
+        out_shape=jax.ShapeDtypeStruct((192, TILE, LANES), BF),
+        in_specs=[pl.BlockSpec(memory_space=pltpu.SMEM), pl.BlockSpec(memory_space=pltpu.VMEM)],
+        out_specs=pl.BlockSpec(memory_space=pltpu.VMEM),
+        compiler_params=params_of(),
+        cost_estimate=cost(0, 3 << 20),
+        name="pack_shard",
+    )(kinds, flat)
+
+
+def unpack_shard(kinds, tiles):
+    return pl.pallas_call(
+        unpack_kernel,
+        out_shape=jax.ShapeDtypeStruct((3072, LANES), F32),
+        in_specs=[pl.BlockSpec(memory_space=pltpu.SMEM), pl.BlockSpec(memory_space=pltpu.VMEM)],
+        out_specs=pl.BlockSpec(memory_space=pltpu.VMEM),
+        compiler_params=params_of(),
+        cost_estimate=cost(0, 3 << 20),
+        name="unpack_shard",
+    )(kinds, tiles)
+
+
+def centre(field):
+    average = jnp.mean(field, -1, keepdims=True)
+    centred = field - average
+    spread = jnp.mean(centred * centred, -1, keepdims=True)
+    inverse = lax.rsqrt(spread + EPS)
+    return centred * inverse, inverse
+
+
+def norm_back(zhat, inverse, grad, gain):
+    scaled = grad * gain
+    mean_one = jnp.mean(scaled, -1, keepdims=True)
+    mean_two = jnp.mean(scaled * zhat, -1, keepdims=True)
+    return inverse * (scaled - mean_one - zhat * mean_two)
+
+
+def qkv_kernel(x_ref, mod_ref, w_ref, low_ref, qkv_ref):
+    @pl.when(pl.program_id(0) == 0)
+    def _():
+        zhat, _ = centre(x_ref[...].astype(F32))
+        low_ref[...] = (zhat * mod_ref[0:1, :] + mod_ref[1:2, :]).astype(BF)
+
+    weights = from_tiles(w_ref, 0, w_ref.shape[1])
+    qkv_ref[...] = dot_nn(low_ref[...], weights).astype(BF)
+
+
+def project_qkv(x, mod, tiles):
+    chunks = 4
+    width = chunks * LANES
+    return pl.pallas_call(
+        qkv_kernel,
+        grid=(3 * D // width,),
+        out_shape=(
+            jax.ShapeDtypeStruct((1024, D), BF),
+            jax.ShapeDtypeStruct((1024, 3 * D), BF),
+        ),
+        in_specs=[
+            pl.BlockSpec((1024, D), lambda j: (0, 0)),
+            pl.BlockSpec((4, D), lambda j: (0, 0)),
+            pl.BlockSpec((64, chunks, TILE, LANES), lambda j: (0, j, 0, 0)),
+        ],
+        out_specs=(
+            pl.BlockSpec((1024, D), lambda j: (0, 0)),
+            pl.BlockSpec((1024, width), lambda j: (0, j)),
+        ),
+        compiler_params=params_of("arbitrary"),
+        cost_estimate=cost(6.4e9, 18e6),
+        name="project_qkv",
+    )(x, mod, tiles.reshape(-1, 24, TILE, LANES))
+
+
+def head_lanes(head):
+    lane = lax.broadcasted_iota(jnp.int32, (1, LANES), 1)
+    return (lane >= 64) if head else (lane < 64)
+
+
+def attend_kernel(len_ref, q_ref, k_ref, v_ref, out_ref):
+    rows = 256
+    frames = k_ref.shape[0]
+    valid = lax.broadcasted_iota(jnp.int32, (1, frames), 1) < len_ref[0]
+    keys = k_ref[...]
+    zero = jnp.zeros((), BF)
+    values = [jnp.where(head_lanes(h), v_ref[...], zero) for h in range(2)]
+    for offset in range(0, frames, rows):
+        queries = q_ref[offset : offset + rows, :] * jnp.asarray(0.125, BF)
+        total = None
+        for h in range(2):
+            scores = dot_nt(jnp.where(head_lanes(h), queries, zero), keys)
+            scores = jnp.where(valid, scores, -1e30)
+            weights = jnp.exp(scores - jnp.max(scores, -1, keepdims=True))
+            weights = weights * (1.0 / jnp.sum(weights, -1, keepdims=True))
+            mixed = dot_nn(weights.astype(BF), values[h])
+            total = mixed if total is None else total + mixed
+        out_ref[offset : offset + rows, :] = total.astype(BF)
+
+
+def attend(key_len, qkv):
+    pairs = HEADS // 2
+    return pl.pallas_call(
+        attend_kernel,
+        grid=(pairs,),
+        out_shape=jax.ShapeDtypeStruct((1024, D), BF),
+        in_specs=[
+            pl.BlockSpec(memory_space=pltpu.SMEM),
+            pl.BlockSpec((1024, LANES), lambda j: (0, j)),
+            pl.BlockSpec((1024, LANES), lambda j: (0, pairs + j)),
+            pl.BlockSpec((1024, LANES), lambda j: (0, 2 * pairs + j)),
+        ],
+        out_specs=pl.BlockSpec((1024, LANES), lambda j: (0, j)),
+        compiler_params=params_of("arbitrary"),
+        cost_estimate=cost(17e9, 8e6, 16e6),
+        name="attend",
+    )(key_len, qkv, qkv, qkv)
+
+
+def attend_back_kernel(len_ref, q_ref, k_ref, v_ref, do_ref, dq_ref, dk_ref, dv_ref, dk_acc, dv_acc):
+    rows = 256
+    frames = k_ref.shape[0]
+    valid = lax.broadcasted_iota(jnp.int32, (frames, 1), 0) < len_ref[0]
+    keys = k_ref[...]
+    values = v_ref[...]
+    zero = jnp.zeros((), BF)
+    masked_keys = [jnp.where(head_lanes(h), keys, zero) for h in range(2)]
+    for offset in range(0, frames, rows):
+        queries = q_ref[offset : offset + rows, :] * jnp.asarray(0.125, BF)
+        grads = do_ref[offset : offset + rows, :]
+        total = None
+        for h in range(2):
+            masked_q = jnp.where(head_lanes(h), queries, zero)
+            masked_g = jnp.where(head_lanes(h), grads, zero)
+            scores = dot_nt(keys, masked_q)
+            scores = jnp.where(valid, scores, -1e30)
+            weights = jnp.exp(scores - jnp.max(scores, 0, keepdims=True))
+            weights = weights * (1.0 / jnp.sum(weights, 0, keepdims=True))
+            grad_w = dot_nt(values, masked_g)
+            product = weights * grad_w
+            back = product - weights * jnp.sum(product, 0, keepdims=True)
+            back = back.astype(BF)
+            part_v = dot_nn(weights.astype(BF), masked_g)
+            part_k = dot_nn(back, masked_q)
+            if offset == 0 and h == 0:
+                dv_acc[...] = part_v
+                dk_acc[...] = part_k
+            else:
+                dv_acc[...] += part_v
+                dk_acc[...] += part_k
+            part_q = dot_tn(back, masked_keys[h])
+            total = part_q if total is None else total + part_q
+        dq_ref[offset : offset + rows, :] = (total * 0.125).astype(BF)
+    dk_ref[...] = dk_acc[...].astype(BF)
+    dv_ref[...] = dv_acc[...].astype(BF)
+
+
+def attend_back(key_len, qkv, grad_mix):
+    pairs = HEADS // 2
+    block = lambda shift: pl.BlockSpec((1024, LANES), lambda j: (0, shift + j))
+    return pl.pallas_call(
+        attend_back_kernel,
+        grid=(pairs,),
+        out_shape=(jax.ShapeDtypeStruct((1024, D), BF),) * 3,
+        in_specs=[
+            pl.BlockSpec(memory_space=pltpu.SMEM),
+            block(0),
+            block(pairs),
+            block(2 * pairs),
+            block(0),
+        ],
+        out_specs=(block(0),) * 3,
+        scratch_shapes=[pltpu.VMEM((1024, LANES), F32)] * 2,
+        compiler_params=params_of("arbitrary"),
+        cost_estimate=cost(43e9, 14e6, 16e6),
+        name="attend_back",
+    )(key_len, qkv, qkv, qkv, grad_mix)
+
+
+def middle_kernel(x_ref, mod_ref, mix_ref, w_ref, mid_ref, low_ref):
+    weights = from_tiles(w_ref, 0, w_ref.shape[1])
+    middle = x_ref[...].astype(F32) + dot_nn(mix_ref[...], weights)
+    mid_ref[...] = middle
+    zhat, _ = centre(middle)
+    low_ref[...] = (zhat * mod_ref[2:3, :] + mod_ref[3:4, :]).astype(BF)
+
+
+def middle_rows(x, mod, mixture, tiles):
+    rows = 256
+    return pl.pallas_call(
+        middle_kernel,
+        grid=(1024 // rows,),
+        out_shape=(jax.ShapeDtypeStruct((1024, D), F32), jax.ShapeDtypeStruct((1024, D), BF)),
+        in_specs=[
+            pl.BlockSpec((rows, D), lambda i: (i, 0)),
+            pl.BlockSpec((4, D), lambda i: (0, 0)),
+            pl.BlockSpec((rows, D), lambda i: (i, 0)),
+            pl.BlockSpec((64, 8, TILE, LANES), lambda i: (3, 0, 0, 0)),
+        ],
+        out_specs=(
+            pl.BlockSpec((rows, D), lambda i: (i, 0)),
+            pl.BlockSpec((rows, D), lambda i: (i, 0)),
+        ),
+        compiler_params=params_of("arbitrary"),
+        cost_estimate=cost(2.2e9, 12e6),
+        name="middle_rows",
+    )(x, mod, mixture, tiles.reshape(-1, 8, TILE, LANES))
+
+
+def ffn_kernel(
+    mid_ref, mod_ref, low_ref, dy_ref, up_ref, down_ref,
+    out_ref, dmid_ref, low_dmid_ref, dmod_ref, dup_ref, ddown_ref,
+    y_acc, dh_acc, low_t, act_s, du_s,
+):
+    step = pl.program_id(0)
+    frames = mid_ref.shape[0]
+    rows = 256
+
+    @pl.when(step == 0)
+    def _():
+        y_acc[...] = jnp.zeros_like(y_acc)
+        dh_acc[...] = jnp.zeros_like(dh_acc)
+        low_t[...] = low_ref[...].T
+
+    up = from_tiles(up_ref, 0, up_ref.shape[1])
+    down = from_tiles(down_ref, 0, down_ref.shape[1])
+    for offset in range(0, frames, rows):
+        here = slice(offset, offset + rows)
+        hidden = dot_nn(low_ref[here, :], up)
+        grad_act = dot_nt(dy_ref[here, :], down)
+        square = hidden * hidden
+        inner = GELU_C * (hidden + GELU_A * (square * hidden))
+        bend = jnp.tanh(inner)
+        half = 0.5 * (1.0 + bend)
+        act = (hidden * half).astype(BF)
+        slope = half + 0.5 * hidden * (1.0 - bend * bend) * (
+            GELU_C * (1.0 + 3.0 * GELU_A * square)
+        )
+        grad_hidden = (grad_act * slope).astype(BF)
+        act_s[here, :] = act
+        du_s[here, :] = grad_hidden
+        y_acc[here, :] += dot_nn(act, down)
+        dh_acc[here, :] += dot_nt(grad_hidden, up)
+    to_tiles(ddown_ref, 0, dot_tn(act_s[...], dy_ref[...]))
+    to_tiles(dup_ref, 0, dot_nn(low_t[...], du_s[...]))
+
+    @pl.when(step == pl.num_programs(0) - 1)
+    def _():
+        grad_gain = jnp.zeros((1, D), F32)
+        grad_shift = jnp.zeros((1, D), F32)
+        for offset in range(0, frames, rows):
+            here = slice(offset, offset + rows)
+            middle = mid_ref[here, :]
+            out_ref[here, :] = (middle + y_acc[here, :]).astype(BF)
+            zhat, inverse = centre(middle)
+            grad = dh_acc[here, :]
+            grad_gain += jnp.sum(grad * zhat, 0, keepdims=True)
+            grad_shift += jnp.sum(grad, 0, keepdims=True)
+            grad_mid = dy_ref[here, :].astype(F32) + norm_back(zhat, inverse, grad, mod_ref[2:3, :])
+            dmid_ref[here, :] = grad_mid
+            low_dmid_ref[here, :] = grad_mid.astype(BF)
+        dmod_ref[0:1, :] = grad_gain
+        dmod_ref[1:2, :] = grad_shift
+
+
+def ffn_both(middle, mod, low_two, dy, tiles):
+    chunks = 4
+    width = chunks * LANES
+    steps = FF // width
+    whole = lambda *shape: pl.BlockSpec(shape, lambda j: (0,) * len(shape))
+    once = lambda *shape: pl.BlockSpec(
+        shape, lambda j: (0,) * len(shape), pipeline_mode=pl.Buffered(1)
+    )
+    return pl.pallas_call(
+        ffn_kernel,
+        grid=(steps,),
+        out_shape=(
+            jax.ShapeDtypeStruct((1024, D), BF),
+            jax.ShapeDtypeStruct((1024, D), F32),
+            jax.ShapeDtypeStruct((1024, D), BF),
+            jax.ShapeDtypeStruct((2, D), F32),
+            jax.ShapeDtypeStruct((64, 32, TILE, LANES), BF),
+            jax.ShapeDtypeStruct((256, 8, TILE, LANES), BF),
+        ),
+        in_specs=[
+            once(1024, D),
+            whole(4, D),
+            once(1024, D),
+            once(1024, D),
+            pl.BlockSpec((64, chunks, TILE, LANES), lambda j: (1, j, 0, 0)),
+            pl.BlockSpec((width // TILE, 8, TILE, LANES), lambda j: (512 * TILE // width + j, 0, 0, 0)),
+        ],
+        out_specs=(
+            once(1024, D),
+            once(1024, D),
+            once(1024, D),
+            whole(2, D),
+            pl.BlockSpec((64, chunks, TILE, LANES), lambda j: (0, j, 0, 0)),
+            pl.BlockSpec((width // TILE, 8, TILE, LANES), lambda j: (j, 0, 0, 0)),
+        ),
+        scratch_shapes=[
+            pltpu.VMEM((1024, D), F32),
+            pltpu.VMEM((1024, D), F32),
+            pltpu.VMEM((D, 1024), BF),
+            pltpu.VMEM((1024, width), BF),
+            pltpu.VMEM((1024, width), BF),
+        ],
+        compiler_params=params_of("arbitrary"),
+        cost_estimate=cost(52e9, 60e6, 4e6),
+        name="ffn_both",
+    )(
+        middle, mod, low_two, dy,
+        tiles.reshape(-1, 32, TILE, LANES), tiles.reshape(-1, 8, TILE, LANES),
+    )
+
+
+def out_back_kernel(mix_ref, dmid_ref, w_ref, dmix_ref, dw_ref):
+    weights = from_tiles(w_ref, 0, w_ref.shape[1])
+    dmix_ref[...] = dot_nt(dmid_ref[...], weights).astype(BF)
+    to_tiles(dw_ref, 0, dot_tn(mix_ref[...], dmid_ref[...]))
+
+
+def out_back(mixture, low_dmid, tiles):
+    width = 256
+    return pl.pallas_call(
+        out_back_kernel,
+        grid=(D // width,),
+        out_shape=(
+            jax.ShapeDtypeStruct((1024, D), BF),
+            jax.ShapeDtypeStruct((64, 8, TILE, LANES), BF),
+        ),
+        in_specs=[
+            pl.BlockSpec((1024, width), lambda j: (0, j)),
+            pl.BlockSpec((1024, D), lambda j: (0, 0)),
+            pl.BlockSpec((width // TILE, 8, TILE, LANES), lambda j: (192 * TILE // width + j, 0, 0, 0)),
+        ],
+        out_specs=(
+            pl.BlockSpec((1024, width), lambda j: (0, j)),
+            pl.BlockSpec((width // TILE, 8, TILE, LANES), lambda j: (j, 0, 0, 0)),
+        ),
+        compiler_params=params_of("arbitrary"),
+        cost_estimate=cost(4.3e9, 10e6),
+        name="out_back",
+    )(mixture, low_dmid, tiles.reshape(-1, 8, TILE, LANES))
+
+
+def qkv_weight_kernel(low_ref, dq_ref, dk_ref, dv_ref, dw_ref):
+    for third, grad_ref in enumerate((dq_ref, dk_ref, dv_ref)):
+        to_tiles(dw_ref, third * 8, dot_tn(low_ref[...], grad_ref[...]))
+
+
+def qkv_weight_grad(low_one, dq, dk, dv):
+    width = 256
+    whole = pl.BlockSpec((1024, D), lambda j: (0, 0))
+    return pl.pallas_call(
+        qkv_weight_kernel,
+        grid=(D // width,),
+        out_shape=jax.ShapeDtypeStruct((64, 24, TILE, LANES), BF),
+        in_specs=[pl.BlockSpec((1024, width), lambda j: (0, j)), whole, whole, whole],
+        out_specs=pl.BlockSpec((width // TILE, 24, TILE, LANES), lambda j: (j, 0, 0, 0)),
+        compiler_params=params_of("arbitrary"),
+        cost_estimate=cost(6.4e9, 15e6),
+        name="qkv_weight_grad",
+    )(low_one, dq, dk, dv)
+
+
+def input_kernel(x_ref, mod_ref, dmid_ref, dq_ref, dk_ref, dv_ref, w_ref, grad_ref, dmod_ref):
+    grad = None
+    for third, part_ref in enumerate((dq_ref, dk_ref, dv_ref)):
+        part = dot_nt(part_ref[...], from_tiles(w_ref, third * 8, 8))
+        grad = part if grad is None else grad + part
+    zhat, inverse = centre(x_ref[...].astype(F32))
+
+    @pl.when(pl.program_id(0) == 0)
+    def _():
+        dmod_ref[...] = jnp.zeros_like(dmod_ref)
+
+    dmod_ref[0:1, :] += jnp.sum(grad * zhat, 0, keepdims=True)
+    dmod_ref[1:2, :] += jnp.sum(grad, 0, keepdims=True)
+    grad_ref[...] = (dmid_ref[...] + norm_back(zhat, inverse, grad, mod_ref[0:1, :])).astype(BF)
+
+
+def input_back(x, mod, dmid, dq, dk, dv, tiles):
+    rows = 256
+    block = pl.BlockSpec((rows, D), lambda i: (i, 0))
+    return pl.pallas_call(
+        input_kernel,
+        grid=(1024 // rows,),
+        out_shape=(jax.ShapeDtypeStruct((1024, D), BF), jax.ShapeDtypeStruct((2, D), F32)),
+        in_specs=[
+            block,
+            pl.BlockSpec((4, D), lambda i: (0, 0)),
+            block,
+            block,
+            block,
+            block,
+            pl.BlockSpec((64, 24, TILE, LANES), lambda i: (0, 0, 0, 0)),
+        ],
+        out_specs=(block, pl.BlockSpec((2, D), lambda i: (0, 0))),
+        compiler_params=params_of("arbitrary"),
+        cost_estimate=cost(6.4e9, 22e6),
+        name="input_back",
+    )(x, mod, dmid, dq, dk, dv, tiles.reshape(-1, 24, TILE, LANES))
+
+
+def flat_index():
+    return lax.axis_index(("dp", "fsdp"))
+
+
+def exchange(value, mask, count):
+    return lax.ppermute(value, ("dp", "fsdp"), [(i, i ^ mask) for i in range(count)])
+
+
+def sum_everywhere(value, count):
+    mask = 1
+    while mask < count:
+        value = value + exchange(value, mask, count)
+        mask *= 2
+    return value
+
+
+def fast_device(tokens, key_len, section, params, first_moment, second_moment, cotangent):
+    count = lax.axis_size(("dp", "fsdp"))
+    index = flat_index()
+    shard = params.shape[0]
+    table_size = SECTIONS * 4 * D
+    aligned = (count * shard - table_size) // count
+    slip = table_size // count
+    kinds = shard_kinds(index)
+    x = tokens[0]
+    dy = cotangent[0]
+
+    before = lax.ppermute(
+        params[shard - table_size :], ("dp", "fsdp"), [(i, i + 1) for i in range(count - 1)]
+    )
+    own = lax.dynamic_slice(
+        jnp.concatenate([before, params]), (table_size - index * slip,), (aligned,)
+    )
+    packed = pack_shard(kinds, own.reshape(aligned // LANES, LANES))
+    tiles = gather_tiles(packed, index, count)
+
+    last = index == count - 1
+    table = jnp.where(last, params[shard - table_size :], 0.0).astype(BF)
+    table = sum_everywhere(table.reshape(SECTIONS, 4 * D), count)
+    picker = (section[0] - 1 == jnp.arange(SECTIONS)).astype(F32)[:, None]
+    mod = jnp.sum(picker * table.astype(F32), 0).reshape(4, D)
+
+    low_one, qkv = project_qkv(x, mod, tiles)
+    mixture = attend(key_len, qkv)
+    middle, low_two = middle_rows(x, mod, mixture, tiles)
+    block_out, dmid, low_dmid, dmod_two, grad_up, grad_down = ffn_both(
+        middle, mod, low_two, dy, tiles
+    )
+    grad_mix, grad_out = out_back(mixture, low_dmid, tiles)
+    dq, dk, dv = attend_back(key_len, qkv, grad_mix)
+    grad_qkv = qkv_weight_grad(low_one, dq, dk, dv)
+    input_grad, dmod_one = input_back(x, mod, dmid, dq, dk, dv, tiles)
+
+    per_item = jnp.concatenate([dmod_one, dmod_two], 0).reshape(1, 4 * D)
+    section_grad = sum_everywhere(picker * per_item, count)
+
+    reduced = reduce_tiles(grad_qkv, grad_out, grad_up, grad_down, index, count)
+    summed = unpack_shard(kinds, reduced).reshape(aligned)
+    after = lax.ppermute(
+        summed[:table_size], ("dp", "fsdp"), [(i, i - 1) for i in range(1, count)]
+    )
+    after = jnp.where(last, section_grad.reshape(table_size), after)
+    param_grad = lax.dynamic_slice(jnp.concatenate([summed, after]), (index * slip,), (shard,))
+    new_first = beta_one * first_moment + (1.0 - beta_one) * param_grad
+    new_second = beta_two * second_moment + (1.0 - beta_two) * param_grad * param_grad
+    new_params = params - learn_rate * (new_first / bias_one) / (
+        jnp.sqrt(new_second / bias_two) + adam_eps
+    )
+    return (
+        block_out[None],
+        input_grad[None],
+        param_grad,
+        new_params,
+        new_first,
+        new_second,
+        section_grad,
+    )
+
+
+def gather_tiles(packed, index, count):
+    return lax.all_gather(packed, ("dp", "fsdp"), axis=0, tiled=True)
+
+
+def reduce_tiles(grad_qkv, grad_out, grad_up, grad_down, index, count):
+    parts = [g.reshape(-1, TILE, LANES) for g in (grad_qkv, grad_out, grad_up, grad_down)]
+    return lax.psum_scatter(
+        jnp.concatenate(parts, 0), ("dp", "fsdp"), scatter_dimension=0, tiled=True
+    )
+
+
 def solution(mesh):
     in_specs = (
         P(("dp", "fsdp"), None, None),
@@ -244,6 +840,7 @@
         P(("dp", "fsdp")),
         P(),
     )
+    fast = dict(mesh.shape) == {"dp": 8, "fsdp": 4}
     return jax.shard_map(
-        per_device, mesh=mesh, in_specs=in_specs, out_specs=out_specs, check_vma=False
-    )
+        fast_device if fast else per_device, mesh=mesh, in_specs=in_specs, out_specs=out_specs, check_vma=False
+    )

time: 1810 us -> 708 us (0.39)
  waiting for transfers between devices: 960 us -> 372 us
  matrix products: 356 us -> 0 us
  Pallas kernels: 0 us -> 247 us
  local copies, waits for them, and re-layouts: 229 us -> 2.62 us
  other arithmetic: 240 us -> 41.3 us
  starting transfers between devices: 0.08 us -> 20.4 us
    psum x1 -> x0, waiting for transfers between devices: 692 us -> none  [per_device(): section_total = lax.psum(table_flat, ('dp', 'fsdp'))]
    dot_general x25 -> x0, matrix products: 356 us -> none  [the longest x2 58.6 us: attend_backward(): jnp.einsum('qhd,khd->hqk', grad_block, values, preferred_element_type=jnp...]
    pallas_call x0 -> x10, Pallas kernels: none -> 247 us  [the longest x1 75.8 us: attend_back(): pl.pallas_call(attend_back_kernel, grid=(pairs,), out_shape=(jax.ShapeDty...]
    reduce_scatter x0 -> x1, waiting for transfers between devices: none -> 209 us  [reduce_tiles(): lax.psum_scatter(jnp.concatenate(parts, 0), ('dp', 'fsdp'), scatter_dimen...]
    unnamed x124 -> x11, local copies, waits for them, and re-layouts: 148 us -> 0.03 us
    all_gather x1 -> x0, other arithmetic: 139 us -> none  [per_device(): gathered = lax.all_gather(low_params, ('dp', 'fsdp'), axis=0, tiled=True)]
    all_gather x1, waiting for transfers between devices: 268 us -> 134 us  [gather_tiles(): return lax.all_gather(packed, ('dp', 'fsdp'), axis=0, tiled=True)]
    convert_element_type x3 -> x2, other arithmetic: 62 us -> 0.92 us  [the longest x1 0.92 us: fast_device(): table = jnp.where(last, params[shard - table_size:], 0.0).astype(BF)]
  transfers between devices with their start and end apart: 2 -> 14, of which waited for: 2 -> 13; matrix products, arithmetic and copies ran while one was open for 2% -> 1% of each run, Pallas kernels for 0% -> 3%
where the time goes in v1:
time: 708 us; the launch traced here: 699 us
  waiting for transfers between devices  372 us (53%)
  Pallas kernels  247 us (35%)
  other arithmetic  41.3 us (6%)
  starting transfers between devices  20.4 us (3%)
  between operations  16 us (2%)
    reduce_scatter x1, waiting for transfers between devices, reduce_tiles(): lax.psum_scatter(jnp.concatenate(parts, 0), ('dp', 'fsdp'), scatter_dimen...  209 us
    all_gather x1, waiting for transfers between devices, gather_tiles(): return lax.all_gather(packed, ('dp', 'fsdp'), axis=0, tiled=True)  134 us
    pallas_call x1, Pallas kernels, attend_back(): pl.pallas_call(attend_back_kernel, grid=(pairs,), out_shape=(jax.ShapeDty...  75.8 us
    pallas_call x1, Pallas kernels, ffn_both(): pl.pallas_call(ffn_kernel, grid=(steps,), out_shape=(jax.ShapeDtypeStruct...  69.8 us
    pallas_call x1, Pallas kernels, attend(): pl.pallas_call(attend_kernel, grid=(pairs,), out_shape=jax.ShapeDtypeStru...  39.8 us
    concatenate x1, other arithmetic, reduce_tiles(): jnp.concatenate(parts, 0)  28.7 us
    ppermute x10, waiting for transfers between devices, exchange(): lax.ppermute(value, ('dp', 'fsdp'), [(i, i ^ mask) for i in range(count)])  24.4 us
    pallas_call x1, Pallas kernels, input_back(): pl.pallas_call(input_kernel, grid=(1024 // rows,), out_shape=(jax.ShapeDt...  15.4 us
  transfers between devices with their start and end apart: 14, of which 13 were waited for; matrix products, arithmetic and copies ran while one was open for 1% of the time, Pallas kernels for 3%

profile of v1, /device:TPU:1, one launch (start us, length us, event | category | flops | bytes accessed | tf_op | source)
XLA Modules:
  0.0 698.9 jit_solution(11286685096975099716)
XLA Ops:
  8.1 4.5 collective-permute-start.5
  13.2 1.2 collective-permute-done.5
  14.4 3.1 fusion.3.flat_ref
  17.5 2.7 pack_shard.1
  21.4 1.2 collective-permute-done
  22.6 2.2 collective-permute-start.1
  24.9 2.1 collective-permute-done.1
  27.0 2.0 collective-permute-start.2
  29.0 1.7 collective-permute-done.2
  30.7 2.6 collective-permute-start.3
  34.5 4.0 collective-permute-done.3
  38.5 2.1 collective-permute-start.4
  40.6 4.2 collective-permute-done.4
  45.6 134.0 %all-gather.2.cloned.1.call-done = bf16[6144,16,128]{2,1,0:T(8,128)(2,1)} async-done(((bf16[192,16,128]{2,1,0:T(8,128)(2,1)}), bf16[6144,16,128]{2,1,0:T(8,128)(2,1)}) %all-gather.2.cloned.1.call-update) | async-done | bytes 25165840 | tf_op jit(solution)/shard_map/all_gather | solution.py:814
  179.6 12.8 %project_qkv.1 = (bf16[1024,1024]{1,0:T(8,128)(2,1)}, bf16[1024,3072]{1,0:T(8,128)(2,1)}) custom-call(bf16[1024,1024]{1,0:T(8,128)(2,1)} %bitcast.28, f32[4,1024]{1,0:T(4,128)} %reshape.66.mod_ref, bf16[256,24,16,128]{3,2,1,0:T(8,128)(2,1)} %bitcast.22), custom_call_target="tpu_custom_call" | custom-call | flops 6400000000 | bytes 18000000 | tf_op jit(solution)/shard_map/project_qkv/pallas_call | solution.py:382
  192.4 39.8 %attend.1.mix_ref = bf16[1024,1024]{1,0:T(8,128)(2,1)} custom-call(s32[1]{0:T(128)S(6)} %copy.17.len_ref, bf16[1024,3072]{1,0:T(8,128)(2,1)} %get-tuple-element.24.q_ref.k_ref.v_ref, bf16[1024,3072]{1,0:T(8,128)(2,1)} %get-tuple-element.24.q_ref.k_ref.v_ref, bf16[1024,3072]{1,0:T(8,128)(2,1)} %get-tuple-element.24.q_ref.k_ref.v_ref), custom_call_target="tpu_custom_call" | custom-call | flops 16999999488 | bytes 8000000 | tf_op jit(solution)/shard_map/attend/pallas_call | solution.py:431
  232.2 7.4 %middle_rows.1 = (f32[1024,1024]{1,0:T(8,128)}, bf16[1024,1024]{1,0:T(8,128)(2,1)}) custom-call(bf16[1024,1024]{1,0:T(8,128)(2,1)} %bitcast.29, f32[4,1024]{1,0:T(4,128)} %reshape.66.mod_ref, bf16[1024,1024]{1,0:T(8,128)(2,1)} %attend.1.mix_ref, bf16[768,8,16,128]{3,2,1,0:T(8,128)(2,1)} %bitcast.23), custom_call_target="tpu_custom_call" | custom-call | flops 2200000000 | bytes 12000000 | tf_op jit(solution)/shard_map/middle_rows/pallas_call | solution.py:518
  239.7 69.8 %ffn_both.1 = (bf16[1024,1024]{1,0:T(8,128)(2,1)}, f32[1024,1024]{1,0:T(8,128)}, bf16[1024,1024]{1,0:T(8,128)(2,1)}, f32[2,1024]{1,0:T(2,128)}, bf16[64,32,16,12...) custom-call(f32[1024,1024]{1,0:T(8,128)} %get-tuple-element.25.mid_ref, f32[4,1024]{1,0:T(4,128)} %reshape.66.mod_ref, ...), custom_call_target="tpu_custom_call" | custom-call | flops 51999997952 | bytes 60000000 | tf_op jit(solution)/shard_map/ffn_both/pallas_call | solution.py:602
  309.5 8.5 %out_back.1 = (bf16[1024,1024]{1,0:T(8,128)(2,1)}, bf16[64,8,16,128]{3,2,1,0:T(8,128)(2,1)}) custom-call(bf16[1024,1024]{1,0:T(8,128)(2,1)} %attend.1.mix_ref, bf16[1024,1024]{1,0:T(8,128)(2,1)} %get-tuple-element.29.dmid_ref, bf16[768,8,16,128]{3,2,1,0:T(8,128)(2,1)} %bitcast.26), custom_call_target="tpu_custom_call" | custom-call | flops 4300000256 | bytes 10000000 | tf_op jit(solution)/shard_map/out_back/pallas_call | solution.py:653
  318.0 75.8 %attend_back.1 = (bf16[1024,1024]{1,0:T(8,128)(2,1)}, bf16[1024,1024]{1,0:T(8,128)(2,1)}, bf16[1024,1024]{1,0:T(8,128)(2,1)}) custom-call(s32[1]{0:T(128)S(6)} %copy.17.len_ref, bf16[1024,3072]{1,0:T(8,128)(2,1)} %get-tuple-element.24.q_ref.k_ref.v_ref, bf16[1024,3072]{1,0:T(8,128)(2,1)} %get-tuple-element.24.q_ref.k_ref.v_ref, ...), custom_call_target="tpu_custom_call" | custom-call | flops 43000000512 | bytes 14000000 | tf_op jit(solution)/shard_map/attend_back/pallas_call | solution.py:489
  393.7 11.6 %qkv_weight_grad.1 = bf16[64,24,16,128]{3,2,1,0:T(8,128)(2,1)} custom-call(bf16[1024,1024]{1,0:T(8,128)(2,1)} %get-tuple-element.35.low_ref, bf16[1024,1024]{1,0:T(8,128)(2,1)} %get-tuple-element.31.dq_ref, bf16[1024,1024]{1,0:T(8,128)(2,1)} %get-tuple-element.32.dk_ref, bf16[1024,1024]{1,0:T(8,128)(2,1)} %get-tuple-element.33.dv_ref), custom_call_target="tpu_custom_call" | custom-call | flops 6400000000 | bytes 15000000 | tf_op jit(solution)/shard_map/qkv_weight_grad/pallas_call | solution.py:683
  405.4 28.7 %pad_maximum_fusion = bf16[6144,16,128]{2,1,0:T(8,128)(2,1)} fusion(bf16[2048,16,128]{2,1,0:T(8,128)(2,1)} %bitcast.32, bf16[2048,16,128]{2,1,0:T(8,128)(2,1)} %bitcast.31, bf16[512,16,128]{2,1,0:T(8,128)(2,1)} %bitcast.35, bf16[1536,16,128]{2,1,0:T(8,128)(2,1)} %bitcast.34), kind=kLoop, calls=%fused_computation | loop fusion | flops 37748736 | bytes 50331648 | tf_op jit(solution)/shard_map/concatenate | solution.py:820
  434.1 15.4 %input_back.1 = (bf16[1024,1024]{1,0:T(8,128)(2,1)}, f32[2,1024]{1,0:T(2,128)}) custom-call(bf16[1024,1024]{1,0:T(8,128)(2,1)} %bitcast.30, f32[4,1024]{1,0:T(4,128)} %reshape.66.mod_ref, f32[1024,1024]{1,0:T(8,128)} %get-tuple-element.28.dmid_ref, bf16[1024,1024]{1,0:T(8,128)(2,1)} %get-tuple-element.31.dq_ref, ...), custom_call_target="tpu_custom_call" | custom-call | flops 6400000000 | bytes 22000000 | tf_op jit(solution)/shard_map/input_back/pallas_call | solution.py:714
  452.9 3.8 collective-permute-done.7
  456.8 1.3 collective-permute-start.8
  458.1 2.6 collective-permute-done.8
  460.7 3.8 collective-permute-done.9
  465.5 209.1 %reduce-scatter.2.cloned.1.call-done.tiles_ref = bf16[192,16,128]{2,1,0:T(8,128)(2,1)} async-done(((bf16[6144,16,128]{2,1,0:T(8,128)(2,1)}), bf16[192,16,128]{2,1,0:T(8,128)(2,1)}) %reduce-scatter.2.cloned.1.call-update) | async-done | bytes 786448 | tf_op jit(solution)/shard_map/reduce_scatter | solution.py:819
  674.6 2.7 unpack_shard.1
  678.1 3.1 collective-permute-start.11
  681.4 3.4 collective-permute-done.11
  684.8 6.8 divide_subtract_fusion
  (43 shorter events, 8.9 us)
Async XLA Ops:
  7.2 172.4 %all-gather.2.cloned.1.call-start = ((), (), s32[]{:S(2)}) async-start(), calls=%async_computation.1 | async-start | bytes 25952256 | tf_op jit(solution)/shard_map/all_gather | solution.py:814
  8.1 6.3 collective-permute-start.5
  20.2 654.3 %reduce-scatter.2.cloned.1.call-start = ((), (), s32[]{:S(2)}) async-start(), calls=%async_computation.2 | async-start | bytes 25952256 | tf_op jit(solution)/shard_map/reduce_scatter | solution.py:819
  21.3 1.3 collective-permute-start
  22.6 4.4 collective-permute-start.1
  27.0 3.6 collective-permute-start.2
  30.7 7.8 %collective-permute-start.3 = (bf16[7,4096]{1,0:T(8,128)(2,1)S(1)}, bf16[7,4096]{1,0:T(8,128)(2,1)S(1)}, u32[]{:S(2)}, u32[]{:S(2)}) collective-permute-start(bf16[7,4096]{1,0:T(8,128)(2,1)S(1)} %add.65), channel_id=1, source_target_pairs={{0,8},{1,9},{2,10},{3,11},{4,12},{5,13},{6,14},{7,15},{8,0},{9,1},... | collective-permute-start | bytes 172040 | tf_op jit(solution)/shard_map/ppermute | solution.py:739
  38.5 6.4 collective-permute-start.4
  40.6 4.3 copy-start.2
  434.1 15.4 %copy-start.4 = (f32[2,1024]{1,0:T(2,128)S(1)}, f32[2,1024]{1,0:T(2,128)}, u32[]{:S(2)}) copy-start(f32[2,1024]{1,0:T(2,128)} %get-tuple-element.40) | copy-start | bytes 24580
  434.1 16.1 %copy-start.3 = (f32[7]{0:T(128)S(1)}, f32[7]{0:T(128)}, u32[]{:S(2)}) copy-start(f32[7]{0:T(128)} %copy-done.2) | copy-start | bytes 88
  450.3 1.4 collective-permute-start.6
  451.8 4.8 collective-permute-start.7
  456.8 3.9 collective-permute-start.8
  460.7 3.9 collective-permute-start.9
  464.6 220.2 %copy-start = (f32[394112]{0:T(1024)S(1)}, f32[394112]{0:T(1024)}, u32[]{:S(2)}) copy-start(f32[394112]{0:T(1024)} %param.10) | copy-start | bytes 4729348
  464.6 216.7 %collective-permute-start.10 = (f32[7,4096]{1,0:T(8,128)S(1)}, f32[7,4096]{1,0:T(8,128)S(1)}, u32[]{:S(2)}, u32[]{:S(2)}) collective-permute-start(f32[7,4096]{1,0:T(8,128)S(1)} %add.74), channel_id=1, source_target_pairs={{0,16},{1,17},{2,18},{3,19},{4,20},{5,21},{6,22},{7,23},{8,24},{9,... | collective-permute-start | bytes 344072 | tf_op jit(solution)/shard_map/ppermute | solution.py:739
  678.1 6.6 collective-permute-start.11
  681.3 10.3 %copy-start.1 = (f32[7,4096]{1,0:T(8,128)}, f32[7,4096]{1,0:T(8,128)S(1)}, u32[]{:S(2)}) copy-start(f32[7,4096]{1,0:T(8,128)S(1)} %add.75) | copy-start | bytes 344068
Sparse Core Ops, SparseCore 0:
  20.3 159.1 all-gather.1
  434.2 240.2 reduce-scatter.1

commit v2 on v1

--- a/solution.py
+++ b/solution.py
@@ -249,6 +249,16 @@
     )
 
 
+ANYWHERE = pl.BlockSpec(memory_space=pl.ANY)
+
+
+def without(kernel, first, count):
+    def called(*refs):
+        kernel(*refs[:first], *refs[first + count :])
+
+    return called
+
+
 def dot_nn(left, right):
     return lax.dot_general(left, right, (((1,), (0,)), ((), ())), preferred_element_type=F32)
 
@@ -483,12 +493,13 @@
     dv_ref[...] = dv_acc[...].astype(BF)
 
 
-def attend_back(key_len, qkv, grad_mix):
+def attend_back(key_len, qkv, grad_mix, first, count, earlier, waits=()):
     pairs = HEADS // 2
-    block = lambda shift: pl.BlockSpec((1024, LANES), lambda j: (0, shift + j))
+    block = lambda shift: pl.BlockSpec((1024, LANES), lambda j: (0, shift + first + j))
+    kept = () if earlier is None else tuple(earlier)
     return pl.pallas_call(
-        attend_back_kernel,
-        grid=(pairs,),
+        without(attend_back_kernel, 5, len(kept) + len(waits)),
+        grid=(count,),
         out_shape=(jax.ShapeDtypeStruct((1024, D), BF),) * 3,
         in_specs=[
             pl.BlockSpec(memory_space=pltpu.SMEM),
@@ -496,13 +507,15 @@
             block(pairs),
             block(2 * pairs),
             block(0),
-        ],
+        ]
+        + [ANYWHERE] * (len(kept) + len(waits)),
         out_specs=(block(0),) * 3,
+        input_output_aliases={5 + i: i for i in range(len(kept))},
         scratch_shapes=[pltpu.VMEM((1024, LANES), F32)] * 2,
         compiler_params=params_of("arbitrary"),
-        cost_estimate=cost(43e9, 14e6, 16e6),
+        cost_estimate=cost(11e9 * count, 2e6 * count, 4e6 * count),
         name="attend_back",
-    )(key_len, qkv, qkv, qkv, grad_mix)
+    )(key_len, qkv, qkv, qkv, grad_mix, *kept, *waits)
 
 
 def middle_kernel(x_ref, mod_ref, mix_ref, w_ref, mid_ref, low_ref):
@@ -537,8 +550,8 @@
 
 def ffn_kernel(
     mid_ref, mod_ref, low_ref, dy_ref, up_ref, down_ref,
-    out_ref, dmid_ref, low_dmid_ref, dmod_ref, dup_ref, ddown_ref,
-    y_acc, dh_acc, low_t, act_s, du_s,
+    out_ref, dmid_ref, low_dmid_ref, dmod_ref, grads_ref,
+    y_acc, dh_acc, low_t, act_s, du_s, dup_s, ddown_s, sems,
 ):
     step = pl.program_id(0)
     frames = mid_ref.shape[0]
@@ -569,8 +582,42 @@
         du_s[here, :] = grad_hidden
         y_acc[here, :] += dot_nn(act, down)
         dh_acc[here, :] += dot_nt(grad_hidden, up)
-    to_tiles(ddown_ref, 0, dot_tn(act_s[...], dy_ref[...]))
-    to_tiles(dup_ref, 0, dot_nn(low_t[...], du_s[...]))
+    slot = step % 2
+
+    def copies(which, index):
+        return (
+            pltpu.make_async_copy(
+                ddown_s.at[which], grads_ref.at[pl.ds(80 + index * 8, 8)], sems.at[which, 0]
+            ),
+            pltpu.make_async_copy(
+                dup_s.at[which],
+                grads_ref.at[pl.ds(16, 64), pl.ds(index * 4, 4)],
+                sems.at[which, 1],
+            ),
+        )
+
+    @pl.when(step >= 2)
+    def _():
+        for copy in copies(slot, step - 2):
+            copy.wait()
+
+    grad_down = dot_tn(act_s[...], dy_ref[...])
+    for c in range(D // LANES):
+        part = grad_down[:, c * LANES : (c + 1) * LANES].astype(BF).reshape(8, 4, TILE, LANES)
+        for r in range(4):
+            ddown_s[slot, :, r * 8 + c] = part[:, r]
+    grad_up = dot_nn(low_t[...], du_s[...])
+    for c in range(4):
+        part = grad_up[:, c * LANES : (c + 1) * LANES].astype(BF)
+        dup_s[slot, :, c] = part.reshape(64, TILE, LANES)
+    for copy in copies(slot, step):
+        copy.start()
+
+    @pl.when(step == pl.num_programs(0) - 1)
+    def _():
+        for index in (step - 1, step):
+            for copy in copies(index % 2, index):
+                copy.wait()
 
     @pl.when(step == pl.num_programs(0) - 1)
     def _():
@@ -607,8 +654,7 @@
             jax.ShapeDtypeStruct((1024, D), F32),
             jax.ShapeDtypeStruct((1024, D), BF),
             jax.ShapeDtypeStruct((2, D), F32),
-            jax.ShapeDtypeStruct((64, 32, TILE, LANES), BF),
-            jax.ShapeDtypeStruct((256, 8, TILE, LANES), BF),
+            jax.ShapeDtypeStruct((144, 32, TILE, LANES), BF),
         ),
         in_specs=[
             once(1024, D),
@@ -623,8 +669,7 @@
             once(1024, D),
             once(1024, D),
             whole(2, D),
-            pl.BlockSpec((64, chunks, TILE, LANES), lambda j: (0, j, 0, 0)),
-            pl.BlockSpec((width // TILE, 8, TILE, LANES), lambda j: (j, 0, 0, 0)),
+            pl.BlockSpec(memory_space=pl.ANY),
         ),
         scratch_shapes=[
             pltpu.VMEM((1024, D), F32),
@@ -632,6 +677,9 @@
             pltpu.VMEM((D, 1024), BF),
             pltpu.VMEM((1024, width), BF),
             pltpu.VMEM((1024, width), BF),
+            pltpu.VMEM((2, 64, 4, TILE, LANES), BF),
+            pltpu.VMEM((2, 8, 32, TILE, LANES), BF),
+            pltpu.SemaphoreType.DMA((2, 2)),
         ],
         compiler_params=params_of("arbitrary"),
         cost_estimate=cost(52e9, 60e6, 4e6),
@@ -642,26 +690,28 @@
     )
 
 
-def out_back_kernel(mix_ref, dmid_ref, w_ref, dmix_ref, dw_ref):
+def out_back_kernel(mix_ref, dmid_ref, w_ref, grads_ref, dmix_ref, dw_ref):
     weights = from_tiles(w_ref, 0, w_ref.shape[1])
     dmix_ref[...] = dot_nt(dmid_ref[...], weights).astype(BF)
     to_tiles(dw_ref, 0, dot_tn(mix_ref[...], dmid_ref[...]))
 
 
-def out_back(mixture, low_dmid, tiles):
+def out_back(mixture, low_dmid, tiles, grads):
     width = 256
     return pl.pallas_call(
         out_back_kernel,
         grid=(D // width,),
         out_shape=(
             jax.ShapeDtypeStruct((1024, D), BF),
-            jax.ShapeDtypeStruct((64, 8, TILE, LANES), BF),
+            jax.ShapeDtypeStruct((576, 8, TILE, LANES), BF),
         ),
         in_specs=[
             pl.BlockSpec((1024, width), lambda j: (0, j)),
             pl.BlockSpec((1024, D), lambda j: (0, 0)),
             pl.BlockSpec((width // TILE, 8, TILE, LANES), lambda j: (192 * TILE // width + j, 0, 0, 0)),
+            pl.BlockSpec(memory_space=pl.ANY),
         ],
+        input_output_aliases={3: 1},
         out_specs=(
             pl.BlockSpec((1024, width), lambda j: (0, j)),
             pl.BlockSpec((width // TILE, 8, TILE, LANES), lambda j: (j, 0, 0, 0)),
@@ -669,7 +719,7 @@
         compiler_params=params_of("arbitrary"),
         cost_estimate=cost(4.3e9, 10e6),
         name="out_back",
-    )(mixture, low_dmid, tiles.reshape(-1, 8, TILE, LANES))
+    )(mixture, low_dmid, tiles.reshape(-1, 8, TILE, LANES), grads.reshape(-1, 8, TILE, LANES))
 
 
 def qkv_weight_kernel(low_ref, dq_ref, dk_ref, dv_ref, dw_ref):
@@ -677,19 +727,20 @@
         to_tiles(dw_ref, third * 8, dot_tn(low_ref[...], grad_ref[...]))
 
 
-def qkv_weight_grad(low_one, dq, dk, dv):
+def qkv_weight_grad(low_one, dq, dk, dv, waits=()):
     width = 256
     whole = pl.BlockSpec((1024, D), lambda j: (0, 0))
     return pl.pallas_call(
-        qkv_weight_kernel,
+        without(qkv_weight_kernel, 4, len(waits)),
         grid=(D // width,),
         out_shape=jax.ShapeDtypeStruct((64, 24, TILE, LANES), BF),
-        in_specs=[pl.BlockSpec((1024, width), lambda j: (0, j)), whole, whole, whole],
+        in_specs=[pl.BlockSpec((1024, width), lambda j: (0, j)), whole, whole, whole]
+        + [ANYWHERE] * len(waits),
         out_specs=pl.BlockSpec((width // TILE, 24, TILE, LANES), lambda j: (j, 0, 0, 0)),
         compiler_params=params_of("arbitrary"),
         cost_estimate=cost(6.4e9, 15e6),
         name="qkv_weight_grad",
-    )(low_one, dq, dk, dv)
+    )(low_one, dq, dk, dv, *waits)
 
 
 def input_kernel(x_ref, mod_ref, dmid_ref, dq_ref, dk_ref, dv_ref, w_ref, grad_ref, dmod_ref):
@@ -708,11 +759,11 @@
     grad_ref[...] = (dmid_ref[...] + norm_back(zhat, inverse, grad, mod_ref[0:1, :])).astype(BF)
 
 
-def input_back(x, mod, dmid, dq, dk, dv, tiles):
+def input_back(x, mod, dmid, dq, dk, dv, tiles, waits=()):
     rows = 256
     block = pl.BlockSpec((rows, D), lambda i: (i, 0))
     return pl.pallas_call(
-        input_kernel,
+        without(input_kernel, 7, len(waits)),
         grid=(1024 // rows,),
         out_shape=(jax.ShapeDtypeStruct((1024, D), BF), jax.ShapeDtypeStruct((2, D), F32)),
         in_specs=[
@@ -723,12 +774,101 @@
             block,
             block,
             pl.BlockSpec((64, 24, TILE, LANES), lambda i: (0, 0, 0, 0)),
-        ],
+        ]
+        + [ANYWHERE] * len(waits),
         out_specs=(block, pl.BlockSpec((2, D), lambda i: (0, 0))),
         compiler_params=params_of("arbitrary"),
         cost_estimate=cost(6.4e9, 22e6),
         name="input_back",
-    )(x, mod, dmid, dq, dk, dv, tiles.reshape(-1, 24, TILE, LANES))
+    )(x, mod, dmid, dq, dk, dv, tiles.reshape(-1, 24, TILE, LANES), *waits)
+
+
+def tile_spec(*lead, index):
+    return pl.BlockSpec((*lead, TILE, LANES), lambda i, at: (*index(i, at), 0, 0))
+
+
+def staged(kernel, name, outs, out_lead, ins, in_specs, sel, steps, moved, waits):
+    spec = tile_spec(*out_lead, index=lambda i, at: (i,) + (0,) * (len(out_lead) - 1))
+    shape = (steps,) + tuple(out_lead[1:]) + (TILE, LANES)
+    return pl.pallas_call(
+        without(kernel, 1 + len(ins), len(waits)),
+        out_shape=(jax.ShapeDtypeStruct(shape, BF),) * outs,
+        grid_spec=pltpu.PrefetchScalarGridSpec(
+            num_scalar_prefetch=1,
+            grid=(steps,),
+            in_specs=in_specs + [ANYWHERE] * len(waits),
+            out_specs=(spec,) * outs,
+        ),
+        compiler_params=params_of("arbitrary"),
+        cost_estimate=cost(0, moved),
+        name=name,
+    )(sel, *ins, *waits)
+
+
+def take_kernel(sel, value_ref, out_ref):
+    out_ref[...] = value_ref[:, :, :, 0]
+
+
+def take_other(sel, value, waits=()):
+    layers = value.shape[0]
+    spec = tile_spec(1, 2, 2, 1, 192, index=lambda i, at: (i, 0, 0, 1 - at[2], 0))
+    return staged(
+        take_kernel, "take_other", 1, (1, 2, 2, 192), [value], [spec], sel, layers, 6e6 * layers, waits
+    )[0]
+
+
+def both(left, right):
+    return (left.astype(F32) + right.astype(F32)).astype(BF)
+
+
+def core_kernel(sel, value_ref, moved_ref, one_send, one_keep, two_send, two_keep):
+    y, x = sel[0], sel[1]
+    one, two = slice(0, 96), slice(96, 192)
+    for k in range(2):
+        one_send[0, k] = both(value_ref[0, k, 1 - x, 0, one], moved_ref[0, k, 1 - x, one])
+        one_keep[0, k] = both(value_ref[0, k, x, 0, one], moved_ref[0, k, x, one])
+        two_send[0, k] = both(value_ref[0, 1 - y, k, 0, two], moved_ref[0, 1 - y, k, two])
+        two_keep[0, k] = both(value_ref[0, y, k, 0, two], moved_ref[0, y, k, two])
+
+
+def core_sum(sel, value, moved, waits=()):
+    layers = value.shape[0]
+    specs = [
+        tile_spec(1, 2, 2, 1, 192, index=lambda i, at: (i, 0, 0, at[2], 0)),
+        tile_spec(1, 2, 2, 192, index=lambda i, at: (i, 0, 0, 0)),
+    ]
+    return staged(
+        core_kernel, "core_sum", 4, (1, 2, 96), [value, moved], specs, sel, layers, 9e6 * layers, waits
+    )
+
+
+def plane_kernel(sel, one_keep, one_moved, two_keep, two_moved, one_send, one_own, two_send, two_own):
+    y, x = sel[0], sel[1]
+    one_send[0] = both(one_keep[0, 1 - y], one_moved[0, 1 - y])
+    one_own[0] = both(one_keep[0, y], one_moved[0, y])
+    two_send[0] = both(two_keep[0, 1 - x], two_moved[0, 1 - x])
+    two_own[0] = both(two_keep[0, x], two_moved[0, x])
+
+
+def plane_sum(sel, *values, waits=()):
+    layers = values[0].shape[0]
+    spec = tile_spec(1, 2, 96, index=lambda i, at: (i, 0, 0))
+    return staged(
+        plane_kernel, "plane_sum", 4, (1, 96), values, [spec] * 4, sel, layers, 5e6 * layers, waits
+    )
+
+
+def line_kernel(sel, one_own, one_moved, two_own, two_moved, out_ref):
+    out_ref[0, 0:96] = both(one_own[0], one_moved[0])
+    out_ref[0, 96:192] = both(two_own[0], two_moved[0])
+
+
+def line_sum(sel, *values, waits=()):
+    layers = values[0].shape[0]
+    spec = tile_spec(1, 96, index=lambda i, at: (i, 0))
+    return staged(
+        line_kernel, "line_sum", 1, (1, 192), values, [spec] * 4, sel, layers, 2.4e6 * layers, waits
+    )[0]
 
 
 def flat_index():
@@ -765,35 +905,62 @@
         jnp.concatenate([before, params]), (table_size - index * slip,), (aligned,)
     )
     packed = pack_shard(kinds, own.reshape(aligned // LANES, LANES))
-    tiles = gather_tiles(packed, index, count)
+    sel = jnp.stack([index // 4 % 2, index // 2 % 2, index % 2]).astype(jnp.int32)
 
     last = index == count - 1
     table = jnp.where(last, params[shard - table_size :], 0.0).astype(BF)
     table = sum_everywhere(table.reshape(SECTIONS, 4 * D), count)
+    tiles = lax.all_gather(packed, ("dp", "fsdp"), axis=0, tiled=True)
     picker = (section[0] - 1 == jnp.arange(SECTIONS)).astype(F32)[:, None]
     mod = jnp.sum(picker * table.astype(F32), 0).reshape(4, D)
 
     low_one, qkv = project_qkv(x, mod, tiles)
     mixture = attend(key_len, qkv)
     middle, low_two = middle_rows(x, mod, mixture, tiles)
-    block_out, dmid, low_dmid, dmod_two, grad_up, grad_down = ffn_both(
-        middle, mod, low_two, dy, tiles
-    )
-    grad_mix, grad_out = out_back(mixture, low_dmid, tiles)
-    dq, dk, dv = attend_back(key_len, qkv, grad_mix)
-    grad_qkv = qkv_weight_grad(low_one, dq, dk, dv)
-    input_grad, dmod_one = input_back(x, mod, dmid, dq, dk, dv, tiles)
+    block_out, dmid, low_dmid, dmod_two, grads = ffn_both(middle, mod, low_two, dy, tiles)
+    grad_mix, grads = out_back(mixture, low_dmid, tiles, grads)
+
+    grads = grads.reshape(3, 2, 2, 2, 192, TILE, LANES)
+    sent = take_other(sel, grads)
+    moved = exchange(sent, 1, count)
+    back = attend_back(key_len, qkv, grad_mix, 0, 2, None, (sent,))
+    one_send, one_keep, two_send, two_keep = core_sum(sel, grads, moved, back[:1])
+    one_moved, two_moved = exchange(one_send, 2, count), exchange(two_send, 4, count)
+    back = attend_back(key_len, qkv, grad_mix, 2, 2, back, (one_send,))
+    back = attend_back(key_len, qkv, grad_mix, 4, 2, back)
+    dq, dk, dv = attend_back(key_len, qkv, grad_mix, 6, 2, back)
+    one_send, one_keep, two_send, two_keep = plane_sum(
+        sel, one_keep, one_moved, two_keep, two_moved, waits=(dq,)
+    )
+    one_moved, two_moved = exchange(one_send, 4, count), exchange(two_send, 2, count)
+    grad_qkv = qkv_weight_grad(low_one, dq, dk, dv, (one_send,))
+    held = (one_keep, one_moved, two_keep, two_moved)
+
+    grad_qkv = grad_qkv.reshape(1, 2, 2, 2, 192, TILE, LANES)
+    sent = take_other(sel, grad_qkv)
+    moved = exchange(sent, 1, count)
+    one_send, one_keep, two_send, two_keep = core_sum(sel, grad_qkv, moved)
+    one_moved, two_moved = exchange(one_send, 2, count), exchange(two_send, 4, count)
+    rest = line_sum(sel, *held, waits=(one_send,))
+    input_grad, dmod_one = input_back(x, mod, dmid, dq, dk, dv, tiles, (rest,))
+    one_send, one_keep, two_send, two_keep = plane_sum(
+        sel, one_keep, one_moved, two_keep, two_moved, waits=(input_grad,)
+    )
+    one_moved, two_moved = exchange(one_send, 4, count), exchange(two_send, 2, count)
+    first = line_sum(sel, one_keep, one_moved, two_keep, two_moved)
 
     per_item = jnp.concatenate([dmod_one, dmod_two], 0).reshape(1, 4 * D)
     section_grad = sum_everywhere(picker * per_item, count)
 
-    reduced = reduce_tiles(grad_qkv, grad_out, grad_up, grad_down, index, count)
+    reduced = jnp.where(
+        index // 8 == 0, reduce_first(first[0], count), reduce_rest(rest, index, count)
+    ).reshape(192, TILE, LANES)
     summed = unpack_shard(kinds, reduced).reshape(aligned)
-    after = lax.ppermute(
+    following = lax.ppermute(
         summed[:table_size], ("dp", "fsdp"), [(i, i - 1) for i in range(1, count)]
     )
-    after = jnp.where(last, section_grad.reshape(table_size), after)
-    param_grad = lax.dynamic_slice(jnp.concatenate([summed, after]), (index * slip,), (shard,))
+    following = jnp.where(last, section_grad.reshape(table_size), following)
+    param_grad = lax.dynamic_slice(jnp.concatenate([summed, following]), (index * slip,), (shard,))
     new_first = beta_one * first_moment + (1.0 - beta_one) * param_grad
     new_second = beta_two * second_moment + (1.0 - beta_two) * param_grad * param_grad
     new_params = params - learn_rate * (new_first / bias_one) / (
@@ -810,15 +977,40 @@
     )
 
 
-def gather_tiles(packed, index, count):
-    return lax.all_gather(packed, ("dp", "fsdp"), axis=0, tiled=True)
-
-
-def reduce_tiles(grad_qkv, grad_out, grad_up, grad_down, index, count):
-    parts = [g.reshape(-1, TILE, LANES) for g in (grad_qkv, grad_out, grad_up, grad_down)]
-    return lax.psum_scatter(
-        jnp.concatenate(parts, 0), ("dp", "fsdp"), scatter_dimension=0, tiled=True
-    )
+def add_low(*terms):
+    return add_wide(*terms).astype(BF)
+
+
+def add_wide(*terms):
+    total = terms[0].astype(F32)
+    for term in terms[1:]:
+        total = total + term.astype(F32)
+    return total
+
+
+def layer_move(value, moves):
+    pairs = [(8 * a + i, 8 * b + i) for a, b in moves for i in range(8)]
+    return lax.ppermute(value, ("dp", "fsdp"), pairs)
+
+
+def pick(value, index, axis):
+    return lax.dynamic_index_in_dim(value, index, axis, keepdims=False)
+
+
+def reduce_first(value, count):
+    value = add_low(value, layer_move(value, [(3, 2), (1, 0)]))
+    return add_wide(value, layer_move(value, [(2, 0)]))
+
+
+def reduce_rest(value, index, count):
+    layer = index // 8
+    choose = lambda at: pick(value, jnp.clip(at, 0, 2), 0)
+    up = layer_move(value[2], [(0, 1)])
+    down = layer_move(value[0], [(3, 2)])
+    up = layer_move(add_low(choose(1 + layer), up), [(0, 1), (1, 2)])
+    down = layer_move(add_low(choose(layer - 2), down), [(3, 2), (2, 1)])
+    up = layer_move(add_low(choose(layer), up), [(0, 1), (1, 2), (2, 3)])
+    return add_wide(choose(layer - 1), up, down)
 
 
 def solution(mesh):

time: 708 us -> 621 us (0.88)
  waiting for transfers between devices: 372 us -> 212 us
  Pallas kernels: 247 us -> 308 us
  starting transfers between devices: 20.4 us -> 49.3 us
  other arithmetic: 41.3 us -> 21.7 us
    reduce_scatter x1 -> x0, waiting for transfers between devices: 209 us -> none  [reduce_tiles(): lax.psum_scatter(jnp.concatenate(parts, 0), ('dp', 'fsdp'), scatter_dimen...]
    pallas_call x3 -> x14, Pallas kernels: 103 us -> 160 us  [the longest x4 82.3 us: attend_back(): pl.pallas_call(without(attend_back_kernel, 5, len(kept) + len(waits)), gr...]
    concatenate x1 -> x0, other arithmetic: 28.7 us -> none  [reduce_tiles(): jnp.concatenate(parts, 0)]
    ppermute x0 -> x7, waiting for transfers between devices: none -> 26.5 us  [layer_move(): return lax.ppermute(value, ('dp', 'fsdp'), pairs)]
    ppermute x10 -> x20, waiting for transfers between devices: 24.4 us -> 47.4 us  [exchange(): lax.ppermute(value, ('dp', 'fsdp'), [(i, i ^ mask) for i in range(count)])]
    ppermute x10 -> x20, starting transfers between devices: 12.7 us -> 26.8 us  [exchange(): lax.ppermute(value, ('dp', 'fsdp'), [(i, i ^ mask) for i in range(count)])]
    ppermute x0 -> x7, starting transfers between devices: none -> 12.6 us  [layer_move(): return lax.ppermute(value, ('dp', 'fsdp'), pairs)]
  transfers between devices with their start and end apart: 14 -> 30, of which waited for: 13 -> 17; matrix products, arithmetic and copies ran while one was open for 1% -> 3% of each run, Pallas kernels for 3% -> 19%
where the time goes in v2:
time: 621 us; the launch traced here: 612 us
  Pallas kernels  308 us (50%)
  waiting for transfers between devices  212 us (34%)
  starting transfers between devices  49.3 us (8%)
  other arithmetic  21.7 us (3%)
  between operations  16.1 us (3%)
    all_gather x1, waiting for transfers between devices, fast_device(): tiles = lax.all_gather(packed, ('dp', 'fsdp'), axis=0, tiled=True)  134 us
    pallas_call x4, Pallas kernels, attend_back(): pl.pallas_call(without(attend_back_kernel, 5, len(kept) + len(waits)), gr...  82.3 us
    pallas_call x1, Pallas kernels, ffn_both(): pl.pallas_call(ffn_kernel, grid=(steps,), out_shape=(jax.ShapeDtypeStruct...  73.5 us
    pallas_call x8, Pallas kernels, staged(): pl.pallas_call(without(kernel, 1 + len(ins), len(waits)), out_shape=(jax....  50.9 us
    ppermute x20, waiting for transfers between devices, exchange(): lax.ppermute(value, ('dp', 'fsdp'), [(i, i ^ mask) for i in range(count)])  47.4 us
    pallas_call x1, Pallas kernels, attend(): pl.pallas_call(attend_kernel, grid=(pairs,), out_shape=jax.ShapeDtypeStru...  39.8 us
    ppermute x20, starting transfers between devices, exchange(): lax.ppermute(value, ('dp', 'fsdp'), [(i, i ^ mask) for i in range(count)])  26.8 us
    ppermute x7, waiting for transfers between devices, layer_move(): return lax.ppermute(value, ('dp', 'fsdp'), pairs)  26.5 us
  transfers between devices with their start and end apart: 30, of which 17 were waited for; matrix products, arithmetic and copies ran while one was open for 3% of the time, Pallas kernels for 19%

profile of v2, /device:TPU:1, one launch (start us, length us, event | category | flops | bytes accessed | tf_op | source)
XLA Modules:
  0.0 612.4 jit_solution(7959864332741764700)
XLA Ops:
  8.1 4.5 collective-permute-start.5
  33.2 4.7 collective-permute-done.3
  41.2 3.7 collective-permute-done.4
  45.6 134.0 %all-gather.2.cloned.1.call-done = bf16[6144,16,128]{2,1,0:T(8,128)(2,1)} async-done(((bf16[192,16,128]{2,1,0:T(8,128)(2,1)}), bf16[6144,16,128]{2,1,0:T(8,128)(2,1)}) %all-gather.2.cloned.1.call-update) | async-done | bytes 25165840 | tf_op jit(solution)/shard_map/all_gather | solution.py:913
  179.6 12.9 %project_qkv.1 = (bf16[1024,1024]{1,0:T(8,128)(2,1)}, bf16[1024,3072]{1,0:T(8,128)(2,1)}) custom-call(bf16[1024,1024]{1,0:T(8,128)(2,1)} %bitcast.53, f32[4,1024]{1,0:T(4,128)} %reshape.71.mod_ref.refs_1_, bf16[256,24,16,128]{3,2,1,0:T(8,128)(2,1)} %bitcast.42), custom_call_target="tpu_custom_call" | custom-call | flops 6400000000 | bytes 18000000 | tf_op jit(solution)/shard_map/project_qkv/pallas_call | solution.py:392
  192.4 39.8 %attend.1.mix_ref = bf16[1024,1024]{1,0:T(8,128)(2,1)} custom-call(s32[1]{0:T(128)S(6)} %copy.37.len_ref.refs_0_, bf16[1024,3072]{1,0:T(8,128)(2,1)} %get-tuple-element.48.q_ref.k_ref.v_ref.refs_1_.refs_2_.refs_3_, bf16[1024,3072]{1,0:T(8,128)(2,1)} %get-tuple-element.48.q_ref.k_ref.v_ref.refs_1_.refs_2_.refs_3_, ...), custom_call_target="tpu_custom_call" | custom-call | flops 16999999488 | bytes 8000000 | tf_op jit(solution)/shard_map/attend/pallas_call | solution.py:441
  232.3 7.4 %middle_rows.1 = (f32[1024,1024]{1,0:T(8,128)}, bf16[1024,1024]{1,0:T(8,128)(2,1)}) custom-call(bf16[1024,1024]{1,0:T(8,128)(2,1)} %bitcast.54, f32[4,1024]{1,0:T(4,128)} %reshape.71.mod_ref.refs_1_, bf16[1024,1024]{1,0:T(8,128)(2,1)} %attend.1.mix_ref, bf16[768,8,16,128]{3,2,1,0:T(8,128)(2,1)} %bitcast.43), custom_call_target="tpu_custom_call" | custom-call | flops 2200000000 | bytes 12000000 | tf_op jit(solution)/shard_map/middle_rows/pallas_call | solution.py:531
  239.7 73.5 %ffn_both.1 = (bf16[1024,1024]{1,0:T(8,128)(2,1)}, f32[1024,1024]{1,0:T(8,128)}, bf16[1024,1024]{1,0:T(8,128)(2,1)}, f32[2,1024]{1,0:T(2,128)}, bf16[144,32,16,128]{3,2,1,0:T(8,128)(2,1)}) custom-call(f32[1024,1024]{1,0:T(8,128)} %get-tuple-element.49.mid_ref, f32[4,1024]{1,0:T(4,128)} %reshape.71.mod_ref.refs_1_, ...), custom_call_target="tpu_custom_call" | custom-call | flops 51999997952 | bytes 60000000 | tf_op jit(solution)/shard_map/ffn_both/pallas_call | solution.py:649
  313.1 8.5 %out_back.1 = (bf16[1024,1024]{1,0:T(8,128)(2,1)}, bf16[576,8,16,128]{3,2,1,0:T(8,128)(2,1)}) custom-call(bf16[1024,1024]{1,0:T(8,128)(2,1)} %attend.1.mix_ref, bf16[1024,1024]{1,0:T(8,128)(2,1)} %get-tuple-element.53.dmid_ref, bf16[768,8,16,128]{3,2,1,0:T(8,128)(2,1)} %bitcast.46, bf16[576,8,16,128]{3,2,1,0:T(8,128)(2,1)} %bitcast.48), custom_call_target="tpu_custom_call", output_to_operand_aliasing={{1}: (3, {})} | custom-call | flops 4300000256 | bytes 10000000 | tf_op jit(solution)/shard_map/out_back/pallas_call | solution.py:701
  321.6 9.0 %take_other.2.refs_5_ = bf16[3,2,2,192,16,128]{5,4,3,2,1,0:T(8,128)(2,1)} custom-call(s32[3]{0:T(128)} %pad_add_fusion.refs_0_, bf16[3,2,2,2,192,16,128]{6,5,4,3,2,1,0:T(8,128)(2,1)} %bitcast.49), custom_call_target="tpu_custom_call" | custom-call | bytes 18000000 | tf_op jit(solution)/shard_map/take_other/pallas_call | solution.py:793
  330.9 20.6 %attend_back.4 = (bf16[1024,1024]{1,0:T(8,128)(2,1)}, bf16[1024,1024]{1,0:T(8,128)(2,1)}, bf16[1024,1024]{1,0:T(8,128)(2,1)}) custom-call(s32[1]{0:T(128)S(6)} %copy.37.len_ref.refs_0_, bf16[1024,3072]{1,0:T(8,128)(2,1)} %get-tuple-element.48.q_ref.k_ref.v_ref.refs_1_.refs_2_.refs_3_, ...), custom_call_target="tpu_custom_call" | custom-call | flops 22000001024 | bytes 4000000 | tf_op jit(solution)/shard_map/attend_back/pallas_call | solution.py:500
  351.5 11.9 %core_sum.2 = (bf16[3,2,96,16,128]{4,3,2,1,0:T(8,128)(2,1)}, bf16[3,2,96,16,128]{4,3,2,1,0:T(8,128)(2,1)}, bf16[3,2,96,16,128]{4,3,2,1,0:T(8,128)(2,1)}, bf16[3,2,96,16,128]{4,3,2,1,0:T(8,128)(2,1)}) custom-call(s32[3]{0:T(128)} %pad_add_fusion.refs_0_, bf16[3,2,2,2,192,16,128]{6,5,4,3,2,1,0:T(8,128)(2,1)} %bitcast.50, ...), custom_call_target="tpu_custom_call" | custom-call | bytes 27000000 | tf_op jit(solution)/shard_map/core_sum/pallas_call | solution.py:793
  364.8 20.7 %attend_back.5 = (bf16[1024,1024]{1,0:T(8,128)(2,1)}, bf16[1024,1024]{1,0:T(8,128)(2,1)}, bf16[1024,1024]{1,0:T(8,128)(2,1)}) custom-call(s32[1]{0:T(128)S(6)} %copy.37.len_ref.refs_0_, bf16[1024,3072]{1,0:T(8,128)(2,1)} %get-tuple-element.48.q_ref.k_ref.v_ref.refs_1_.refs_2_.refs_3_, ...), custom_call_target="tpu_custom_call", output_to_operand_aliasing={{0}: (5, {}), {1}: (6, {}), {2}: (7, {})} | custom-call | flops 22000001024 | bytes 4000000 | tf_op jit(solution)/shard_map/attend_back/pallas_call | solution.py:500
  385.6 20.5 %attend_back.6 = (bf16[1024,1024]{1,0:T(8,128)(2,1)}, bf16[1024,1024]{1,0:T(8,128)(2,1)}, bf16[1024,1024]{1,0:T(8,128)(2,1)}) custom-call(s32[1]{0:T(128)S(6)} %copy.37.len_ref.refs_0_, bf16[1024,3072]{1,0:T(8,128)(2,1)} %get-tuple-element.48.q_ref.k_ref.v_ref.refs_1_.refs_2_.refs_3_, ...), custom_call_target="tpu_custom_call", output_to_operand_aliasing={{0}: (5, {}), {1}: (6, {}), {2}: (7, {})} | custom-call | flops 22000001024 | bytes 4000000 | tf_op jit(solution)/shard_map/attend_back/pallas_call | solution.py:500
  406.1 20.5 %attend_back.7 = (bf16[1024,1024]{1,0:T(8,128)(2,1)}, bf16[1024,1024]{1,0:T(8,128)(2,1)}, bf16[1024,1024]{1,0:T(8,128)(2,1)}) custom-call(s32[1]{0:T(128)S(6)} %copy.37.len_ref.refs_0_, bf16[1024,3072]{1,0:T(8,128)(2,1)} %get-tuple-element.48.q_ref.k_ref.v_ref.refs_1_.refs_2_.refs_3_, ...), custom_call_target="tpu_custom_call", output_to_operand_aliasing={{0}: (5, {}), {1}: (6, {}), {2}: (7, {})} | custom-call | flops 22000001024 | bytes 4000000 | tf_op jit(solution)/shard_map/attend_back/pallas_call | solution.py:500
  426.6 7.4 %plane_sum.2 = (bf16[3,96,16,128]{3,2,1,0:T(8,128)(2,1)}, bf16[3,96,16,128]{3,2,1,0:T(8,128)(2,1)}, bf16[3,96,16,128]{3,2,1,0:T(8,128)(2,1)}, bf16[3,96,16,128]{3,2,1,0:T(8,128)(2,1)}) custom-call(s32[3]{0:T(128)} %pad_add_fusion.refs_0_, bf16[3,2,96,16,128]{4,3,2,1,0:T(8,128)(2,1)} %get-tuple-element.70.refs_1_, ...), custom_call_target="tpu_custom_call" | custom-call | bytes 15000000 | tf_op jit(solution)/shard_map/plane_sum/pallas_call | solution.py:793
  434.0 11.8 %qkv_weight_grad.1 = bf16[64,24,16,128]{3,2,1,0:T(8,128)(2,1)} custom-call(bf16[1024,1024]{1,0:T(8,128)(2,1)} %get-tuple-element.77.refs_0_, bf16[1024,1024]{1,0:T(8,128)(2,1)} %get-tuple-element.67.refs_5_.refs_1_.refs_3_, bf16[1024,1024]{1,0:T(8,128)(2,1)} %get-tuple-element.68.refs_2_.refs_4_, bf16[1024,1024]{1,0:T(8,128)(2,1)} %get-tuple-element.69.refs_3_.refs_5_, ...), custom_call_target="tpu_custom_call" | custom-call | flops 6400000000 | bytes 15000000 | tf_op jit(solution)/shard_map/qkv_weight_grad/pallas_call | solution.py:733
  445.8 4.5 take_other.3
  452.5 4.2 collective-permute-done.11.refs_2_
  456.7 5.8 core_sum.3
  464.0 14.9 %collective-permute-done.10.refs_4_ = bf16[3,96,16,128]{3,2,1,0:T(8,128)(2,1)S(1)} collective-permute-done((bf16[3,96,16,128]{3,2,1,0:T(8,128)(2,1)}, bf16[3,96,16,128]{3,2,1,0:T(8,128)(2,1)S(1)}, u32[]{:S(2)}, u32[]{:S(2)}) %collective-permute-start.10) | collective-permute-done | bytes 1179680 | tf_op jit(solution)/shard_map/ppermute | solution.py:879
  479.9 5.3 line_sum.2.refs_7_
  490.1 15.0 %input_back.1 = (bf16[1024,1024]{1,0:T(8,128)(2,1)}, f32[2,1024]{1,0:T(2,128)}) custom-call(bf16[1024,1024]{1,0:T(8,128)(2,1)} %bitcast.55, f32[4,1024]{1,0:T(4,128)} %reshape.71.mod_ref.refs_1_, f32[1024,1024]{1,0:T(8,128)} %get-tuple-element.52.refs_2_, bf16[1024,1024]{1,0:T(8,128)(2,1)} %get-tuple-element.67.refs_5_.refs_1_.refs_3_, ...), custom_call_target="tpu_custom_call" | custom-call | flops 6400000000 | bytes 22000000 | tf_op jit(solution)/shard_map/input_back/pallas_call | solution.py:765
  505.9 4.0 plane_sum.3
  525.1 9.9 %collective-permute-done.19 = bf16[192,16,128]{2,1,0:T(8,128)(2,1)} collective-permute-done((bf16[192,16,128]{2,1,0:T(8,128)(2,1)}, bf16[192,16,128]{2,1,0:T(8,128)(2,1)}, u32[]{:S(2)}, u32[]{:S(2)}) %collective-permute-start.19) | collective-permute-done | bytes 786464 | tf_op jit(solution)/shard_map/ppermute | solution.py:993
  537.9 4.1 collective-permute-start.20
  551.0 10.3 %collective-permute-done.26 = f32[7,4096]{1,0:T(8,128)S(1)} collective-permute-done((f32[7,4096]{1,0:T(8,128)S(1)}, f32[7,4096]{1,0:T(8,128)S(1)}, u32[]{:S(2)}, u32[]{:S(2)}) %collective-permute-start.26) | collective-permute-done | bytes 114720 | tf_op jit(solution)/shard_map/ppermute | solution.py:879
  561.4 4.8 collective-permute-start.27
  566.2 16.6 %collective-permute-done.17 = bf16[192,16,128]{2,1,0:T(8,128)(2,1)} collective-permute-done((bf16[192,16,128]{2,1,0:T(8,128)(2,1)S(1)}, bf16[192,16,128]{2,1,0:T(8,128)(2,1)}, u32[]{:S(2)}, u32[]{:S(2)}) %collective-permute-start.17) | collective-permute-done | bytes 786464 | tf_op jit(solution)/shard_map/ppermute | solution.py:993
  582.8 3.2 fusion.8.tiles_ref
  589.9 5.3 collective-permute-start.28
  598.3 6.8 %divide_subtract_fusion = (f32[394112]{0:T(1024)}, f32[394112]{0:T(1024)}, f32[394112]{0:T(1024)}, f32[394112]{0:T(1024)}) fusion(f32[394112]{0:T(1024)S(1)} %copy-done, f32[394112]{0:T(1024)} %param.11, f32[394112]{0:T(1024)} %param.12, s32[]{:T(128)S(6)} %select_n.83, f32[28672]{0:T(1024)S(1)} %broadcast_select_fusion, f32[393216]{0:T(1024)} %bitcast.56), kind=kLoop, calls=%fused_computation.7 | loop fusion | flops 5123456 | bytes 12722692 | tf_op jit(solution)/shard_map/sub | solution.py:966
  (94 shorter events, 70.2 us)
Async XLA Ops:
  7.2 172.4 %all-gather.2.cloned.1.call-start = ((), (), s32[]{:S(2)}) async-start(), calls=%async_computation | async-start | bytes 25952256 | tf_op jit(solution)/shard_map/all_gather | solution.py:913
  8.1 6.3 %collective-permute-start.5 = (f32[28672]{0:T(1024)S(1)}, f32[28672]{0:T(1024)S(1)}, u32[]{:S(2)}, u32[]{:S(2)}) collective-permute-start(f32[28672]{0:T(1024)S(1)} %slice.16), channel_id=1, source_target_pairs={{0,1},{1,2},{2,3},{3,4},{4,5},{5,6},{6,7},{7,8},{8,9},{9,10},{10,1... | collective-permute-start | bytes 344072 | tf_op jit(solution)/shard_map/ppermute | solution.py:901
  21.2 1.3 collective-permute-start
  22.6 4.4 collective-permute-start.1
  27.0 3.6 collective-permute-start.2
  30.6 7.3 %collective-permute-start.3 = (bf16[7,4096]{1,0:T(8,128)(2,1)S(1)}, bf16[7,4096]{1,0:T(8,128)(2,1)S(1)}, u32[]{:S(2)}, u32[]{:S(2)}) collective-permute-start(bf16[7,4096]{1,0:T(8,128)(2,1)S(1)} %add.107), channel_id=1, source_target_pairs={{0,8},{1,9},{2,10},{3,11},{4,12},{5,13},{6,14},{7,15},{8,0},{9,1},... | collective-permute-start | bytes 172040 | tf_op jit(solution)/shard_map/ppermute | solution.py:879
  38.0 6.9 %collective-permute-start.4 = (bf16[7,4096]{1,0:T(8,128)(2,1)S(1)}, bf16[7,4096]{1,0:T(8,128)(2,1)S(1)}, u32[]{:S(2)}, u32[]{:S(2)}) collective-permute-start(bf16[7,4096]{1,0:T(8,128)(2,1)S(1)} %add.108), channel_id=1, source_target_pairs={{0,16},{1,17},{2,18},{3,19},{4,20},{5,21},{6,22},{7,23},{8,24},{9,... | collective-permute-start | bytes 172040 | tf_op jit(solution)/shard_map/ppermute | solution.py:879
  330.6 20.8 %collective-permute-start.6 = (bf16[3,2,2,192,16,128]{5,4,3,2,1,0:T(8,128)(2,1)}, bf16[3,2,2,192,16,128]{5,4,3,2,1,0:T(8,128)(2,1)}, u32[]{:S(2)}, u32[]{:S(2)}) collective-permute-start(bf16[3,2,2,192,16,128]{5,4,3,2,1,0:T(8,128)(2,1)} %take_other.2.refs_5_), channel_id=1, source_target_pairs={{0,1},{1,0},{2,3},{3,2},{4,5},{5,4},{6,7},{7,6},{8,9},{9,8},{10,11... | collective-permute-start | bytes 28311560 | tf_op jit(solution)/shard_map/ppermute | solution.py:879
  363.4 63.2 %collective-permute-start.7 = (bf16[3,2,96,16,128]{4,3,2,1,0:T(8,128)(2,1)}, bf16[3,2,96,16,128]{4,3,2,1,0:T(8,128)(2,1)}, u32[]{:S(2)}, u32[]{:S(2)}) collective-permute-start(bf16[3,2,96,16,128]{4,3,2,1,0:T(8,128)(2,1)} %get-tuple-element.60.refs_8_), channel_id=1, source_target_pairs={{0,2},{1,3},{2,0},{3,1},{4,6},{5,7},{6,4},{7,5},{8,10},{9,11},{10,... | collective-permute-start | bytes 7077896 | tf_op jit(solution)/shard_map/ppermute | solution.py:879
  364.5 62.1 %collective-permute-start.8 = (bf16[3,2,96,16,128]{4,3,2,1,0:T(8,128)(2,1)}, bf16[3,2,96,16,128]{4,3,2,1,0:T(8,128)(2,1)}, u32[]{:S(2)}, u32[]{:S(2)}) collective-permute-start(bf16[3,2,96,16,128]{4,3,2,1,0:T(8,128)(2,1)} %get-tuple-element.72), channel_id=1, source_target_pairs={{0,4},{1,5},{2,6},{3,7},{4,0},{5,1},{6,2},{7,3},{8,12},{9,13},{10,... | collective-permute-start | bytes 7077896 | tf_op jit(solution)/shard_map/ppermute | solution.py:879
  450.3 6.4 %collective-permute-start.11 = (bf16[1,2,2,192,16,128]{5,4,3,2,1,0:T(8,128)(2,1)}, bf16[1,2,2,192,16,128]{5,4,3,2,1,0:T(8,128)(2,1)}, u32[]{:S(2)}, u32[]{:S(2)}) collective-permute-start(bf16[1,2,2,192,16,128]{5,4,3,2,1,0:T(8,128)(2,1)} %take_other.3), channel_id=1, source_target_pairs={{0,1},{1,0},{2,3},{3,2},{4,5},{5,4},{6,7},{7,6},{8,9},{9,8},{10,11... | collective-permute-start | bytes 9437192 | tf_op jit(solution)/shard_map/ppermute | solution.py:879
  451.1 27.8 %collective-permute-start.10 = (bf16[3,96,16,128]{3,2,1,0:T(8,128)(2,1)}, bf16[3,96,16,128]{3,2,1,0:T(8,128)(2,1)S(1)}, u32[]{:S(2)}, u32[]{:S(2)}) collective-permute-start(bf16[3,96,16,128]{3,2,1,0:T(8,128)(2,1)} %get-tuple-element.76), channel_id=1, source_target_pairs={{0,2},{1,3},{2,0},{3,1},{4,6},{5,7},{6,4},{7,5},{8,10},{9,11},{10,... | collective-permute-start | bytes 3538952 | tf_op jit(solution)/shard_map/ppermute | solution.py:879
  452.3 27.6 %collective-permute-start.9 = (bf16[3,96,16,128]{3,2,1,0:T(8,128)(2,1)}, bf16[3,96,16,128]{3,2,1,0:T(8,128)(2,1)}, u32[]{:S(2)}, u32[]{:S(2)}) collective-permute-start(bf16[3,96,16,128]{3,2,1,0:T(8,128)(2,1)} %get-tuple-element.74.refs_4_), channel_id=1, source_target_pairs={{0,4},{1,5},{2,6},{3,7},{4,0},{5,1},{6,2},{7,3},{8,12},{9,13},{10,... | collective-permute-start | bytes 3538952 | tf_op jit(solution)/shard_map/ppermute | solution.py:879
  462.5 43.4 %collective-permute-start.12 = (bf16[1,2,96,16,128]{4,3,2,1,0:T(8,128)(2,1)}, bf16[1,2,96,16,128]{4,3,2,1,0:T(8,128)(2,1)}, u32[]{:S(2)}, u32[]{:S(2)}) collective-permute-start(bf16[1,2,96,16,128]{4,3,2,1,0:T(8,128)(2,1)} %get-tuple-element.78.refs_5_), channel_id=1, source_target_pairs={{0,2},{1,3},{2,0},{3,1},{4,6},{5,7},{6,4},{7,5},{8,10},{9,11},{10,... | collective-permute-start | bytes 2359304 | tf_op jit(solution)/shard_map/ppermute | solution.py:879
  463.7 42.2 %collective-permute-start.13 = (bf16[1,2,96,16,128]{4,3,2,1,0:T(8,128)(2,1)}, bf16[1,2,96,16,128]{4,3,2,1,0:T(8,128)(2,1)}, u32[]{:S(2)}, u32[]{:S(2)}) collective-permute-start(bf16[1,2,96,16,128]{4,3,2,1,0:T(8,128)(2,1)} %get-tuple-element.82), channel_id=1, source_target_pairs={{0,4},{1,5},{2,6},{3,7},{4,0},{5,1},{6,2},{7,3},{8,12},{9,13},{10,... | collective-permute-start | bytes 2359304 | tf_op jit(solution)/shard_map/ppermute | solution.py:879
  488.0 26.1 %collective-permute-start.18 = (bf16[192,16,128]{2,1,0:T(8,128)(2,1)}, bf16[192,16,128]{2,1,0:T(8,128)(2,1)S(1)}, u32[]{:S(2)}, u32[]{:S(2)}) collective-permute-start(bf16[192,16,128]{2,1,0:T(8,128)(2,1)} %get-tuple-element.95), channel_id=1, source_target_pairs={{0,8},{1,9},{2,10},{3,11},{4,12},{5,13},{6,14},{7,15}} | collective-permute-start | bytes 2359304 | tf_op jit(solution)/shard_map/ppermute | solution.py:993
  489.4 35.7 %collective-permute-start.21 = (bf16[192,16,128]{2,1,0:T(8,128)(2,1)}, bf16[192,16,128]{2,1,0:T(8,128)(2,1)S(1)}, u32[]{:S(2)}, u32[]{:S(2)}) collective-permute-start(bf16[192,16,128]{2,1,0:T(8,128)(2,1)} %get-tuple-element.96), channel_id=1, source_target_pairs={{24,16},{25,17},{26,18},{27,19},{28,20},{29,21},{30,22},{31,23}} | collective-permute-start | bytes 2359304 | tf_op jit(solution)/shard_map/ppermute | solution.py:993
  490.1 15.0 %copy-start.6 = (f32[2,1024]{1,0:T(2,128)S(1)}, f32[2,1024]{1,0:T(2,128)}, u32[]{:S(2)}) copy-start(f32[2,1024]{1,0:T(2,128)} %get-tuple-element.88) | copy-start | bytes 24580
  509.9 8.9 %collective-permute-start.14 = (bf16[1,96,16,128]{3,2,1,0:T(8,128)(2,1)}, bf16[1,96,16,128]{3,2,1,0:T(8,128)(2,1)}, u32[]{:S(2)}, u32[]{:S(2)}) collective-permute-start(bf16[1,96,16,128]{3,2,1,0:T(8,128)(2,1)} %get-tuple-element.84), channel_id=1, source_target_pairs={{0,4},{1,5},{2,6},{3,7},{4,0},{5,1},{6,2},{7,3},{8,12},{9,13},{10,... | collective-permute-start | bytes 1179656 | tf_op jit(solution)/shard_map/ppermute | solution.py:879
  511.0 9.2 %collective-permute-start.15 = (bf16[1,96,16,128]{3,2,1,0:T(8,128)(2,1)}, bf16[1,96,16,128]{3,2,1,0:T(8,128)(2,1)}, u32[]{:S(2)}, u32[]{:S(2)}) collective-permute-start(bf16[1,96,16,128]{3,2,1,0:T(8,128)(2,1)} %get-tuple-element.86), channel_id=1, source_target_pairs={{0,2},{1,3},{2,0},{3,1},{4,6},{5,7},{6,4},{7,5},{8,10},{9,11},{10,... | collective-permute-start | bytes 1179656 | tf_op jit(solution)/shard_map/ppermute | solution.py:879
  511.4 13.2 %collective-permute-start.23 = (f32[7,4096]{1,0:T(8,128)S(1)}, f32[7,4096]{1,0:T(8,128)S(1)}, u32[]{:S(2)}, u32[]{:S(2)}) collective-permute-start(f32[7,4096]{1,0:T(8,128)S(1)} %broadcast_multiply_fusion), channel_id=1, source_target_pairs={{0,1},{1,0},{2,3},{3,2},{4,5},{5,4},{6,7},{7,6},{8,9},{9,8},{10,11... | collective-permute-start | bytes 344072 | tf_op jit(solution)/shard_map/ppermute | solution.py:879
  516.3 18.7 %collective-permute-start.19 = (bf16[192,16,128]{2,1,0:T(8,128)(2,1)}, bf16[192,16,128]{2,1,0:T(8,128)(2,1)}, u32[]{:S(2)}, u32[]{:S(2)}) collective-permute-start(bf16[192,16,128]{2,1,0:T(8,128)(2,1)} %fusion.5), channel_id=1, source_target_pairs={{0,8},{1,9},{2,10},{3,11},{4,12},{5,13},{6,14},{7,15},{8,16},{9,17... | collective-permute-start | bytes 2359304 | tf_op jit(solution)/shard_map/ppermute | solution.py:993
  523.3 20.3 %collective-permute-start.16 = (bf16[192,16,128]{2,1,0:T(8,128)(2,1)}, bf16[192,16,128]{2,1,0:T(8,128)(2,1)S(1)}, u32[]{:S(2)}, u32[]{:S(2)}) collective-permute-start(bf16[192,16,128]{2,1,0:T(8,128)(2,1)} %bitcast.57), channel_id=1, source_target_pairs={{24,16},{25,17},{26,18},{27,19},{28,20},{29,21},{30,22},{31,23},{8... | collective-permute-start | bytes 2359304 | tf_op jit(solution)/shard_map/ppermute | solution.py:993
  524.7 18.9 %copy-start.1 = (bf16[1,192,16,128]{3,2,1,0:T(8,128)(2,1)S(1)}, bf16[1,192,16,128]{3,2,1,0:T(8,128)(2,1)}, u32[]{:S(2)}) copy-start(bf16[1,192,16,128]{3,2,1,0:T(8,128)(2,1)} %line_sum.3) | copy-start | bytes 2359300
  524.7 20.4 %collective-permute-start.24 = (f32[7,4096]{1,0:T(8,128)S(1)}, f32[7,4096]{1,0:T(8,128)S(1)}, u32[]{:S(2)}, u32[]{:S(2)}) collective-permute-start(f32[7,4096]{1,0:T(8,128)S(1)} %fusion.9), channel_id=1, source_target_pairs={{0,2},{1,3},{2,0},{3,1},{4,6},{5,7},{6,4},{7,5},{8,10},{9,11},{10,... | collective-permute-start | bytes 344072 | tf_op jit(solution)/shard_map/ppermute | solution.py:879
  537.9 28.2 %collective-permute-start.20 = (bf16[192,16,128]{2,1,0:T(8,128)(2,1)}, bf16[192,16,128]{2,1,0:T(8,128)(2,1)S(1)}, u32[]{:S(2)}, u32[]{:S(2)}) collective-permute-start(bf16[192,16,128]{2,1,0:T(8,128)(2,1)} %get-tuple-element.93), channel_id=1, source_target_pairs={{0,8},{1,9},{2,10},{3,11},{4,12},{5,13},{6,14},{7,15},{8,16},{9,17... | collective-permute-start | bytes 2359304 | tf_op jit(solution)/shard_map/ppermute | solution.py:993
  542.1 24.1 %collective-permute-start.22 = (bf16[192,16,128]{2,1,0:T(8,128)(2,1)S(1)}, bf16[192,16,128]{2,1,0:T(8,128)(2,1)}, u32[]{:S(2)}, u32[]{:S(2)}) collective-permute-start(bf16[192,16,128]{2,1,0:T(8,128)(2,1)S(1)} %get-tuple-element.94), channel_id=1, source_target_pairs={{24,16},{25,17},{26,18},{27,19},{28,20},{29,21},{30,22},{31,23},{1... | collective-permute-start | bytes 2359304 | tf_op jit(solution)/shard_map/ppermute | solution.py:993
  543.9 38.9 %collective-permute-start.17 = (bf16[192,16,128]{2,1,0:T(8,128)(2,1)S(1)}, bf16[192,16,128]{2,1,0:T(8,128)(2,1)}, u32[]{:S(2)}, u32[]{:S(2)}) collective-permute-start(bf16[192,16,128]{2,1,0:T(8,128)(2,1)S(1)} %add_convert_fusion), channel_id=1, source_target_pairs={{16,0},{17,1},{18,2},{19,3},{20,4},{21,5},{22,6},{23,7}} | collective-permute-start | bytes 2359304 | tf_op jit(solution)/shard_map/ppermute | solution.py:993
  545.3 3.9 collective-permute-start.25
  549.2 12.2 %collective-permute-start.26 = (f32[7,4096]{1,0:T(8,128)S(1)}, f32[7,4096]{1,0:T(8,128)S(1)}, u32[]{:S(2)}, u32[]{:S(2)}) collective-permute-start(f32[7,4096]{1,0:T(8,128)S(1)} %add.126), channel_id=1, source_target_pairs={{0,8},{1,9},{2,10},{3,11},{4,12},{5,13},{6,14},{7,15},{8,0},{9,1},... | collective-permute-start | bytes 344072 | tf_op jit(solution)/shard_map/ppermute | solution.py:879
  561.4 33.9 %collective-permute-start.27 = (f32[7,4096]{1,0:T(8,128)S(1)}, f32[7,4096]{1,0:T(8,128)S(1)}, u32[]{:S(2)}, u32[]{:S(2)}) collective-permute-start(f32[7,4096]{1,0:T(8,128)S(1)} %add.127), channel_id=1, source_target_pairs={{0,16},{1,17},{2,18},{3,19},{4,20},{5,21},{6,22},{7,23},{8,24},{9,... | collective-permute-start | bytes 344072 | tf_op jit(solution)/shard_map/ppermute | solution.py:879
  589.9 8.3 %collective-permute-start.28 = (f32[28672]{0:T(1024)S(1)}, f32[28672]{0:T(1024)S(1)}, u32[]{:S(2)}, u32[]{:S(2)}) collective-permute-start(f32[28672]{0:T(1024)S(1)} %slice_bitcast_fusion.2), channel_id=1, source_target_pairs={{1,0},{2,1},{3,2},{4,3},{5,4},{6,5},{7,6},{8,7},{9,8},{10,9},{11,1... | collective-permute-start | bytes 344072 | tf_op jit(solution)/shard_map/ppermute | solution.py:959
  (5 other events, 40.2 us)
Sparse Core Ops, SparseCore 0:
  20.3 159.1 all-gather.1

commit v3 on v2

--- a/solution.py
+++ b/solution.py
@@ -416,24 +416,53 @@
     return (lane >= 64) if head else (lane < 64)
 
 
-def attend_kernel(len_ref, q_ref, k_ref, v_ref, out_ref):
+def with_bias(keys, head, bias):
+    lane = lax.broadcasted_iota(jnp.int32, (1, LANES), 1)
+    rest = jnp.where(lane == 64 * (1 - head), bias, jnp.zeros((), BF))
+    return jnp.where(head_lanes(head), keys, rest)
+
+
+def with_one(queries, head):
+    lane = lax.broadcasted_iota(jnp.int32, (1, LANES), 1)
+    rest = jnp.where(lane == 64 * (1 - head), 1.0, 0.0).astype(BF)
+    return jnp.where(head_lanes(head), queries * jnp.asarray(0.125, BF), rest)
+
+
+def key_bias(len_ref, frames):
+    row = lax.broadcasted_iota(jnp.int32, (frames, 1), 0)
+    return jnp.where(row < len_ref[0], 0.0, -1e30).astype(BF)
+
+
+def paired_blocks(body, frames, rows):
+    def pair(index, carry):
+        body(index * 2 * rows)
+        body(index * 2 * rows + rows)
+        return carry
+
+    lax.fori_loop(0, frames // (2 * rows), pair, 0)
+
+
+def attend_kernel(len_ref, q_ref, k_ref, v_ref, out_ref, total_ref):
     rows = 256
     frames = k_ref.shape[0]
-    valid = lax.broadcasted_iota(jnp.int32, (1, frames), 1) < len_ref[0]
-    keys = k_ref[...]
+    bias = key_bias(len_ref, frames)
     zero = jnp.zeros((), BF)
-    values = [jnp.where(head_lanes(h), v_ref[...], zero) for h in range(2)]
-    for offset in range(0, frames, rows):
-        queries = q_ref[offset : offset + rows, :] * jnp.asarray(0.125, BF)
-        total = None
+    keys = [with_bias(k_ref[...], h, bias) for h in range(2)]
+
+    def one_block(offset):
+        here = pl.ds(pl.multiple_of(offset, rows), rows)
+        mixed = []
         for h in range(2):
-            scores = dot_nt(jnp.where(head_lanes(h), queries, zero), keys)
-            scores = jnp.where(valid, scores, -1e30)
-            weights = jnp.exp(scores - jnp.max(scores, -1, keepdims=True))
-            weights = weights * (1.0 / jnp.sum(weights, -1, keepdims=True))
-            mixed = dot_nn(weights.astype(BF), values[h])
-            total = mixed if total is None else total + mixed
-        out_ref[offset : offset + rows, :] = total.astype(BF)
+            scores = dot_nt(with_one(q_ref[here, :], h), keys[h])
+            largest = jnp.max(scores, -1, keepdims=True)
+            weights = jnp.exp(scores - largest)
+            total = jnp.sum(weights, -1, keepdims=True)
+            mixed.append(dot_nn(weights.astype(BF), v_ref[...]) * (1.0 / total))
+            wide = jnp.broadcast_to(largest + jnp.log(total), (rows, LANES))
+            total_ref[0, h : h + 1, here] = wide.T[0:1, :]
+        out_ref[here, :] = jnp.where(head_lanes(0), mixed[0], mixed[1]).astype(BF)
+
+    paired_blocks(one_block, frames, rows)
 
 
 def attend(key_len, qkv):
@@ -441,64 +470,71 @@
     return pl.pallas_call(
         attend_kernel,
         grid=(pairs,),
-        out_shape=jax.ShapeDtypeStruct((1024, D), BF),
+        out_shape=(
+            jax.ShapeDtypeStruct((1024, D), BF),
+            jax.ShapeDtypeStruct((pairs, 2, 1024), F32),
+        ),
         in_specs=[
             pl.BlockSpec(memory_space=pltpu.SMEM),
             pl.BlockSpec((1024, LANES), lambda j: (0, j)),
             pl.BlockSpec((1024, LANES), lambda j: (0, pairs + j)),
             pl.BlockSpec((1024, LANES), lambda j: (0, 2 * pairs + j)),
         ],
-        out_specs=pl.BlockSpec((1024, LANES), lambda j: (0, j)),
+        out_specs=(
+            pl.BlockSpec((1024, LANES), lambda j: (0, j)),
+            pl.BlockSpec((1, 2, 1024), lambda j: (j, 0, 0)),
+        ),
         compiler_params=params_of("arbitrary"),
         cost_estimate=cost(17e9, 8e6, 16e6),
         name="attend",
     )(key_len, qkv, qkv, qkv)
 
 
-def attend_back_kernel(len_ref, q_ref, k_ref, v_ref, do_ref, dq_ref, dk_ref, dv_ref, dk_acc, dv_acc):
+def attend_back_kernel(
+    len_ref, q_ref, k_ref, v_ref, do_ref, mix_ref, total_ref,
+    dq_ref, dk_ref, dv_ref, dk_acc, dv_acc,
+):
     rows = 256
     frames = k_ref.shape[0]
-    valid = lax.broadcasted_iota(jnp.int32, (frames, 1), 0) < len_ref[0]
-    keys = k_ref[...]
+    bias = key_bias(len_ref, frames)
     values = v_ref[...]
     zero = jnp.zeros((), BF)
-    masked_keys = [jnp.where(head_lanes(h), keys, zero) for h in range(2)]
-    for offset in range(0, frames, rows):
-        queries = q_ref[offset : offset + rows, :] * jnp.asarray(0.125, BF)
-        grads = do_ref[offset : offset + rows, :]
+    keys = [with_bias(k_ref[...], h, bias) for h in range(2)]
+    masked_keys = [jnp.where(head_lanes(h), k_ref[...], zero) for h in range(2)]
+    dk_acc[...] = jnp.zeros_like(dk_acc)
+    dv_acc[...] = jnp.zeros_like(dv_acc)
+
+    def one_block(offset):
+        here = pl.ds(pl.multiple_of(offset, rows), rows)
+        queries = q_ref[here, :]
+        grads = do_ref[here, :]
+        products = (grads.astype(F32) * mix_ref[here, :].astype(F32)).T
         total = None
         for h in range(2):
-            masked_q = jnp.where(head_lanes(h), queries, zero)
+            masked_q = jnp.where(head_lanes(h), queries * jnp.asarray(0.125, BF), zero)
             masked_g = jnp.where(head_lanes(h), grads, zero)
-            scores = dot_nt(keys, masked_q)
-            scores = jnp.where(valid, scores, -1e30)
-            weights = jnp.exp(scores - jnp.max(scores, 0, keepdims=True))
-            weights = weights * (1.0 / jnp.sum(weights, 0, keepdims=True))
+            inner = jnp.sum(products[64 * h : 64 * h + 64, :], 0, keepdims=True)
+            scores = dot_nt(keys[h], with_one(queries, h))
+            weights = jnp.exp(scores - total_ref[0, h : h + 1, here])
             grad_w = dot_nt(values, masked_g)
-            product = weights * grad_w
-            back = product - weights * jnp.sum(product, 0, keepdims=True)
-            back = back.astype(BF)
-            part_v = dot_nn(weights.astype(BF), masked_g)
-            part_k = dot_nn(back, masked_q)
-            if offset == 0 and h == 0:
-                dv_acc[...] = part_v
-                dk_acc[...] = part_k
-            else:
-                dv_acc[...] += part_v
-                dk_acc[...] += part_k
+            back = (weights * (grad_w - inner)).astype(BF)
+            dv_acc[...] += dot_nn(weights.astype(BF), masked_g)
+            dk_acc[...] += dot_nn(back, masked_q)
             part_q = dot_tn(back, masked_keys[h])
             total = part_q if total is None else total + part_q
-        dq_ref[offset : offset + rows, :] = (total * 0.125).astype(BF)
+        dq_ref[here, :] = (total * 0.125).astype(BF)
+
+    paired_blocks(one_block, frames, rows)
     dk_ref[...] = dk_acc[...].astype(BF)
     dv_ref[...] = dv_acc[...].astype(BF)
 
 
-def attend_back(key_len, qkv, grad_mix, first, count, earlier, waits=()):
+def attend_back(key_len, qkv, grad_mix, mixture, totals, first, count, earlier, waits=()):
     pairs = HEADS // 2
     block = lambda shift: pl.BlockSpec((1024, LANES), lambda j: (0, shift + first + j))
     kept = () if earlier is None else tuple(earlier)
     return pl.pallas_call(
-        without(attend_back_kernel, 5, len(kept) + len(waits)),
+        without(attend_back_kernel, 7, len(kept) + len(waits)),
         grid=(count,),
         out_shape=(jax.ShapeDtypeStruct((1024, D), BF),) * 3,
         in_specs=[
@@ -507,15 +543,17 @@
             block(pairs),
             block(2 * pairs),
             block(0),
+            block(0),
+            pl.BlockSpec((1, 2, 1024), lambda j: (first + j, 0, 0)),
         ]
         + [ANYWHERE] * (len(kept) + len(waits)),
         out_specs=(block(0),) * 3,
-        input_output_aliases={5 + i: i for i in range(len(kept))},
+        input_output_aliases={7 + i: i for i in range(len(kept))},
         scratch_shapes=[pltpu.VMEM((1024, LANES), F32)] * 2,
         compiler_params=params_of("arbitrary"),
         cost_estimate=cost(11e9 * count, 2e6 * count, 4e6 * count),
         name="attend_back",
-    )(key_len, qkv, qkv, qkv, grad_mix, *kept, *waits)
+    )(key_len, qkv, qkv, qkv, grad_mix, mixture, totals, *kept, *waits)
 
 
 def middle_kernel(x_ref, mod_ref, mix_ref, w_ref, mid_ref, low_ref):
@@ -621,21 +659,22 @@
 
     @pl.when(step == pl.num_programs(0) - 1)
     def _():
-        grad_gain = jnp.zeros((1, D), F32)
-        grad_shift = jnp.zeros((1, D), F32)
-        for offset in range(0, frames, rows):
-            here = slice(offset, offset + rows)
+        dmod_ref[...] = jnp.zeros_like(dmod_ref)
+
+        def finish(index, carry):
+            here = pl.ds(pl.multiple_of(index * rows, rows), rows)
             middle = mid_ref[here, :]
             out_ref[here, :] = (middle + y_acc[here, :]).astype(BF)
             zhat, inverse = centre(middle)
             grad = dh_acc[here, :]
-            grad_gain += jnp.sum(grad * zhat, 0, keepdims=True)
-            grad_shift += jnp.sum(grad, 0, keepdims=True)
+            dmod_ref[0:1, :] += jnp.sum(grad * zhat, 0, keepdims=True)
+            dmod_ref[1:2, :] += jnp.sum(grad, 0, keepdims=True)
             grad_mid = dy_ref[here, :].astype(F32) + norm_back(zhat, inverse, grad, mod_ref[2:3, :])
             dmid_ref[here, :] = grad_mid
             low_dmid_ref[here, :] = grad_mid.astype(BF)
-        dmod_ref[0:1, :] = grad_gain
-        dmod_ref[1:2, :] = grad_shift
+            return carry
+
+        lax.fori_loop(0, frames // rows, finish, 0)
 
 
 def ffn_both(middle, mod, low_two, dy, tiles):
@@ -915,7 +954,7 @@
     mod = jnp.sum(picker * table.astype(F32), 0).reshape(4, D)
 
     low_one, qkv = project_qkv(x, mod, tiles)
-    mixture = attend(key_len, qkv)
+    mixture, totals = attend(key_len, qkv)
     middle, low_two = middle_rows(x, mod, mixture, tiles)
     block_out, dmid, low_dmid, dmod_two, grads = ffn_both(middle, mod, low_two, dy, tiles)
     grad_mix, grads = out_back(mixture, low_dmid, tiles, grads)
@@ -923,28 +962,25 @@
     grads = grads.reshape(3, 2, 2, 2, 192, TILE, LANES)
     sent = take_other(sel, grads)
     moved = exchange(sent, 1, count)
-    back = attend_back(key_len, qkv, grad_mix, 0, 2, None, (sent,))
+    back = attend_back(key_len, qkv, grad_mix, mixture, totals, 0, 2, None, (sent,))
     one_send, one_keep, two_send, two_keep = core_sum(sel, grads, moved, back[:1])
     one_moved, two_moved = exchange(one_send, 2, count), exchange(two_send, 4, count)
-    back = attend_back(key_len, qkv, grad_mix, 2, 2, back, (one_send,))
-    back = attend_back(key_len, qkv, grad_mix, 4, 2, back)
-    dq, dk, dv = attend_back(key_len, qkv, grad_mix, 6, 2, back)
+    dq, dk, dv = attend_back(key_len, qkv, grad_mix, mixture, totals, 2, 6, back, (one_send,))
+    grad_qkv = qkv_weight_grad(low_one, dq, dk, dv)
+    grad_qkv = grad_qkv.reshape(1, 2, 2, 2, 192, TILE, LANES)
     one_send, one_keep, two_send, two_keep = plane_sum(
-        sel, one_keep, one_moved, two_keep, two_moved, waits=(dq,)
+        sel, one_keep, one_moved, two_keep, two_moved, waits=(grad_qkv,)
     )
     one_moved, two_moved = exchange(one_send, 4, count), exchange(two_send, 2, count)
-    grad_qkv = qkv_weight_grad(low_one, dq, dk, dv, (one_send,))
     held = (one_keep, one_moved, two_keep, two_moved)
-
-    grad_qkv = grad_qkv.reshape(1, 2, 2, 2, 192, TILE, LANES)
-    sent = take_other(sel, grad_qkv)
+    sent = take_other(sel, grad_qkv, (one_send,))
     moved = exchange(sent, 1, count)
     one_send, one_keep, two_send, two_keep = core_sum(sel, grad_qkv, moved)
     one_moved, two_moved = exchange(one_send, 2, count), exchange(two_send, 4, count)
-    rest = line_sum(sel, *held, waits=(one_send,))
-    input_grad, dmod_one = input_back(x, mod, dmid, dq, dk, dv, tiles, (rest,))
+    input_grad, dmod_one = input_back(x, mod, dmid, dq, dk, dv, tiles, (one_send,))
+    rest = line_sum(sel, *held, waits=(input_grad,))
     one_send, one_keep, two_send, two_keep = plane_sum(
-        sel, one_keep, one_moved, two_keep, two_moved, waits=(input_grad,)
+        sel, one_keep, one_moved, two_keep, two_moved, waits=(rest,)
     )
     one_moved, two_moved = exchange(one_send, 4, count), exchange(two_send, 2, count)
     first = line_sum(sel, one_keep, one_moved, two_keep, two_moved)

time: 621 us -> 582 us (0.937)
  Pallas kernels: 308 us -> 280 us
  waiting for transfers between devices: 212 us -> 201 us
    pallas_call x5 -> x3, Pallas kernels: 122 us -> 93.9 us  [the longest x2 55.1 us: attend_back(): pl.pallas_call(without(attend_back_kernel, 7, len(kept) + len(waits)), gr...]
    ppermute x20, waiting for transfers between devices: 47.4 us -> 35.4 us  [exchange(): lax.ppermute(value, ('dp', 'fsdp'), [(i, i ^ mask) for i in range(count)])]
  transfers between devices with their start and end apart: 30 -> 30, of which waited for: 17 -> 16; matrix products, arithmetic and copies ran while one was open for 3% -> 3% of each run, Pallas kernels for 19% -> 18%
where the time goes in v3:
time: 582 us; the launch traced here: 575 us
  Pallas kernels  280 us (48%)
  waiting for transfers between devices  201 us (35%)
  starting transfers between devices  50.6 us (9%)
  other arithmetic  21 us (4%)
  between operations  16.1 us (3%)
  local copies, waits for them, and re-layouts  6.41 us (1%)
    all_gather x1, waiting for transfers between devices, fast_device(): tiles = lax.all_gather(packed, ('dp', 'fsdp'), axis=0, tiled=True)  134 us
    pallas_call x1, Pallas kernels, ffn_both(): pl.pallas_call(ffn_kernel, grid=(steps,), out_shape=(jax.ShapeDtypeStruct...  73.5 us
    pallas_call x2, Pallas kernels, attend_back(): pl.pallas_call(without(attend_back_kernel, 7, len(kept) + len(waits)), gr...  55.1 us
    pallas_call x8, Pallas kernels, staged(): pl.pallas_call(without(kernel, 1 + len(ins), len(waits)), out_shape=(jax....  51 us
    pallas_call x1, Pallas kernels, attend(): pl.pallas_call(attend_kernel, grid=(pairs,), out_shape=(jax.ShapeDtypeStr...  38.8 us
    ppermute x20, waiting for transfers between devices, exchange(): lax.ppermute(value, ('dp', 'fsdp'), [(i, i ^ mask) for i in range(count)])  35.4 us
    ppermute x7, waiting for transfers between devices, layer_move(): return lax.ppermute(value, ('dp', 'fsdp'), pairs)  29.4 us
    ppermute x20, starting transfers between devices, exchange(): lax.ppermute(value, ('dp', 'fsdp'), [(i, i ^ mask) for i in range(count)])  24 us
  transfers between devices with their start and end apart: 30, of which 16 were waited for; matrix products, arithmetic and copies ran while one was open for 3% of the time, Pallas kernels for 18%

profile of v3, /device:TPU:1, one launch (start us, length us, event | category | flops | bytes accessed | tf_op | source)
XLA Modules:
  0.0 575.3 jit_solution(1518728245851006134)
XLA Ops:
  8.1 4.5 collective-permute-start.5
  33.2 4.7 collective-permute-done.3
  41.3 3.6 collective-permute-done.4
  45.6 134.0 %all-gather.2.cloned.1.call-done = bf16[6144,16,128]{2,1,0:T(8,128)(2,1)} async-done(((bf16[192,16,128]{2,1,0:T(8,128)(2,1)}), bf16[6144,16,128]{2,1,0:T(8,128)(2,1)}) %all-gather.2.cloned.1.call-update) | async-done | bytes 25165840 | tf_op jit(solution)/shard_map/all_gather | solution.py:952
  179.6 12.9 %project_qkv.1 = (bf16[1024,1024]{1,0:T(8,128)(2,1)}, bf16[1024,3072]{1,0:T(8,128)(2,1)}) custom-call(bf16[1024,1024]{1,0:T(8,128)(2,1)} %bitcast.54, f32[4,1024]{1,0:T(4,128)} %reshape.71.mod_ref.refs_1_, bf16[256,24,16,128]{3,2,1,0:T(8,128)(2,1)} %bitcast.42), custom_call_target="tpu_custom_call" | custom-call | flops 6400000000 | bytes 18000000 | tf_op jit(solution)/shard_map/project_qkv/pallas_call | solution.py:392
  192.4 38.8 %attend.1 = (bf16[1024,1024]{1,0:T(8,128)(2,1)}, f32[8,2,1024]{2,1,0:T(2,128)}) custom-call(s32[1]{0:T(128)S(6)} %copy.25.len_ref.refs_0_, bf16[1024,3072]{1,0:T(8,128)(2,1)} %get-tuple-element.44.q_ref.k_ref.v_ref.refs_1_.refs_2_.refs_3_, bf16[1024,3072]{1,0:T(8,128)(2,1)} %get-tuple-element.44.q_ref.k_ref.v_ref.refs_1_.refs_2_.refs_3_, ...), custom_call_target="tpu_custom_call" | custom-call | flops 16999999488 | bytes 8000000 | tf_op jit(solution)/shard_map/attend/pallas_call | solution.py:470
  231.3 7.4 %middle_rows.1 = (f32[1024,1024]{1,0:T(8,128)}, bf16[1024,1024]{1,0:T(8,128)(2,1)}) custom-call(bf16[1024,1024]{1,0:T(8,128)(2,1)} %bitcast.55, f32[4,1024]{1,0:T(4,128)} %reshape.71.mod_ref.refs_1_, bf16[1024,1024]{1,0:T(8,128)(2,1)} %get-tuple-element.45.mix_ref.refs_5_, bf16[768,8,16,128]{3,2,1,0:T(8,128)(2,1)} %bitcast.43), custom_call_target="tpu_custom_call" | custom-call | flops 2200000000 | bytes 12000000 | tf_op jit(solution)/shard_map/middle_rows/pallas_call | solution.py:569
  238.7 73.5 %ffn_both.1 = (bf16[1024,1024]{1,0:T(8,128)(2,1)}, f32[1024,1024]{1,0:T(8,128)}, bf16[1024,1024]{1,0:T(8,128)(2,1)}, f32[2,1024]{1,0:T(2,128)}, bf16[144,32,16,128]{3,2,1,0:T(8,128)(2,1)}) custom-call(f32[1024,1024]{1,0:T(8,128)} %get-tuple-element.46.mid_ref, f32[4,1024]{1,0:T(4,128)} %reshape.71.mod_ref.refs_1_, ...), custom_call_target="tpu_custom_call" | custom-call | flops 51999997952 | bytes 60000000 | tf_op jit(solution)/shard_map/ffn_both/pallas_call | solution.py:688
  312.2 8.5 %out_back.1 = (bf16[1024,1024]{1,0:T(8,128)(2,1)}, bf16[576,8,16,128]{3,2,1,0:T(8,128)(2,1)}) custom-call(bf16[1024,1024]{1,0:T(8,128)(2,1)} %get-tuple-element.45.mix_ref.refs_5_, bf16[1024,1024]{1,0:T(8,128)(2,1)} %get-tuple-element.50.dmid_ref, bf16[768,8,16,128]{3,2,1,0:T(8,128)(2,1)} %bitcast.46, ...), custom_call_target="tpu_custom_call", output_to_operand_aliasing={{1}: (3, {})} | custom-call | flops 4300000256 | bytes 10000000 | tf_op jit(solution)/shard_map/out_back/pallas_call | solution.py:740
  320.6 9.0 %take_other.2.refs_7_ = bf16[3,2,2,192,16,128]{5,4,3,2,1,0:T(8,128)(2,1)} custom-call(s32[3]{0:T(128)} %pad_add_fusion.refs_0_, bf16[3,2,2,2,192,16,128]{6,5,4,3,2,1,0:T(8,128)(2,1)} %bitcast.49), custom_call_target="tpu_custom_call" | custom-call | bytes 18000000 | tf_op jit(solution)/shard_map/take_other/pallas_call | solution.py:832
  329.9 15.0 %attend_back.2 = (bf16[1024,1024]{1,0:T(8,128)(2,1)}, bf16[1024,1024]{1,0:T(8,128)(2,1)}, bf16[1024,1024]{1,0:T(8,128)(2,1)}) custom-call(s32[1]{0:T(128)S(6)} %copy.25.len_ref.refs_0_, bf16[1024,3072]{1,0:T(8,128)(2,1)} %get-tuple-element.44.q_ref.k_ref.v_ref.refs_1_.refs_2_.refs_3_, ...), custom_call_target="tpu_custom_call" | custom-call | flops 22000001024 | bytes 4000000 | tf_op jit(solution)/shard_map/attend_back/pallas_call | solution.py:536
  344.9 11.9 %core_sum.2 = (bf16[3,2,96,16,128]{4,3,2,1,0:T(8,128)(2,1)}, bf16[3,2,96,16,128]{4,3,2,1,0:T(8,128)(2,1)}, bf16[3,2,96,16,128]{4,3,2,1,0:T(8,128)(2,1)}, bf16[3,2,96,16,128]{4,3,2,1,0:T(8,128)(2,1)}) custom-call(s32[3]{0:T(128)} %pad_add_fusion.refs_0_, bf16[3,2,2,2,192,16,128]{6,5,4,3,2,1,0:T(8,128)(2,1)} %bitcast.50, ...), custom_call_target="tpu_custom_call" | custom-call | bytes 27000000 | tf_op jit(solution)/shard_map/core_sum/pallas_call | solution.py:832
  358.3 40.1 %attend_back.3 = (bf16[1024,1024]{1,0:T(8,128)(2,1)}, bf16[1024,1024]{1,0:T(8,128)(2,1)}, bf16[1024,1024]{1,0:T(8,128)(2,1)}) custom-call(s32[1]{0:T(128)S(6)} %copy.25.len_ref.refs_0_, bf16[1024,3072]{1,0:T(8,128)(2,1)} %get-tuple-element.44.q_ref.k_ref.v_ref.refs_1_.refs_2_.refs_3_, ...), custom_call_target="tpu_custom_call", output_to_operand_aliasing={{0}: (7, {}), {1}: (8, {}), {2}: (9, {})} | custom-call | flops 65999998976 | bytes 12000000 | tf_op jit(solution)/shard_map/attend_back/pallas_call | solution.py:536
  398.4 11.6 %qkv_weight_grad.1 = bf16[64,24,16,128]{3,2,1,0:T(8,128)(2,1)} custom-call(bf16[1024,1024]{1,0:T(8,128)(2,1)} %get-tuple-element.62.refs_0_, bf16[1024,1024]{1,0:T(8,128)(2,1)} %get-tuple-element.59.refs_1_.refs_3_, bf16[1024,1024]{1,0:T(8,128)(2,1)} %get-tuple-element.60.refs_2_.refs_4_, bf16[1024,1024]{1,0:T(8,128)(2,1)} %get-tuple-element.61.refs_3_.refs_5_), custom_call_target="tpu_custom_call" | custom-call | flops 6400000000 | bytes 15000000 | tf_op jit(solution)/shard_map/qkv_weight_grad/pallas_call | solution.py:772
  410.5 7.4 %plane_sum.2 = (bf16[3,96,16,128]{3,2,1,0:T(8,128)(2,1)}, bf16[3,96,16,128]{3,2,1,0:T(8,128)(2,1)}, bf16[3,96,16,128]{3,2,1,0:T(8,128)(2,1)}, bf16[3,96,16,128]{3,2,1,0:T(8,128)(2,1)}) custom-call(s32[3]{0:T(128)} %pad_add_fusion.refs_0_, bf16[3,2,96,16,128]{4,3,2,1,0:T(8,128)(2,1)} %get-tuple-element.63.refs_1_, ...), custom_call_target="tpu_custom_call" | custom-call | bytes 15000000 | tf_op jit(solution)/shard_map/plane_sum/pallas_call | solution.py:832
  417.9 4.5 take_other.3
  425.3 4.1 collective-permute-done.9.refs_2_
  429.4 5.8 %core_sum.3 = (bf16[1,2,96,16,128]{4,3,2,1,0:T(8,128)(2,1)}, bf16[1,2,96,16,128]{4,3,2,1,0:T(8,128)(2,1)}, bf16[1,2,96,16,128]{4,3,2,1,0:T(8,128)(2,1)}, bf16[1,2,96,16,128]{4,3,2,1,0:T(8,128)(2,1)}) custom-call(s32[3]{0:T(128)} %pad_add_fusion.refs_0_, bf16[1,2,2,2,192,16,128]{6,5,4,3,2,1,0:T(8,128)(2,1)} %bitcast.53, ...), custom_call_target="tpu_custom_call" | custom-call | bytes 9000000 | tf_op jit(solution)/shard_map/core_sum/pallas_call | solution.py:832
  436.7 15.2 %input_back.1 = (bf16[1024,1024]{1,0:T(8,128)(2,1)}, f32[2,1024]{1,0:T(2,128)}) custom-call(bf16[1024,1024]{1,0:T(8,128)(2,1)} %bitcast.56, f32[4,1024]{1,0:T(4,128)} %reshape.71.mod_ref.refs_1_, f32[1024,1024]{1,0:T(8,128)} %get-tuple-element.49.refs_2_, bf16[1024,1024]{1,0:T(8,128)(2,1)} %get-tuple-element.59.refs_1_.refs_3_, ...), custom_call_target="tpu_custom_call" | custom-call | flops 6400000000 | bytes 22000000 | tf_op jit(solution)/shard_map/input_back/pallas_call | solution.py:804
  453.0 5.3 line_sum.2.refs_5_
  463.3 5.2 collective-permute-done.10.refs_2_
  468.5 4.1 plane_sum.3
  480.9 5.0 collective-permute-start.19
  490.5 10.1 %collective-permute-done.19 = bf16[192,16,128]{2,1,0:T(8,128)(2,1)} collective-permute-done((bf16[192,16,128]{2,1,0:T(8,128)(2,1)}, bf16[192,16,128]{2,1,0:T(8,128)(2,1)}, u32[]{:S(2)}, u32[]{:S(2)}) %collective-permute-start.19) | collective-permute-done | bytes 786464 | tf_op jit(solution)/shard_map/ppermute | solution.py:1029
  503.4 4.1 collective-permute-start.20
  510.8 3.8 collective-permute-done.25
  515.3 9.6 %collective-permute-done.26 = f32[7,4096]{1,0:T(8,128)S(1)} collective-permute-done((f32[7,4096]{1,0:T(8,128)S(1)}, f32[7,4096]{1,0:T(8,128)S(1)}, u32[]{:S(2)}, u32[]{:S(2)}) %collective-permute-start.26) | collective-permute-done | bytes 114720 | tf_op jit(solution)/shard_map/ppermute | solution.py:918
  524.9 4.4 collective-permute-start.27
  529.3 16.5 %collective-permute-done.17 = bf16[192,16,128]{2,1,0:T(8,128)(2,1)} collective-permute-done((bf16[192,16,128]{2,1,0:T(8,128)(2,1)S(1)}, bf16[192,16,128]{2,1,0:T(8,128)(2,1)}, u32[]{:S(2)}, u32[]{:S(2)}) %collective-permute-start.17) | collective-permute-done | bytes 786464 | tf_op jit(solution)/shard_map/ppermute | solution.py:1029
  545.8 3.2 fusion.8.tiles_ref
  553.0 6.7 %collective-permute-start.28 = (f32[28672]{0:T(1024)S(1)}, f32[28672]{0:T(1024)S(1)}, u32[]{:S(2)}, u32[]{:S(2)}) collective-permute-start(f32[28672]{0:T(1024)S(1)} %slice_bitcast_fusion.2), channel_id=1, source_target_pairs={{1,0},{2,1},{3,2},{4,3},{5,4},{6,5},{7,6},{8,7},{9,8},{10,9},{11,1... | collective-permute-start | bytes 344072 | tf_op jit(solution)/shard_map/ppermute | solution.py:995
  561.2 6.8 %divide_subtract_fusion = (f32[394112]{0:T(1024)}, f32[394112]{0:T(1024)}, f32[394112]{0:T(1024)}, f32[394112]{0:T(1024)}) fusion(f32[394112]{0:T(1024)S(1)} %copy-done, f32[394112]{0:T(1024)} %param.11, f32[394112]{0:T(1024)} %param.12, s32[]{:T(128)S(6)} %select_n.83, f32[28672]{0:T(1024)S(1)} %broadcast_select_fusion, f32[393216]{0:T(1024)} %bitcast.57), kind=kLoop, calls=%fused_computation.7 | loop fusion | flops 5123456 | bytes 12722692 | tf_op jit(solution)/shard_map/sub | solution.py:1002
  (94 shorter events, 62.0 us)
Async XLA Ops:
  7.2 172.4 %all-gather.2.cloned.1.call-start = ((), (), s32[]{:S(2)}) async-start(), calls=%async_computation | async-start | bytes 25952256 | tf_op jit(solution)/shard_map/all_gather | solution.py:952
  8.1 6.3 %collective-permute-start.5 = (f32[28672]{0:T(1024)S(1)}, f32[28672]{0:T(1024)S(1)}, u32[]{:S(2)}, u32[]{:S(2)}) collective-permute-start(f32[28672]{0:T(1024)S(1)} %slice.16), channel_id=1, source_target_pairs={{0,1},{1,2},{2,3},{3,4},{4,5},{5,6},{6,7},{7,8},{8,9},{9,10},{10,1... | collective-permute-start | bytes 344072 | tf_op jit(solution)/shard_map/ppermute | solution.py:940
  21.2 1.3 collective-permute-start
  22.6 4.4 collective-permute-start.1
  27.0 3.6 collective-permute-start.2
  30.6 7.3 %collective-permute-start.3 = (bf16[7,4096]{1,0:T(8,128)(2,1)S(1)}, bf16[7,4096]{1,0:T(8,128)(2,1)S(1)}, u32[]{:S(2)}, u32[]{:S(2)}) collective-permute-start(bf16[7,4096]{1,0:T(8,128)(2,1)S(1)} %add.107), channel_id=1, source_target_pairs={{0,8},{1,9},{2,10},{3,11},{4,12},{5,13},{6,14},{7,15},{8,0},{9,1},... | collective-permute-start | bytes 172040 | tf_op jit(solution)/shard_map/ppermute | solution.py:918
  38.0 6.9 %collective-permute-start.4 = (bf16[7,4096]{1,0:T(8,128)(2,1)S(1)}, bf16[7,4096]{1,0:T(8,128)(2,1)S(1)}, u32[]{:S(2)}, u32[]{:S(2)}) collective-permute-start(bf16[7,4096]{1,0:T(8,128)(2,1)S(1)} %add.108), channel_id=1, source_target_pairs={{0,16},{1,17},{2,18},{3,19},{4,20},{5,21},{6,22},{7,23},{8,24},{9,... | collective-permute-start | bytes 172040 | tf_op jit(solution)/shard_map/ppermute | solution.py:918
  329.7 15.2 %collective-permute-start.6 = (bf16[3,2,2,192,16,128]{5,4,3,2,1,0:T(8,128)(2,1)}, bf16[3,2,2,192,16,128]{5,4,3,2,1,0:T(8,128)(2,1)}, u32[]{:S(2)}, u32[]{:S(2)}) collective-permute-start(bf16[3,2,2,192,16,128]{5,4,3,2,1,0:T(8,128)(2,1)} %take_other.2.refs_7_), channel_id=1, source_target_pairs={{0,1},{1,0},{2,3},{3,2},{4,5},{5,4},{6,7},{7,6},{8,9},{9,8},{10,11... | collective-permute-start | bytes 28311560 | tf_op jit(solution)/shard_map/ppermute | solution.py:918
  356.8 53.2 %collective-permute-start.7 = (bf16[3,2,96,16,128]{4,3,2,1,0:T(8,128)(2,1)}, bf16[3,2,96,16,128]{4,3,2,1,0:T(8,128)(2,1)}, u32[]{:S(2)}, u32[]{:S(2)}) collective-permute-start(bf16[3,2,96,16,128]{4,3,2,1,0:T(8,128)(2,1)} %get-tuple-element.58.refs_10_), channel_id=1, source_target_pairs={{0,2},{1,3},{2,0},{3,1},{4,6},{5,7},{6,4},{7,5},{8,10},{9,11},{10,... | collective-permute-start | bytes 7077896 | tf_op jit(solution)/shard_map/ppermute | solution.py:918
  357.9 52.6 %collective-permute-start.8 = (bf16[3,2,96,16,128]{4,3,2,1,0:T(8,128)(2,1)}, bf16[3,2,96,16,128]{4,3,2,1,0:T(8,128)(2,1)}, u32[]{:S(2)}, u32[]{:S(2)}) collective-permute-start(bf16[3,2,96,16,128]{4,3,2,1,0:T(8,128)(2,1)} %get-tuple-element.65), channel_id=1, source_target_pairs={{0,4},{1,5},{2,6},{3,7},{4,0},{5,1},{6,2},{7,3},{8,12},{9,13},{10,... | collective-permute-start | bytes 7077896 | tf_op jit(solution)/shard_map/ppermute | solution.py:918
  422.4 7.0 %collective-permute-start.9 = (bf16[1,2,2,192,16,128]{5,4,3,2,1,0:T(8,128)(2,1)}, bf16[1,2,2,192,16,128]{5,4,3,2,1,0:T(8,128)(2,1)}, u32[]{:S(2)}, u32[]{:S(2)}) collective-permute-start(bf16[1,2,2,192,16,128]{5,4,3,2,1,0:T(8,128)(2,1)} %take_other.3), channel_id=1, source_target_pairs={{0,1},{1,0},{2,3},{3,2},{4,5},{5,4},{6,7},{7,6},{8,9},{9,8},{10,11... | collective-permute-start | bytes 9437192 | tf_op jit(solution)/shard_map/ppermute | solution.py:918
  423.8 28.2 %collective-permute-start.12 = (bf16[3,96,16,128]{3,2,1,0:T(8,128)(2,1)}, bf16[3,96,16,128]{3,2,1,0:T(8,128)(2,1)S(1)}, u32[]{:S(2)}, u32[]{:S(2)}) collective-permute-start(bf16[3,96,16,128]{3,2,1,0:T(8,128)(2,1)} %get-tuple-element.66.refs_2_), channel_id=1, source_target_pairs={{0,4},{1,5},{2,6},{3,7},{4,0},{5,1},{6,2},{7,3},{8,12},{9,13},{10,... | collective-permute-start | bytes 3538952 | tf_op jit(solution)/shard_map/ppermute | solution.py:918
  424.1 27.9 %collective-permute-start.13 = (bf16[3,96,16,128]{3,2,1,0:T(8,128)(2,1)}, bf16[3,96,16,128]{3,2,1,0:T(8,128)(2,1)}, u32[]{:S(2)}, u32[]{:S(2)}) collective-permute-start(bf16[3,96,16,128]{3,2,1,0:T(8,128)(2,1)} %get-tuple-element.74), channel_id=1, source_target_pairs={{0,2},{1,3},{2,0},{3,1},{4,6},{5,7},{6,4},{7,5},{8,10},{9,11},{10,... | collective-permute-start | bytes 3538952 | tf_op jit(solution)/shard_map/ppermute | solution.py:918
  435.2 33.3 %collective-permute-start.10 = (bf16[1,2,96,16,128]{4,3,2,1,0:T(8,128)(2,1)}, bf16[1,2,96,16,128]{4,3,2,1,0:T(8,128)(2,1)}, u32[]{:S(2)}, u32[]{:S(2)}) collective-permute-start(bf16[1,2,96,16,128]{4,3,2,1,0:T(8,128)(2,1)} %get-tuple-element.67.refs_7_), channel_id=1, source_target_pairs={{0,2},{1,3},{2,0},{3,1},{4,6},{5,7},{6,4},{7,5},{8,10},{9,11},{10,... | collective-permute-start | bytes 2359304 | tf_op jit(solution)/shard_map/ppermute | solution.py:918
  435.5 33.0 %collective-permute-start.11 = (bf16[1,2,96,16,128]{4,3,2,1,0:T(8,128)(2,1)}, bf16[1,2,96,16,128]{4,3,2,1,0:T(8,128)(2,1)}, u32[]{:S(2)}, u32[]{:S(2)}) collective-permute-start(bf16[1,2,96,16,128]{4,3,2,1,0:T(8,128)(2,1)} %get-tuple-element.71), channel_id=1, source_target_pairs={{0,4},{1,5},{2,6},{3,7},{4,0},{5,1},{6,2},{7,3},{8,12},{9,13},{10,... | collective-permute-start | bytes 2359304 | tf_op jit(solution)/shard_map/ppermute | solution.py:918
  461.1 17.7 %collective-permute-start.18 = (bf16[192,16,128]{2,1,0:T(8,128)(2,1)}, bf16[192,16,128]{2,1,0:T(8,128)(2,1)S(1)}, u32[]{:S(2)}, u32[]{:S(2)}) collective-permute-start(bf16[192,16,128]{2,1,0:T(8,128)(2,1)} %get-tuple-element.87), channel_id=1, source_target_pairs={{0,8},{1,9},{2,10},{3,11},{4,12},{5,13},{6,14},{7,15}} | collective-permute-start | bytes 2359304 | tf_op jit(solution)/shard_map/ppermute | solution.py:1029
  462.5 28.0 %collective-permute-start.21 = (bf16[192,16,128]{2,1,0:T(8,128)(2,1)}, bf16[192,16,128]{2,1,0:T(8,128)(2,1)S(1)}, u32[]{:S(2)}, u32[]{:S(2)}) collective-permute-start(bf16[192,16,128]{2,1,0:T(8,128)(2,1)} %get-tuple-element.88), channel_id=1, source_target_pairs={{24,16},{25,17},{26,18},{27,19},{28,20},{29,21},{30,22},{31,23}} | collective-permute-start | bytes 2359304 | tf_op jit(solution)/shard_map/ppermute | solution.py:1029
  472.6 13.3 %collective-permute-start.14 = (bf16[1,96,16,128]{3,2,1,0:T(8,128)(2,1)}, bf16[1,96,16,128]{3,2,1,0:T(8,128)(2,1)}, u32[]{:S(2)}, u32[]{:S(2)}) collective-permute-start(bf16[1,96,16,128]{3,2,1,0:T(8,128)(2,1)} %get-tuple-element.76), channel_id=1, source_target_pairs={{0,4},{1,5},{2,6},{3,7},{4,0},{5,1},{6,2},{7,3},{8,12},{9,13},{10,... | collective-permute-start | bytes 1179656 | tf_op jit(solution)/shard_map/ppermute | solution.py:918
  473.7 12.2 %collective-permute-start.15 = (bf16[1,96,16,128]{3,2,1,0:T(8,128)(2,1)}, bf16[1,96,16,128]{3,2,1,0:T(8,128)(2,1)}, u32[]{:S(2)}, u32[]{:S(2)}) collective-permute-start(bf16[1,96,16,128]{3,2,1,0:T(8,128)(2,1)} %get-tuple-element.78), channel_id=1, source_target_pairs={{0,2},{1,3},{2,0},{3,1},{4,6},{5,7},{6,4},{7,5},{8,10},{9,11},{10,... | collective-permute-start | bytes 1179656 | tf_op jit(solution)/shard_map/ppermute | solution.py:918
  474.1 16.2 %collective-permute-start.23 = (f32[7,4096]{1,0:T(8,128)S(1)}, f32[7,4096]{1,0:T(8,128)S(1)}, u32[]{:S(2)}, u32[]{:S(2)}) collective-permute-start(f32[7,4096]{1,0:T(8,128)S(1)} %broadcast_multiply_fusion), channel_id=1, source_target_pairs={{0,1},{1,0},{2,3},{3,2},{4,5},{5,4},{6,7},{7,6},{8,9},{9,8},{10,11... | collective-permute-start | bytes 344072 | tf_op jit(solution)/shard_map/ppermute | solution.py:918
  480.9 19.6 %collective-permute-start.19 = (bf16[192,16,128]{2,1,0:T(8,128)(2,1)}, bf16[192,16,128]{2,1,0:T(8,128)(2,1)}, u32[]{:S(2)}, u32[]{:S(2)}) collective-permute-start(bf16[192,16,128]{2,1,0:T(8,128)(2,1)} %fusion.5), channel_id=1, source_target_pairs={{0,8},{1,9},{2,10},{3,11},{4,12},{5,13},{6,14},{7,15},{8,16},{9,17... | collective-permute-start | bytes 2359304 | tf_op jit(solution)/shard_map/ppermute | solution.py:1029
  489.0 20.1 %collective-permute-start.16 = (bf16[192,16,128]{2,1,0:T(8,128)(2,1)}, bf16[192,16,128]{2,1,0:T(8,128)(2,1)S(1)}, u32[]{:S(2)}, u32[]{:S(2)}) collective-permute-start(bf16[192,16,128]{2,1,0:T(8,128)(2,1)} %bitcast.58), channel_id=1, source_target_pairs={{24,16},{25,17},{26,18},{27,19},{28,20},{29,21},{30,22},{31,23},{8... | collective-permute-start | bytes 2359304 | tf_op jit(solution)/shard_map/ppermute | solution.py:1029
  490.4 18.8 %copy-start.1 = (bf16[1,192,16,128]{3,2,1,0:T(8,128)(2,1)S(1)}, bf16[1,192,16,128]{3,2,1,0:T(8,128)(2,1)}, u32[]{:S(2)}) copy-start(bf16[1,192,16,128]{3,2,1,0:T(8,128)(2,1)} %line_sum.3) | copy-start | bytes 2359300
  490.4 20.3 %collective-permute-start.24 = (f32[7,4096]{1,0:T(8,128)S(1)}, f32[7,4096]{1,0:T(8,128)S(1)}, u32[]{:S(2)}, u32[]{:S(2)}) collective-permute-start(f32[7,4096]{1,0:T(8,128)S(1)} %fusion.9), channel_id=1, source_target_pairs={{0,2},{1,3},{2,0},{3,1},{4,6},{5,7},{6,4},{7,5},{8,10},{9,11},{10,... | collective-permute-start | bytes 344072 | tf_op jit(solution)/shard_map/ppermute | solution.py:918
  503.4 25.9 %collective-permute-start.20 = (bf16[192,16,128]{2,1,0:T(8,128)(2,1)}, bf16[192,16,128]{2,1,0:T(8,128)(2,1)S(1)}, u32[]{:S(2)}, u32[]{:S(2)}) collective-permute-start(bf16[192,16,128]{2,1,0:T(8,128)(2,1)} %get-tuple-element.85), channel_id=1, source_target_pairs={{0,8},{1,9},{2,10},{3,11},{4,12},{5,13},{6,14},{7,15},{8,16},{9,17... | collective-permute-start | bytes 2359304 | tf_op jit(solution)/shard_map/ppermute | solution.py:1029
  507.6 21.7 %collective-permute-start.22 = (bf16[192,16,128]{2,1,0:T(8,128)(2,1)S(1)}, bf16[192,16,128]{2,1,0:T(8,128)(2,1)}, u32[]{:S(2)}, u32[]{:S(2)}) collective-permute-start(bf16[192,16,128]{2,1,0:T(8,128)(2,1)S(1)} %get-tuple-element.86), channel_id=1, source_target_pairs={{24,16},{25,17},{26,18},{27,19},{28,20},{29,21},{30,22},{31,23},{1... | collective-permute-start | bytes 2359304 | tf_op jit(solution)/shard_map/ppermute | solution.py:1029
  509.3 36.4 %collective-permute-start.17 = (bf16[192,16,128]{2,1,0:T(8,128)(2,1)S(1)}, bf16[192,16,128]{2,1,0:T(8,128)(2,1)}, u32[]{:S(2)}, u32[]{:S(2)}) collective-permute-start(bf16[192,16,128]{2,1,0:T(8,128)(2,1)S(1)} %add_convert_fusion), channel_id=1, source_target_pairs={{16,0},{17,1},{18,2},{19,3},{20,4},{21,5},{22,6},{23,7}} | collective-permute-start | bytes 2359304 | tf_op jit(solution)/shard_map/ppermute | solution.py:1029
  510.7 3.9 collective-permute-start.25
  514.6 10.2 %collective-permute-start.26 = (f32[7,4096]{1,0:T(8,128)S(1)}, f32[7,4096]{1,0:T(8,128)S(1)}, u32[]{:S(2)}, u32[]{:S(2)}) collective-permute-start(f32[7,4096]{1,0:T(8,128)S(1)} %add.126), channel_id=1, source_target_pairs={{0,8},{1,9},{2,10},{3,11},{4,12},{5,13},{6,14},{7,15},{8,0},{9,1},... | collective-permute-start | bytes 344072 | tf_op jit(solution)/shard_map/ppermute | solution.py:918
  524.9 34.8 %collective-permute-start.27 = (f32[7,4096]{1,0:T(8,128)S(1)}, f32[7,4096]{1,0:T(8,128)S(1)}, u32[]{:S(2)}, u32[]{:S(2)}) collective-permute-start(f32[7,4096]{1,0:T(8,128)S(1)} %add.127), channel_id=1, source_target_pairs={{0,16},{1,17},{2,18},{3,19},{4,20},{5,21},{6,22},{7,23},{8,24},{9,... | collective-permute-start | bytes 344072 | tf_op jit(solution)/shard_map/ppermute | solution.py:918
  549.0 12.2 %copy-start = (f32[394112]{0:T(1024)S(1)}, f32[394112]{0:T(1024)}, u32[]{:S(2)}) copy-start(f32[394112]{0:T(1024)} %param.10) | copy-start | bytes 4729348
  553.0 8.2 %collective-permute-start.28 = (f32[28672]{0:T(1024)S(1)}, f32[28672]{0:T(1024)S(1)}, u32[]{:S(2)}, u32[]{:S(2)}) collective-permute-start(f32[28672]{0:T(1024)S(1)} %slice_bitcast_fusion.2), channel_id=1, source_target_pairs={{1,0},{2,1},{3,2},{4,3},{5,4},{6,5},{7,6},{8,7},{9,8},{10,9},{11,1... | collective-permute-start | bytes 344072 | tf_op jit(solution)/shard_map/ppermute | solution.py:995
  (6 other events, 36.5 us)
Sparse Core Ops, SparseCore 0:
  20.3 159.1 all-gather.1

commit v4 on v3

--- a/solution.py
+++ b/solution.py
@@ -305,12 +305,16 @@
     def _():
         span(0, 0, 3072)
 
-    for part in range(3):
+    def one_part(part, carry):
         for kind in (1, 2):
 
             @pl.when(kinds[part] == kind)
             def _():
                 span(kind, part * 1024, 1024)
+
+        return carry
+
+    lax.fori_loop(0, 3, one_part, 0)
 
 
 def pack_kernel(kinds, flat_ref, tiles_ref):
@@ -448,9 +452,8 @@
     bias = key_bias(len_ref, frames)
     zero = jnp.zeros((), BF)
     keys = [with_bias(k_ref[...], h, bias) for h in range(2)]
-
-    def one_block(offset):
-        here = pl.ds(pl.multiple_of(offset, rows), rows)
+    for offset in range(0, frames, rows):
+        here = slice(offset, offset + rows)
         mixed = []
         for h in range(2):
             scores = dot_nt(with_one(q_ref[here, :], h), keys[h])
@@ -461,8 +464,6 @@
             wide = jnp.broadcast_to(largest + jnp.log(total), (rows, LANES))
             total_ref[0, h : h + 1, here] = wide.T[0:1, :]
         out_ref[here, :] = jnp.where(head_lanes(0), mixed[0], mixed[1]).astype(BF)
-
-    paired_blocks(one_block, frames, rows)
 
 
 def attend(key_len, qkv):
@@ -845,15 +846,17 @@
 
 
 def take_kernel(sel, value_ref, out_ref):
-    out_ref[...] = value_ref[:, :, :, 0]
+    out_ref[...] = value_ref[:, :, 0]
 
 
 def take_other(sel, value, waits=()):
     layers = value.shape[0]
-    spec = tile_spec(1, 2, 2, 1, 192, index=lambda i, at: (i, 0, 0, 1 - at[2], 0))
-    return staged(
-        take_kernel, "take_other", 1, (1, 2, 2, 192), [value], [spec], sel, layers, 6e6 * layers, waits
+    value = value.reshape(2 * layers, 2, 2, 192, TILE, LANES)
+    spec = tile_spec(1, 2, 1, 192, index=lambda i, at: (i, 0, 1 - at[2], 0))
+    sent = staged(
+        take_kernel, "take_other", 1, (1, 2, 192), [value], [spec], sel, 2 * layers, 6e6, waits
     )[0]
+    return sent.reshape(layers, 2, 2, 192, TILE, LANES)
 
 
 def both(left, right):

time: 582 us -> 580 us (level)
  no operation moved by 1% of the time
where the time goes in v4:
time: 580 us; the launch traced here: 572 us
  Pallas kernels  276 us (48%)
  waiting for transfers between devices  202 us (35%)
  starting transfers between devices  50.6 us (9%)
  other arithmetic  21 us (4%)
  between operations  16.1 us (3%)
  local copies, waits for them, and re-layouts  6.41 us (1%)
    all_gather x1, waiting for transfers between devices, fast_device(): tiles = lax.all_gather(packed, ('dp', 'fsdp'), axis=0, tiled=True)  134 us
    pallas_call x1, Pallas kernels, ffn_both(): pl.pallas_call(ffn_kernel, grid=(steps,), out_shape=(jax.ShapeDtypeStruct...  73.5 us
    pallas_call x2, Pallas kernels, attend_back(): pl.pallas_call(without(attend_back_kernel, 7, len(kept) + len(waits)), gr...  55.1 us
    pallas_call x8, Pallas kernels, staged(): pl.pallas_call(without(kernel, 1 + len(ins), len(waits)), out_shape=(jax....  50.7 us
    pallas_call x1, Pallas kernels, attend(): pl.pallas_call(attend_kernel, grid=(pairs,), out_shape=(jax.ShapeDtypeStr...  35.7 us
    ppermute x20, waiting for transfers between devices, exchange(): lax.ppermute(value, ('dp', 'fsdp'), [(i, i ^ mask) for i in range(count)])  35.5 us
    ppermute x7, waiting for transfers between devices, layer_move(): return lax.ppermute(value, ('dp', 'fsdp'), pairs)  29.4 us
    ppermute x20, starting transfers between devices, exchange(): lax.ppermute(value, ('dp', 'fsdp'), [(i, i ^ mask) for i in range(count)])  24 us
  transfers between devices with their start and end apart: 30, of which 16 were waited for; matrix products, arithmetic and copies ran while one was open for 3% of the time, Pallas kernels for 18%

profile of v4, /device:TPU:1, one launch (start us, length us, event | category | flops | bytes accessed | tf_op | source)
XLA Modules:
  0.0 572.2 jit_solution(9107745647020176107)
XLA Ops:
  8.1 4.5 collective-permute-start.5
  33.3 4.8 collective-permute-done.3
  41.3 3.6 collective-permute-done.4
  45.6 134.0 %all-gather.2.cloned.1.call-done = bf16[6144,16,128]{2,1,0:T(8,128)(2,1)} async-done(((bf16[192,16,128]{2,1,0:T(8,128)(2,1)}), bf16[6144,16,128]{2,1,0:T(8,128)(2,1)}) %all-gather.2.cloned.1.call-update) | async-done | bytes 25165840 | tf_op jit(solution)/shard_map/all_gather | solution.py:955
  179.6 12.9 %project_qkv.1 = (bf16[1024,1024]{1,0:T(8,128)(2,1)}, bf16[1024,3072]{1,0:T(8,128)(2,1)}) custom-call(bf16[1024,1024]{1,0:T(8,128)(2,1)} %bitcast.58, f32[4,1024]{1,0:T(4,128)} %reshape.77.mod_ref.refs_1_, bf16[256,24,16,128]{3,2,1,0:T(8,128)(2,1)} %bitcast.46), custom_call_target="tpu_custom_call" | custom-call | flops 6400000000 | bytes 18000000 | tf_op jit(solution)/shard_map/project_qkv/pallas_call | solution.py:396
  192.5 35.7 %attend.1 = (bf16[1024,1024]{1,0:T(8,128)(2,1)}, f32[8,2,1024]{2,1,0:T(2,128)}) custom-call(s32[1]{0:T(128)S(6)} %copy.25.len_ref.refs_0_, bf16[1024,3072]{1,0:T(8,128)(2,1)} %get-tuple-element.44.q_ref.k_ref.v_ref.refs_1_.refs_2_.refs_3_, bf16[1024,3072]{1,0:T(8,128)(2,1)} %get-tuple-element.44.q_ref.k_ref.v_ref.refs_1_.refs_2_.refs_3_, ...), custom_call_target="tpu_custom_call" | custom-call | flops 16999999488 | bytes 8000000 | tf_op jit(solution)/shard_map/attend/pallas_call | solution.py:471
  228.2 7.4 %middle_rows.1 = (f32[1024,1024]{1,0:T(8,128)}, bf16[1024,1024]{1,0:T(8,128)(2,1)}) custom-call(bf16[1024,1024]{1,0:T(8,128)(2,1)} %bitcast.59, f32[4,1024]{1,0:T(4,128)} %reshape.77.mod_ref.refs_1_, bf16[1024,1024]{1,0:T(8,128)(2,1)} %get-tuple-element.45.mix_ref.refs_5_, bf16[768,8,16,128]{3,2,1,0:T(8,128)(2,1)} %bitcast.47), custom_call_target="tpu_custom_call" | custom-call | flops 2200000000 | bytes 12000000 | tf_op jit(solution)/shard_map/middle_rows/pallas_call | solution.py:570
  235.6 73.5 %ffn_both.1 = (bf16[1024,1024]{1,0:T(8,128)(2,1)}, f32[1024,1024]{1,0:T(8,128)}, bf16[1024,1024]{1,0:T(8,128)(2,1)}, f32[2,1024]{1,0:T(2,128)}, bf16[144,32,16,128]{3,2,1,0:T(8,128)(2,1)}) custom-call(f32[1024,1024]{1,0:T(8,128)} %get-tuple-element.46.mid_ref, f32[4,1024]{1,0:T(4,128)} %reshape.77.mod_ref.refs_1_, ...), custom_call_target="tpu_custom_call" | custom-call | flops 51999997952 | bytes 60000000 | tf_op jit(solution)/shard_map/ffn_both/pallas_call | solution.py:689
  309.2 8.5 %out_back.1 = (bf16[1024,1024]{1,0:T(8,128)(2,1)}, bf16[576,8,16,128]{3,2,1,0:T(8,128)(2,1)}) custom-call(bf16[1024,1024]{1,0:T(8,128)(2,1)} %get-tuple-element.45.mix_ref.refs_5_, bf16[1024,1024]{1,0:T(8,128)(2,1)} %get-tuple-element.50.dmid_ref, bf16[768,8,16,128]{3,2,1,0:T(8,128)(2,1)} %bitcast.50, ...), custom_call_target="tpu_custom_call", output_to_operand_aliasing={{1}: (3, {})} | custom-call | flops 4300000256 | bytes 10000000 | tf_op jit(solution)/shard_map/out_back/pallas_call | solution.py:741
  317.6 9.4 %take_other.2 = bf16[6,2,192,16,128]{4,3,2,1,0:T(8,128)(2,1)} custom-call(s32[3]{0:T(128)} %pad_add_fusion.refs_0_, bf16[6,2,2,192,16,128]{5,4,3,2,1,0:T(8,128)(2,1)} %bitcast.53), custom_call_target="tpu_custom_call" | custom-call | bytes 6000000 | tf_op jit(solution)/shard_map/take_other/pallas_call | solution.py:833
  327.3 15.0 %attend_back.2 = (bf16[1024,1024]{1,0:T(8,128)(2,1)}, bf16[1024,1024]{1,0:T(8,128)(2,1)}, bf16[1024,1024]{1,0:T(8,128)(2,1)}) custom-call(s32[1]{0:T(128)S(6)} %copy.25.len_ref.refs_0_, bf16[1024,3072]{1,0:T(8,128)(2,1)} %get-tuple-element.44.q_ref.k_ref.v_ref.refs_1_.refs_2_.refs_3_, ...), custom_call_target="tpu_custom_call" | custom-call | flops 22000001024 | bytes 4000000 | tf_op jit(solution)/shard_map/attend_back/pallas_call | solution.py:537
  342.3 11.9 %core_sum.2 = (bf16[3,2,96,16,128]{4,3,2,1,0:T(8,128)(2,1)}, bf16[3,2,96,16,128]{4,3,2,1,0:T(8,128)(2,1)}, bf16[3,2,96,16,128]{4,3,2,1,0:T(8,128)(2,1)}, bf16[3,2,96,16,128]{4,3,2,1,0:T(8,128)(2,1)}) custom-call(s32[3]{0:T(128)} %pad_add_fusion.refs_0_, bf16[3,2,2,2,192,16,128]{6,5,4,3,2,1,0:T(8,128)(2,1)} %bitcast.54, ...), custom_call_target="tpu_custom_call" | custom-call | bytes 27000000 | tf_op jit(solution)/shard_map/core_sum/pallas_call | solution.py:833
  355.7 40.1 %attend_back.3 = (bf16[1024,1024]{1,0:T(8,128)(2,1)}, bf16[1024,1024]{1,0:T(8,128)(2,1)}, bf16[1024,1024]{1,0:T(8,128)(2,1)}) custom-call(s32[1]{0:T(128)S(6)} %copy.25.len_ref.refs_0_, bf16[1024,3072]{1,0:T(8,128)(2,1)} %get-tuple-element.44.q_ref.k_ref.v_ref.refs_1_.refs_2_.refs_3_, ...), custom_call_target="tpu_custom_call", output_to_operand_aliasing={{0}: (7, {}), {1}: (8, {}), {2}: (9, {})} | custom-call | flops 65999998976 | bytes 12000000 | tf_op jit(solution)/shard_map/attend_back/pallas_call | solution.py:537
  395.8 11.6 %qkv_weight_grad.1 = bf16[64,24,16,128]{3,2,1,0:T(8,128)(2,1)} custom-call(bf16[1024,1024]{1,0:T(8,128)(2,1)} %get-tuple-element.62.refs_0_, bf16[1024,1024]{1,0:T(8,128)(2,1)} %get-tuple-element.59.refs_1_.refs_3_, bf16[1024,1024]{1,0:T(8,128)(2,1)} %get-tuple-element.60.refs_2_.refs_4_, bf16[1024,1024]{1,0:T(8,128)(2,1)} %get-tuple-element.61.refs_3_.refs_5_), custom_call_target="tpu_custom_call" | custom-call | flops 6400000000 | bytes 15000000 | tf_op jit(solution)/shard_map/qkv_weight_grad/pallas_call | solution.py:773
  408.0 7.4 %plane_sum.2 = (bf16[3,96,16,128]{3,2,1,0:T(8,128)(2,1)}, bf16[3,96,16,128]{3,2,1,0:T(8,128)(2,1)}, bf16[3,96,16,128]{3,2,1,0:T(8,128)(2,1)}, bf16[3,96,16,128]{3,2,1,0:T(8,128)(2,1)}) custom-call(s32[3]{0:T(128)} %pad_add_fusion.refs_0_, bf16[3,2,96,16,128]{4,3,2,1,0:T(8,128)(2,1)} %get-tuple-element.63.refs_1_, ...), custom_call_target="tpu_custom_call" | custom-call | bytes 15000000 | tf_op jit(solution)/shard_map/plane_sum/pallas_call | solution.py:833
  415.3 3.9 take_other.3
  422.1 4.1 collective-permute-done.9.refs_2_
  426.2 5.8 %core_sum.3 = (bf16[1,2,96,16,128]{4,3,2,1,0:T(8,128)(2,1)}, bf16[1,2,96,16,128]{4,3,2,1,0:T(8,128)(2,1)}, bf16[1,2,96,16,128]{4,3,2,1,0:T(8,128)(2,1)}, bf16[1,2,96,16,128]{4,3,2,1,0:T(8,128)(2,1)}) custom-call(s32[3]{0:T(128)} %pad_add_fusion.refs_0_, bf16[1,2,2,2,192,16,128]{6,5,4,3,2,1,0:T(8,128)(2,1)} %bitcast.57, ...), custom_call_target="tpu_custom_call" | custom-call | bytes 9000000 | tf_op jit(solution)/shard_map/core_sum/pallas_call | solution.py:833
  433.5 15.2 %input_back.1 = (bf16[1024,1024]{1,0:T(8,128)(2,1)}, f32[2,1024]{1,0:T(2,128)}) custom-call(bf16[1024,1024]{1,0:T(8,128)(2,1)} %bitcast.60, f32[4,1024]{1,0:T(4,128)} %reshape.77.mod_ref.refs_1_, f32[1024,1024]{1,0:T(8,128)} %get-tuple-element.49.refs_2_, bf16[1024,1024]{1,0:T(8,128)(2,1)} %get-tuple-element.59.refs_1_.refs_3_, ...), custom_call_target="tpu_custom_call" | custom-call | flops 6400000000 | bytes 22000000 | tf_op jit(solution)/shard_map/input_back/pallas_call | solution.py:805
  449.8 5.3 line_sum.2.refs_5_
  460.1 5.3 collective-permute-done.10.refs_2_
  465.3 4.1 plane_sum.3
  477.7 5.0 collective-permute-start.19
  487.3 10.1 %collective-permute-done.19 = bf16[192,16,128]{2,1,0:T(8,128)(2,1)} collective-permute-done((bf16[192,16,128]{2,1,0:T(8,128)(2,1)}, bf16[192,16,128]{2,1,0:T(8,128)(2,1)}, u32[]{:S(2)}, u32[]{:S(2)}) %collective-permute-start.19) | collective-permute-done | bytes 786464 | tf_op jit(solution)/shard_map/ppermute | solution.py:1032
  500.2 4.1 collective-permute-start.20
  507.6 3.8 collective-permute-done.25
  512.1 9.6 %collective-permute-done.26 = f32[7,4096]{1,0:T(8,128)S(1)} collective-permute-done((f32[7,4096]{1,0:T(8,128)S(1)}, f32[7,4096]{1,0:T(8,128)S(1)}, u32[]{:S(2)}, u32[]{:S(2)}) %collective-permute-start.26) | collective-permute-done | bytes 114720 | tf_op jit(solution)/shard_map/ppermute | solution.py:921
  521.7 4.4 collective-permute-start.27
  526.1 16.5 %collective-permute-done.17 = bf16[192,16,128]{2,1,0:T(8,128)(2,1)} collective-permute-done((bf16[192,16,128]{2,1,0:T(8,128)(2,1)S(1)}, bf16[192,16,128]{2,1,0:T(8,128)(2,1)}, u32[]{:S(2)}, u32[]{:S(2)}) %collective-permute-start.17) | collective-permute-done | bytes 786464 | tf_op jit(solution)/shard_map/ppermute | solution.py:1032
  542.6 3.2 fusion.8.tiles_ref
  549.8 6.7 %collective-permute-start.28 = (f32[28672]{0:T(1024)S(1)}, f32[28672]{0:T(1024)S(1)}, u32[]{:S(2)}, u32[]{:S(2)}) collective-permute-start(f32[28672]{0:T(1024)S(1)} %slice_bitcast_fusion.2), channel_id=1, source_target_pairs={{1,0},{2,1},{3,2},{4,3},{5,4},{6,5},{7,6},{8,7},{9,8},{10,9},{11,1... | collective-permute-start | bytes 344072 | tf_op jit(solution)/shard_map/ppermute | solution.py:998
  558.1 6.8 %divide_subtract_fusion = (f32[394112]{0:T(1024)}, f32[394112]{0:T(1024)}, f32[394112]{0:T(1024)}, f32[394112]{0:T(1024)}) fusion(f32[394112]{0:T(1024)S(1)} %copy-done, f32[394112]{0:T(1024)} %param.11, f32[394112]{0:T(1024)} %param.12, s32[]{:T(128)S(6)} %select_n.83, f32[28672]{0:T(1024)S(1)} %broadcast_select_fusion, f32[393216]{0:T(1024)} %bitcast.63), kind=kLoop, calls=%fused_computation.7 | loop fusion | flops 5123456 | bytes 12722692 | tf_op jit(solution)/shard_map/sub | solution.py:1005
  (94 shorter events, 62.1 us)
Async XLA Ops:
  7.2 172.5 %all-gather.2.cloned.1.call-start = ((), (), s32[]{:S(2)}) async-start(), calls=%async_computation | async-start | bytes 25952256 | tf_op jit(solution)/shard_map/all_gather | solution.py:955
  8.1 6.3 %collective-permute-start.5 = (f32[28672]{0:T(1024)S(1)}, f32[28672]{0:T(1024)S(1)}, u32[]{:S(2)}, u32[]{:S(2)}) collective-permute-start(f32[28672]{0:T(1024)S(1)} %slice.16), channel_id=1, source_target_pairs={{0,1},{1,2},{2,3},{3,4},{4,5},{5,6},{6,7},{7,8},{8,9},{9,10},{10,1... | collective-permute-start | bytes 344072 | tf_op jit(solution)/shard_map/ppermute | solution.py:943
  21.3 1.3 collective-permute-start
  22.6 4.4 collective-permute-start.1
  27.0 3.6 collective-permute-start.2
  30.7 7.4 %collective-permute-start.3 = (bf16[7,4096]{1,0:T(8,128)(2,1)S(1)}, bf16[7,4096]{1,0:T(8,128)(2,1)S(1)}, u32[]{:S(2)}, u32[]{:S(2)}) collective-permute-start(bf16[7,4096]{1,0:T(8,128)(2,1)S(1)} %add.107), channel_id=1, source_target_pairs={{0,8},{1,9},{2,10},{3,11},{4,12},{5,13},{6,14},{7,15},{8,0},{9,1},... | collective-permute-start | bytes 172040 | tf_op jit(solution)/shard_map/ppermute | solution.py:921
  38.1 6.8 %collective-permute-start.4 = (bf16[7,4096]{1,0:T(8,128)(2,1)S(1)}, bf16[7,4096]{1,0:T(8,128)(2,1)S(1)}, u32[]{:S(2)}, u32[]{:S(2)}) collective-permute-start(bf16[7,4096]{1,0:T(8,128)(2,1)S(1)} %add.108), channel_id=1, source_target_pairs={{0,16},{1,17},{2,18},{3,19},{4,20},{5,21},{6,22},{7,23},{8,24},{9,... | collective-permute-start | bytes 172040 | tf_op jit(solution)/shard_map/ppermute | solution.py:921
  327.0 15.3 %collective-permute-start.6 = (bf16[3,2,2,192,16,128]{5,4,3,2,1,0:T(8,128)(2,1)}, bf16[3,2,2,192,16,128]{5,4,3,2,1,0:T(8,128)(2,1)}, u32[]{:S(2)}, u32[]{:S(2)}) collective-permute-start(bf16[3,2,2,192,16,128]{5,4,3,2,1,0:T(8,128)(2,1)} %bitcast.61), channel_id=1, source_target_pairs={{0,1},{1,0},{2,3},{3,2},{4,5},{5,4},{6,7},{7,6},{8,9},{9,8},{10,11... | collective-permute-start | bytes 28311560 | tf_op jit(solution)/shard_map/ppermute | solution.py:921
  354.2 53.2 %collective-permute-start.7 = (bf16[3,2,96,16,128]{4,3,2,1,0:T(8,128)(2,1)}, bf16[3,2,96,16,128]{4,3,2,1,0:T(8,128)(2,1)}, u32[]{:S(2)}, u32[]{:S(2)}) collective-permute-start(bf16[3,2,96,16,128]{4,3,2,1,0:T(8,128)(2,1)} %get-tuple-element.58.refs_10_), channel_id=1, source_target_pairs={{0,2},{1,3},{2,0},{3,1},{4,6},{5,7},{6,4},{7,5},{8,10},{9,11},{10,... | collective-permute-start | bytes 7077896 | tf_op jit(solution)/shard_map/ppermute | solution.py:921
  355.3 52.6 %collective-permute-start.8 = (bf16[3,2,96,16,128]{4,3,2,1,0:T(8,128)(2,1)}, bf16[3,2,96,16,128]{4,3,2,1,0:T(8,128)(2,1)}, u32[]{:S(2)}, u32[]{:S(2)}) collective-permute-start(bf16[3,2,96,16,128]{4,3,2,1,0:T(8,128)(2,1)} %get-tuple-element.65), channel_id=1, source_target_pairs={{0,4},{1,5},{2,6},{3,7},{4,0},{5,1},{6,2},{7,3},{8,12},{9,13},{10,... | collective-permute-start | bytes 7077896 | tf_op jit(solution)/shard_map/ppermute | solution.py:921
  419.3 7.0 %collective-permute-start.9 = (bf16[1,2,2,192,16,128]{5,4,3,2,1,0:T(8,128)(2,1)}, bf16[1,2,2,192,16,128]{5,4,3,2,1,0:T(8,128)(2,1)}, u32[]{:S(2)}, u32[]{:S(2)}) collective-permute-start(bf16[1,2,2,192,16,128]{5,4,3,2,1,0:T(8,128)(2,1)} %bitcast.65), channel_id=1, source_target_pairs={{0,1},{1,0},{2,3},{3,2},{4,5},{5,4},{6,7},{7,6},{8,9},{9,8},{10,11... | collective-permute-start | bytes 9437192 | tf_op jit(solution)/shard_map/ppermute | solution.py:921
  420.6 28.2 %collective-permute-start.12 = (bf16[3,96,16,128]{3,2,1,0:T(8,128)(2,1)}, bf16[3,96,16,128]{3,2,1,0:T(8,128)(2,1)S(1)}, u32[]{:S(2)}, u32[]{:S(2)}) collective-permute-start(bf16[3,96,16,128]{3,2,1,0:T(8,128)(2,1)} %get-tuple-element.66.refs_2_), channel_id=1, source_target_pairs={{0,4},{1,5},{2,6},{3,7},{4,0},{5,1},{6,2},{7,3},{8,12},{9,13},{10,... | collective-permute-start | bytes 3538952 | tf_op jit(solution)/shard_map/ppermute | solution.py:921
  420.9 27.9 %collective-permute-start.13 = (bf16[3,96,16,128]{3,2,1,0:T(8,128)(2,1)}, bf16[3,96,16,128]{3,2,1,0:T(8,128)(2,1)}, u32[]{:S(2)}, u32[]{:S(2)}) collective-permute-start(bf16[3,96,16,128]{3,2,1,0:T(8,128)(2,1)} %get-tuple-element.74), channel_id=1, source_target_pairs={{0,2},{1,3},{2,0},{3,1},{4,6},{5,7},{6,4},{7,5},{8,10},{9,11},{10,... | collective-permute-start | bytes 3538952 | tf_op jit(solution)/shard_map/ppermute | solution.py:921
  432.0 33.3 %collective-permute-start.10 = (bf16[1,2,96,16,128]{4,3,2,1,0:T(8,128)(2,1)}, bf16[1,2,96,16,128]{4,3,2,1,0:T(8,128)(2,1)}, u32[]{:S(2)}, u32[]{:S(2)}) collective-permute-start(bf16[1,2,96,16,128]{4,3,2,1,0:T(8,128)(2,1)} %get-tuple-element.67.refs_7_), channel_id=1, source_target_pairs={{0,2},{1,3},{2,0},{3,1},{4,6},{5,7},{6,4},{7,5},{8,10},{9,11},{10,... | collective-permute-start | bytes 2359304 | tf_op jit(solution)/shard_map/ppermute | solution.py:921
  432.4 33.0 %collective-permute-start.11 = (bf16[1,2,96,16,128]{4,3,2,1,0:T(8,128)(2,1)}, bf16[1,2,96,16,128]{4,3,2,1,0:T(8,128)(2,1)}, u32[]{:S(2)}, u32[]{:S(2)}) collective-permute-start(bf16[1,2,96,16,128]{4,3,2,1,0:T(8,128)(2,1)} %get-tuple-element.71), channel_id=1, source_target_pairs={{0,4},{1,5},{2,6},{3,7},{4,0},{5,1},{6,2},{7,3},{8,12},{9,13},{10,... | collective-permute-start | bytes 2359304 | tf_op jit(solution)/shard_map/ppermute | solution.py:921
  457.9 17.7 %collective-permute-start.18 = (bf16[192,16,128]{2,1,0:T(8,128)(2,1)}, bf16[192,16,128]{2,1,0:T(8,128)(2,1)S(1)}, u32[]{:S(2)}, u32[]{:S(2)}) collective-permute-start(bf16[192,16,128]{2,1,0:T(8,128)(2,1)} %get-tuple-element.87), channel_id=1, source_target_pairs={{0,8},{1,9},{2,10},{3,11},{4,12},{5,13},{6,14},{7,15}} | collective-permute-start | bytes 2359304 | tf_op jit(solution)/shard_map/ppermute | solution.py:1032
  459.3 28.0 %collective-permute-start.21 = (bf16[192,16,128]{2,1,0:T(8,128)(2,1)}, bf16[192,16,128]{2,1,0:T(8,128)(2,1)S(1)}, u32[]{:S(2)}, u32[]{:S(2)}) collective-permute-start(bf16[192,16,128]{2,1,0:T(8,128)(2,1)} %get-tuple-element.88), channel_id=1, source_target_pairs={{24,16},{25,17},{26,18},{27,19},{28,20},{29,21},{30,22},{31,23}} | collective-permute-start | bytes 2359304 | tf_op jit(solution)/shard_map/ppermute | solution.py:1032
  469.4 13.3 %collective-permute-start.14 = (bf16[1,96,16,128]{3,2,1,0:T(8,128)(2,1)}, bf16[1,96,16,128]{3,2,1,0:T(8,128)(2,1)}, u32[]{:S(2)}, u32[]{:S(2)}) collective-permute-start(bf16[1,96,16,128]{3,2,1,0:T(8,128)(2,1)} %get-tuple-element.76), channel_id=1, source_target_pairs={{0,4},{1,5},{2,6},{3,7},{4,0},{5,1},{6,2},{7,3},{8,12},{9,13},{10,... | collective-permute-start | bytes 1179656 | tf_op jit(solution)/shard_map/ppermute | solution.py:921
  470.5 12.2 %collective-permute-start.15 = (bf16[1,96,16,128]{3,2,1,0:T(8,128)(2,1)}, bf16[1,96,16,128]{3,2,1,0:T(8,128)(2,1)}, u32[]{:S(2)}, u32[]{:S(2)}) collective-permute-start(bf16[1,96,16,128]{3,2,1,0:T(8,128)(2,1)} %get-tuple-element.78), channel_id=1, source_target_pairs={{0,2},{1,3},{2,0},{3,1},{4,6},{5,7},{6,4},{7,5},{8,10},{9,11},{10,... | collective-permute-start | bytes 1179656 | tf_op jit(solution)/shard_map/ppermute | solution.py:921
  470.9 16.1 %collective-permute-start.23 = (f32[7,4096]{1,0:T(8,128)S(1)}, f32[7,4096]{1,0:T(8,128)S(1)}, u32[]{:S(2)}, u32[]{:S(2)}) collective-permute-start(f32[7,4096]{1,0:T(8,128)S(1)} %broadcast_multiply_fusion), channel_id=1, source_target_pairs={{0,1},{1,0},{2,3},{3,2},{4,5},{5,4},{6,7},{7,6},{8,9},{9,8},{10,11... | collective-permute-start | bytes 344072 | tf_op jit(solution)/shard_map/ppermute | solution.py:921
  477.7 19.6 %collective-permute-start.19 = (bf16[192,16,128]{2,1,0:T(8,128)(2,1)}, bf16[192,16,128]{2,1,0:T(8,128)(2,1)}, u32[]{:S(2)}, u32[]{:S(2)}) collective-permute-start(bf16[192,16,128]{2,1,0:T(8,128)(2,1)} %fusion.5), channel_id=1, source_target_pairs={{0,8},{1,9},{2,10},{3,11},{4,12},{5,13},{6,14},{7,15},{8,16},{9,17... | collective-permute-start | bytes 2359304 | tf_op jit(solution)/shard_map/ppermute | solution.py:1032
  485.8 20.1 %collective-permute-start.16 = (bf16[192,16,128]{2,1,0:T(8,128)(2,1)}, bf16[192,16,128]{2,1,0:T(8,128)(2,1)S(1)}, u32[]{:S(2)}, u32[]{:S(2)}) collective-permute-start(bf16[192,16,128]{2,1,0:T(8,128)(2,1)} %bitcast.64), channel_id=1, source_target_pairs={{24,16},{25,17},{26,18},{27,19},{28,20},{29,21},{30,22},{31,23},{8... | collective-permute-start | bytes 2359304 | tf_op jit(solution)/shard_map/ppermute | solution.py:1032
  487.2 18.8 %copy-start.1 = (bf16[1,192,16,128]{3,2,1,0:T(8,128)(2,1)S(1)}, bf16[1,192,16,128]{3,2,1,0:T(8,128)(2,1)}, u32[]{:S(2)}) copy-start(bf16[1,192,16,128]{3,2,1,0:T(8,128)(2,1)} %line_sum.3) | copy-start | bytes 2359300
  487.2 20.3 %collective-permute-start.24 = (f32[7,4096]{1,0:T(8,128)S(1)}, f32[7,4096]{1,0:T(8,128)S(1)}, u32[]{:S(2)}, u32[]{:S(2)}) collective-permute-start(f32[7,4096]{1,0:T(8,128)S(1)} %fusion.9), channel_id=1, source_target_pairs={{0,2},{1,3},{2,0},{3,1},{4,6},{5,7},{6,4},{7,5},{8,10},{9,11},{10,... | collective-permute-start | bytes 344072 | tf_op jit(solution)/shard_map/ppermute | solution.py:921
  500.2 25.9 %collective-permute-start.20 = (bf16[192,16,128]{2,1,0:T(8,128)(2,1)}, bf16[192,16,128]{2,1,0:T(8,128)(2,1)S(1)}, u32[]{:S(2)}, u32[]{:S(2)}) collective-permute-start(bf16[192,16,128]{2,1,0:T(8,128)(2,1)} %get-tuple-element.85), channel_id=1, source_target_pairs={{0,8},{1,9},{2,10},{3,11},{4,12},{5,13},{6,14},{7,15},{8,16},{9,17... | collective-permute-start | bytes 2359304 | tf_op jit(solution)/shard_map/ppermute | solution.py:1032
  504.4 21.7 %collective-permute-start.22 = (bf16[192,16,128]{2,1,0:T(8,128)(2,1)S(1)}, bf16[192,16,128]{2,1,0:T(8,128)(2,1)}, u32[]{:S(2)}, u32[]{:S(2)}) collective-permute-start(bf16[192,16,128]{2,1,0:T(8,128)(2,1)S(1)} %get-tuple-element.86), channel_id=1, source_target_pairs={{24,16},{25,17},{26,18},{27,19},{28,20},{29,21},{30,22},{31,23},{1... | collective-permute-start | bytes 2359304 | tf_op jit(solution)/shard_map/ppermute | solution.py:1032
  506.1 36.4 %collective-permute-start.17 = (bf16[192,16,128]{2,1,0:T(8,128)(2,1)S(1)}, bf16[192,16,128]{2,1,0:T(8,128)(2,1)}, u32[]{:S(2)}, u32[]{:S(2)}) collective-permute-start(bf16[192,16,128]{2,1,0:T(8,128)(2,1)S(1)} %add_convert_fusion), channel_id=1, source_target_pairs={{16,0},{17,1},{18,2},{19,3},{20,4},{21,5},{22,6},{23,7}} | collective-permute-start | bytes 2359304 | tf_op jit(solution)/shard_map/ppermute | solution.py:1032
  507.5 3.9 collective-permute-start.25
  511.4 10.2 %collective-permute-start.26 = (f32[7,4096]{1,0:T(8,128)S(1)}, f32[7,4096]{1,0:T(8,128)S(1)}, u32[]{:S(2)}, u32[]{:S(2)}) collective-permute-start(f32[7,4096]{1,0:T(8,128)S(1)} %add.126), channel_id=1, source_target_pairs={{0,8},{1,9},{2,10},{3,11},{4,12},{5,13},{6,14},{7,15},{8,0},{9,1},... | collective-permute-start | bytes 344072 | tf_op jit(solution)/shard_map/ppermute | solution.py:921
  521.7 34.8 %collective-permute-start.27 = (f32[7,4096]{1,0:T(8,128)S(1)}, f32[7,4096]{1,0:T(8,128)S(1)}, u32[]{:S(2)}, u32[]{:S(2)}) collective-permute-start(f32[7,4096]{1,0:T(8,128)S(1)} %add.127), channel_id=1, source_target_pairs={{0,16},{1,17},{2,18},{3,19},{4,20},{5,21},{6,22},{7,23},{8,24},{9,... | collective-permute-start | bytes 344072 | tf_op jit(solution)/shard_map/ppermute | solution.py:921
  545.8 12.3 %copy-start = (f32[394112]{0:T(1024)S(1)}, f32[394112]{0:T(1024)}, u32[]{:S(2)}) copy-start(f32[394112]{0:T(1024)} %param.10) | copy-start | bytes 4729348
  549.8 8.3 %collective-permute-start.28 = (f32[28672]{0:T(1024)S(1)}, f32[28672]{0:T(1024)S(1)}, u32[]{:S(2)}, u32[]{:S(2)}) collective-permute-start(f32[28672]{0:T(1024)S(1)} %slice_bitcast_fusion.2), channel_id=1, source_target_pairs={{1,0},{2,1},{3,2},{4,3},{5,4},{6,5},{7,6},{8,7},{9,8},{10,9},{11,1... | collective-permute-start | bytes 344072 | tf_op jit(solution)/shard_map/ppermute | solution.py:998
  (6 other events, 36.5 us)
Sparse Core Ops, SparseCore 0:
  20.4 159.2 all-gather.1

commit v5 on v4

--- a/solution.py
+++ b/solution.py
@@ -900,17 +900,32 @@
     )
 
 
-def line_kernel(sel, one_own, one_moved, two_own, two_moved, out_ref):
-    out_ref[0, 0:96] = both(one_own[0], one_moved[0])
-    out_ref[0, 96:192] = both(two_own[0], two_moved[0])
+def line_kernel(sel, one_own, one_moved, two_own, two_moved, *outs):
+    for layer, out_ref in enumerate(outs):
+
+        @pl.when(pl.program_id(0) == layer)
+        def _():
+            out_ref[0:96] = both(one_own[0], one_moved[0])
+            out_ref[96:192] = both(two_own[0], two_moved[0])
 
 
 def line_sum(sel, *values, waits=()):
     layers = values[0].shape[0]
     spec = tile_spec(1, 96, index=lambda i, at: (i, 0))
-    return staged(
-        line_kernel, "line_sum", 1, (1, 192), values, [spec] * 4, sel, layers, 2.4e6 * layers, waits
-    )[0]
+    whole = tile_spec(192, index=lambda i, at: (0,))
+    return pl.pallas_call(
+        without(line_kernel, 1 + len(values), len(waits)),
+        out_shape=(jax.ShapeDtypeStruct((192, TILE, LANES), BF),) * layers,
+        grid_spec=pltpu.PrefetchScalarGridSpec(
+            num_scalar_prefetch=1,
+            grid=(layers,),
+            in_specs=[spec] * 4 + [ANYWHERE] * len(waits),
+            out_specs=(whole,) * layers,
+        ),
+        compiler_params=params_of("arbitrary"),
+        cost_estimate=cost(0, 2.4e6 * layers),
+        name="line_sum",
+    )(sel, *values, *waits)
 
 
 def flat_index():
@@ -983,7 +998,7 @@
     input_grad, dmod_one = input_back(x, mod, dmid, dq, dk, dv, tiles, (one_send,))
     rest = line_sum(sel, *held, waits=(input_grad,))
     one_send, one_keep, two_send, two_keep = plane_sum(
-        sel, one_keep, one_moved, two_keep, two_moved, waits=(rest,)
+        sel, one_keep, one_moved, two_keep, two_moved, waits=(rest[0],)
     )
     one_moved, two_moved = exchange(one_send, 4, count), exchange(two_send, 2, count)
     first = line_sum(sel, one_keep, one_moved, two_keep, two_moved)
@@ -1043,7 +1058,7 @@
 
 def reduce_rest(value, index, count):
     layer = index // 8
-    choose = lambda at: pick(value, jnp.clip(at, 0, 2), 0)
+    choose = lambda at: jnp.where(at <= 0, value[0], jnp.where(at == 1, value[1], value[2]))
     up = layer_move(value[2], [(0, 1)])
     down = layer_move(value[0], [(3, 2)])
     up = layer_move(add_low(choose(1 + layer), up), [(0, 1), (1, 2)])

time: 580 us -> 582 us (level)
  starting transfers between devices: 50.6 us -> 57.4 us
    pallas_call x0 -> x2, Pallas kernels: none -> 8.45 us  [line_sum(): pl.pallas_call(without(line_kernel, 1 + len(values), len(waits)), out_sha...]
    pallas_call x8 -> x6, Pallas kernels: 50.7 us -> 42.5 us  [staged(): pl.pallas_call(without(kernel, 1 + len(ins), len(waits)), out_shape=(jax....]
    ppermute x7, waiting for transfers between devices: 29.4 us -> 23.3 us  [layer_move(): return lax.ppermute(value, ('dp', 'fsdp'), pairs)]
    ppermute x20, starting transfers between devices: 24 us -> 29.8 us  [exchange(): lax.ppermute(value, ('dp', 'fsdp'), [(i, i ^ mask) for i in range(count)])]
  transfers between devices with their start and end apart: 30 -> 30, of which waited for: 16 -> 17; matrix products, arithmetic and copies ran while one was open for 3% -> 3% of each run, Pallas kernels for 18% -> 18%
where the time goes in v5:
time: 582 us; the launch traced here: 574 us
  Pallas kernels  277 us (48%)
  waiting for transfers between devices  198 us (34%)
  starting transfers between devices  57.4 us (10%)
  other arithmetic  23.1 us (4%)
  between operations  16.1 us (3%)
    all_gather x1, waiting for transfers between devices, fast_device(): tiles = lax.all_gather(packed, ('dp', 'fsdp'), axis=0, tiled=True)  134 us
    pallas_call x1, Pallas kernels, ffn_both(): pl.pallas_call(ffn_kernel, grid=(steps,), out_shape=(jax.ShapeDtypeStruct...  73.6 us
    pallas_call x2, Pallas kernels, attend_back(): pl.pallas_call(without(attend_back_kernel, 7, len(kept) + len(waits)), gr...  55.1 us
    pallas_call x6, Pallas kernels, staged(): pl.pallas_call(without(kernel, 1 + len(ins), len(waits)), out_shape=(jax....  42.5 us
    pallas_call x1, Pallas kernels, attend(): pl.pallas_call(attend_kernel, grid=(pairs,), out_shape=(jax.ShapeDtypeStr...  35.7 us
    ppermute x20, waiting for transfers between devices, exchange(): lax.ppermute(value, ('dp', 'fsdp'), [(i, i ^ mask) for i in range(count)])  35.3 us
    ppermute x20, starting transfers between devices, exchange(): lax.ppermute(value, ('dp', 'fsdp'), [(i, i ^ mask) for i in range(count)])  29.8 us
    ppermute x7, waiting for transfers between devices, layer_move(): return lax.ppermute(value, ('dp', 'fsdp'), pairs)  23.3 us
  transfers between devices with their start and end apart: 30, of which 17 were waited for; matrix products, arithmetic and copies ran while one was open for 3% of the time, Pallas kernels for 18%

profile of v5, /device:TPU:1, one launch (start us, length us, event | category | flops | bytes accessed | tf_op | source)
XLA Modules:
  0.0 574.4 jit_solution(12979059510515065402)
XLA Ops:
  8.1 4.5 collective-permute-start.5
  33.3 4.8 collective-permute-done.3
  41.3 3.6 collective-permute-done.4
  45.6 134.0 %all-gather.2.cloned.1.call-done = bf16[6144,16,128]{2,1,0:T(8,128)(2,1)} async-done(((bf16[192,16,128]{2,1,0:T(8,128)(2,1)}), bf16[6144,16,128]{2,1,0:T(8,128)(2,1)}) %all-gather.2.cloned.1.call-update) | async-done | bytes 25165840 | tf_op jit(solution)/shard_map/all_gather | solution.py:970
  179.6 12.9 %project_qkv.1 = (bf16[1024,1024]{1,0:T(8,128)(2,1)}, bf16[1024,3072]{1,0:T(8,128)(2,1)}) custom-call(bf16[1024,1024]{1,0:T(8,128)(2,1)} %bitcast.40, f32[4,1024]{1,0:T(4,128)} %reshape.69.mod_ref.refs_1_, bf16[256,24,16,128]{3,2,1,0:T(8,128)(2,1)} %bitcast.28), custom_call_target="tpu_custom_call" | custom-call | flops 6400000000 | bytes 18000000 | tf_op jit(solution)/shard_map/project_qkv/pallas_call | solution.py:396
  192.6 35.7 %attend.1 = (bf16[1024,1024]{1,0:T(8,128)(2,1)}, f32[8,2,1024]{2,1,0:T(2,128)}) custom-call(s32[1]{0:T(128)S(6)} %copy.25.len_ref.refs_0_, bf16[1024,3072]{1,0:T(8,128)(2,1)} %get-tuple-element.47.q_ref.k_ref.v_ref.refs_1_.refs_2_.refs_3_, bf16[1024,3072]{1,0:T(8,128)(2,1)} %get-tuple-element.47.q_ref.k_ref.v_ref.refs_1_.refs_2_.refs_3_, ...), custom_call_target="tpu_custom_call" | custom-call | flops 16999999488 | bytes 8000000 | tf_op jit(solution)/shard_map/attend/pallas_call | solution.py:471
  228.3 7.4 %middle_rows.1 = (f32[1024,1024]{1,0:T(8,128)}, bf16[1024,1024]{1,0:T(8,128)(2,1)}) custom-call(bf16[1024,1024]{1,0:T(8,128)(2,1)} %bitcast.41, f32[4,1024]{1,0:T(4,128)} %reshape.69.mod_ref.refs_1_, bf16[1024,1024]{1,0:T(8,128)(2,1)} %get-tuple-element.48.mix_ref.refs_5_, bf16[768,8,16,128]{3,2,1,0:T(8,128)(2,1)} %bitcast.29), custom_call_target="tpu_custom_call" | custom-call | flops 2200000000 | bytes 12000000 | tf_op jit(solution)/shard_map/middle_rows/pallas_call | solution.py:570
  235.7 73.6 %ffn_both.1 = (bf16[1024,1024]{1,0:T(8,128)(2,1)}, f32[1024,1024]{1,0:T(8,128)}, bf16[1024,1024]{1,0:T(8,128)(2,1)}, f32[2,1024]{1,0:T(2,128)}, bf16[144,32,16,128]{3,2,1,0:T(8,128)(2,1)}) custom-call(f32[1024,1024]{1,0:T(8,128)} %get-tuple-element.49.mid_ref, f32[4,1024]{1,0:T(4,128)} %reshape.69.mod_ref.refs_1_, ...), custom_call_target="tpu_custom_call" | custom-call | flops 51999997952 | bytes 60000000 | tf_op jit(solution)/shard_map/ffn_both/pallas_call | solution.py:689
  309.3 8.5 %out_back.1 = (bf16[1024,1024]{1,0:T(8,128)(2,1)}, bf16[576,8,16,128]{3,2,1,0:T(8,128)(2,1)}) custom-call(bf16[1024,1024]{1,0:T(8,128)(2,1)} %get-tuple-element.48.mix_ref.refs_5_, bf16[1024,1024]{1,0:T(8,128)(2,1)} %get-tuple-element.53.dmid_ref, bf16[768,8,16,128]{3,2,1,0:T(8,128)(2,1)} %bitcast.32, ...), custom_call_target="tpu_custom_call", output_to_operand_aliasing={{1}: (3, {})} | custom-call | flops 4300000256 | bytes 10000000 | tf_op jit(solution)/shard_map/out_back/pallas_call | solution.py:741
  317.7 9.4 %take_other.2 = bf16[6,2,192,16,128]{4,3,2,1,0:T(8,128)(2,1)} custom-call(s32[3]{0:T(128)} %pad_add_fusion.refs_0_, bf16[6,2,2,192,16,128]{5,4,3,2,1,0:T(8,128)(2,1)} %bitcast.35), custom_call_target="tpu_custom_call" | custom-call | bytes 6000000 | tf_op jit(solution)/shard_map/take_other/pallas_call | solution.py:833
  327.4 15.0 %attend_back.2 = (bf16[1024,1024]{1,0:T(8,128)(2,1)}, bf16[1024,1024]{1,0:T(8,128)(2,1)}, bf16[1024,1024]{1,0:T(8,128)(2,1)}) custom-call(s32[1]{0:T(128)S(6)} %copy.25.len_ref.refs_0_, bf16[1024,3072]{1,0:T(8,128)(2,1)} %get-tuple-element.47.q_ref.k_ref.v_ref.refs_1_.refs_2_.refs_3_, ...), custom_call_target="tpu_custom_call" | custom-call | flops 22000001024 | bytes 4000000 | tf_op jit(solution)/shard_map/attend_back/pallas_call | solution.py:537
  342.4 11.8 %core_sum.2 = (bf16[3,2,96,16,128]{4,3,2,1,0:T(8,128)(2,1)}, bf16[3,2,96,16,128]{4,3,2,1,0:T(8,128)(2,1)}, bf16[3,2,96,16,128]{4,3,2,1,0:T(8,128)(2,1)}, bf16[3,2,96,16,128]{4,3,2,1,0:T(8,128)(2,1)}) custom-call(s32[3]{0:T(128)} %pad_add_fusion.refs_0_, bf16[3,2,2,2,192,16,128]{6,5,4,3,2,1,0:T(8,128)(2,1)} %bitcast.36, ...), custom_call_target="tpu_custom_call" | custom-call | bytes 27000000 | tf_op jit(solution)/shard_map/core_sum/pallas_call | solution.py:833
  355.7 40.1 %attend_back.3 = (bf16[1024,1024]{1,0:T(8,128)(2,1)}, bf16[1024,1024]{1,0:T(8,128)(2,1)}, bf16[1024,1024]{1,0:T(8,128)(2,1)}) custom-call(s32[1]{0:T(128)S(6)} %copy.25.len_ref.refs_0_, bf16[1024,3072]{1,0:T(8,128)(2,1)} %get-tuple-element.47.q_ref.k_ref.v_ref.refs_1_.refs_2_.refs_3_, ...), custom_call_target="tpu_custom_call", output_to_operand_aliasing={{0}: (7, {}), {1}: (8, {}), {2}: (9, {})} | custom-call | flops 65999998976 | bytes 12000000 | tf_op jit(solution)/shard_map/attend_back/pallas_call | solution.py:537
  395.8 11.6 %qkv_weight_grad.1 = bf16[64,24,16,128]{3,2,1,0:T(8,128)(2,1)} custom-call(bf16[1024,1024]{1,0:T(8,128)(2,1)} %get-tuple-element.65.refs_0_, bf16[1024,1024]{1,0:T(8,128)(2,1)} %get-tuple-element.62.refs_1_.refs_3_, bf16[1024,1024]{1,0:T(8,128)(2,1)} %get-tuple-element.63.refs_2_.refs_4_, bf16[1024,1024]{1,0:T(8,128)(2,1)} %get-tuple-element.64.refs_3_.refs_5_), custom_call_target="tpu_custom_call" | custom-call | flops 6400000000 | bytes 15000000 | tf_op jit(solution)/shard_map/qkv_weight_grad/pallas_call | solution.py:773
  408.0 7.4 %plane_sum.2 = (bf16[3,96,16,128]{3,2,1,0:T(8,128)(2,1)}, bf16[3,96,16,128]{3,2,1,0:T(8,128)(2,1)}, bf16[3,96,16,128]{3,2,1,0:T(8,128)(2,1)}, bf16[3,96,16,128]{3,2,1,0:T(8,128)(2,1)}) custom-call(s32[3]{0:T(128)} %pad_add_fusion.refs_0_, bf16[3,2,96,16,128]{4,3,2,1,0:T(8,128)(2,1)} %get-tuple-element.66.refs_1_, ...), custom_call_target="tpu_custom_call" | custom-call | bytes 15000000 | tf_op jit(solution)/shard_map/plane_sum/pallas_call | solution.py:833
  415.4 4.0 take_other.3
  422.3 4.1 collective-permute-done.9.refs_2_
  426.4 5.8 %core_sum.3 = (bf16[1,2,96,16,128]{4,3,2,1,0:T(8,128)(2,1)}, bf16[1,2,96,16,128]{4,3,2,1,0:T(8,128)(2,1)}, bf16[1,2,96,16,128]{4,3,2,1,0:T(8,128)(2,1)}, bf16[1,2,96,16,128]{4,3,2,1,0:T(8,128)(2,1)}) custom-call(s32[3]{0:T(128)} %pad_add_fusion.refs_0_, bf16[1,2,2,2,192,16,128]{6,5,4,3,2,1,0:T(8,128)(2,1)} %bitcast.39, ...), custom_call_target="tpu_custom_call" | custom-call | bytes 9000000 | tf_op jit(solution)/shard_map/core_sum/pallas_call | solution.py:833
  433.7 15.2 %input_back.1 = (bf16[1024,1024]{1,0:T(8,128)(2,1)}, f32[2,1024]{1,0:T(2,128)}) custom-call(bf16[1024,1024]{1,0:T(8,128)(2,1)} %bitcast.42, f32[4,1024]{1,0:T(4,128)} %reshape.69.mod_ref.refs_1_, f32[1024,1024]{1,0:T(8,128)} %get-tuple-element.52.refs_2_, bf16[1024,1024]{1,0:T(8,128)(2,1)} %get-tuple-element.62.refs_1_.refs_3_, ...), custom_call_target="tpu_custom_call" | custom-call | flops 6400000000 | bytes 22000000 | tf_op jit(solution)/shard_map/input_back/pallas_call | solution.py:805
  449.0 5.4 line_sum.2
  458.2 7.3 %collective-permute-done.10.refs_2_ = bf16[1,2,96,16,128]{4,3,2,1,0:T(8,128)(2,1)S(1)} collective-permute-done((bf16[1,2,96,16,128]{4,3,2,1,0:T(8,128)(2,1)}, bf16[1,2,96,16,128]{4,3,2,1,0:T(8,128)(2,1)S(1)}, u32[]{:S(2)}, u32[]{:S(2)}) %collective-permute-start.10) | collective-permute-done | bytes 786464 | tf_op jit(solution)/shard_map/ppermute | solution.py:936
  466.4 4.0 plane_sum.3
  486.1 6.8 %collective-permute-done.19 = bf16[192,16,128]{2,1,0:T(8,128)(2,1)} collective-permute-done((bf16[192,16,128]{2,1,0:T(8,128)(2,1)}, bf16[192,16,128]{2,1,0:T(8,128)(2,1)}, u32[]{:S(2)}, u32[]{:S(2)}) %collective-permute-start.19) | collective-permute-done | bytes 786464 | tf_op jit(solution)/shard_map/ppermute | solution.py:1047
  493.0 3.4 add_convert_fusion.1
  496.4 6.1 %collective-permute-start.20 = (bf16[192,16,128]{2,1,0:T(8,128)(2,1)}, bf16[192,16,128]{2,1,0:T(8,128)(2,1)}, u32[]{:S(2)}, u32[]{:S(2)}) collective-permute-start(bf16[192,16,128]{2,1,0:T(8,128)(2,1)} %get-tuple-element.91), channel_id=1, source_target_pairs={{0,8},{1,9},{2,10},{3,11},{4,12},{5,13},{6,14},{7,15},{8,16},{9,17... | collective-permute-start | bytes 2359304 | tf_op jit(solution)/shard_map/ppermute | solution.py:1047
  512.5 6.9 %collective-permute-done.26 = f32[7,4096]{1,0:T(8,128)S(1)} collective-permute-done((f32[7,4096]{1,0:T(8,128)S(1)}, f32[7,4096]{1,0:T(8,128)S(1)}, u32[]{:S(2)}, u32[]{:S(2)}) %collective-permute-start.26) | collective-permute-done | bytes 114720 | tf_op jit(solution)/shard_map/ppermute | solution.py:936
  519.4 7.0 %collective-permute-start.27 = (f32[7,4096]{1,0:T(8,128)S(1)}, f32[7,4096]{1,0:T(8,128)S(1)}, u32[]{:S(2)}, u32[]{:S(2)}) collective-permute-start(f32[7,4096]{1,0:T(8,128)S(1)} %add.122), channel_id=1, source_target_pairs={{0,16},{1,17},{2,18},{3,19},{4,20},{5,21},{6,22},{7,23},{8,24},{9,... | collective-permute-start | bytes 344072 | tf_op jit(solution)/shard_map/ppermute | solution.py:936
  526.4 16.5 %collective-permute-done.17 = bf16[192,16,128]{2,1,0:T(8,128)(2,1)} collective-permute-done((bf16[192,16,128]{2,1,0:T(8,128)(2,1)}, bf16[192,16,128]{2,1,0:T(8,128)(2,1)}, u32[]{:S(2)}, u32[]{:S(2)}) %collective-permute-start.17) | collective-permute-done | bytes 786464 | tf_op jit(solution)/shard_map/ppermute | solution.py:1047
  542.9 3.6 add_select_fusion.tiles_ref
  550.6 5.9 %collective-permute-start.28 = (f32[28672]{0:T(1024)S(1)}, f32[28672]{0:T(1024)S(1)}, u32[]{:S(2)}, u32[]{:S(2)}) collective-permute-start(f32[28672]{0:T(1024)S(1)} %slice_bitcast_fusion), channel_id=1, source_target_pairs={{1,0},{2,1},{3,2},{4,3},{5,4},{6,5},{7,6},{8,7},{9,8},{10,9},{11,1... | collective-permute-start | bytes 344072 | tf_op jit(solution)/shard_map/ppermute | solution.py:1013
  556.6 3.7 collective-permute-done.28
  560.3 6.8 %divide_subtract_fusion = (f32[394112]{0:T(1024)}, f32[394112]{0:T(1024)}, f32[394112]{0:T(1024)}, f32[394112]{0:T(1024)}) fusion(f32[394112]{0:T(1024)S(1)} %copy-done.3, f32[394112]{0:T(1024)} %param.11, f32[394112]{0:T(1024)} %param.12, s32[]{:T(128)S(6)} %select_n.144, f32[28672]{0:T(1024)S(1)} %broadcast_select_fusion, f32[393216]{0:T(1024)} %bitcast.45), kind=kLoop, calls=%fused_computation.7 | loop fusion | flops 5123456 | bytes 12722692 | tf_op jit(solution)/shard_map/sub | solution.py:1020
  (101 shorter events, 65.4 us)
Async XLA Ops:
  7.2 172.5 %all-gather.2.cloned.1.call-start = ((), (), s32[]{:S(2)}) async-start(), calls=%async_computation | async-start | bytes 25952256 | tf_op jit(solution)/shard_map/all_gather | solution.py:970
  8.1 6.3 %collective-permute-start.5 = (f32[28672]{0:T(1024)S(1)}, f32[28672]{0:T(1024)S(1)}, u32[]{:S(2)}, u32[]{:S(2)}) collective-permute-start(f32[28672]{0:T(1024)S(1)} %slice.10), channel_id=1, source_target_pairs={{0,1},{1,2},{2,3},{3,4},{4,5},{5,6},{6,7},{7,8},{8,9},{9,10},{10,1... | collective-permute-start | bytes 344072 | tf_op jit(solution)/shard_map/ppermute | solution.py:958
  21.3 1.3 collective-permute-start
  22.6 4.4 collective-permute-start.1
  27.0 3.6 collective-permute-start.2
  30.7 7.4 %collective-permute-start.3 = (bf16[7,4096]{1,0:T(8,128)(2,1)S(1)}, bf16[7,4096]{1,0:T(8,128)(2,1)S(1)}, u32[]{:S(2)}, u32[]{:S(2)}) collective-permute-start(bf16[7,4096]{1,0:T(8,128)(2,1)S(1)} %add.102), channel_id=1, source_target_pairs={{0,8},{1,9},{2,10},{3,11},{4,12},{5,13},{6,14},{7,15},{8,0},{9,1},... | collective-permute-start | bytes 172040 | tf_op jit(solution)/shard_map/ppermute | solution.py:936
  38.1 6.8 %collective-permute-start.4 = (bf16[7,4096]{1,0:T(8,128)(2,1)S(1)}, bf16[7,4096]{1,0:T(8,128)(2,1)S(1)}, u32[]{:S(2)}, u32[]{:S(2)}) collective-permute-start(bf16[7,4096]{1,0:T(8,128)(2,1)S(1)} %add.103), channel_id=1, source_target_pairs={{0,16},{1,17},{2,18},{3,19},{4,20},{5,21},{6,22},{7,23},{8,24},{9,... | collective-permute-start | bytes 172040 | tf_op jit(solution)/shard_map/ppermute | solution.py:936
  327.1 15.3 %collective-permute-start.6 = (bf16[3,2,2,192,16,128]{5,4,3,2,1,0:T(8,128)(2,1)}, bf16[3,2,2,192,16,128]{5,4,3,2,1,0:T(8,128)(2,1)}, u32[]{:S(2)}, u32[]{:S(2)}) collective-permute-start(bf16[3,2,2,192,16,128]{5,4,3,2,1,0:T(8,128)(2,1)} %bitcast.43), channel_id=1, source_target_pairs={{0,1},{1,0},{2,3},{3,2},{4,5},{5,4},{6,7},{7,6},{8,9},{9,8},{10,11... | collective-permute-start | bytes 28311560 | tf_op jit(solution)/shard_map/ppermute | solution.py:936
  354.2 53.2 %collective-permute-start.7 = (bf16[3,2,96,16,128]{4,3,2,1,0:T(8,128)(2,1)}, bf16[3,2,96,16,128]{4,3,2,1,0:T(8,128)(2,1)}, u32[]{:S(2)}, u32[]{:S(2)}) collective-permute-start(bf16[3,2,96,16,128]{4,3,2,1,0:T(8,128)(2,1)} %get-tuple-element.61.refs_10_), channel_id=1, source_target_pairs={{0,2},{1,3},{2,0},{3,1},{4,6},{5,7},{6,4},{7,5},{8,10},{9,11},{10,... | collective-permute-start | bytes 7077896 | tf_op jit(solution)/shard_map/ppermute | solution.py:936
  355.4 52.6 %collective-permute-start.8 = (bf16[3,2,96,16,128]{4,3,2,1,0:T(8,128)(2,1)}, bf16[3,2,96,16,128]{4,3,2,1,0:T(8,128)(2,1)}, u32[]{:S(2)}, u32[]{:S(2)}) collective-permute-start(bf16[3,2,96,16,128]{4,3,2,1,0:T(8,128)(2,1)} %get-tuple-element.68), channel_id=1, source_target_pairs={{0,4},{1,5},{2,6},{3,7},{4,0},{5,1},{6,2},{7,3},{8,12},{9,13},{10,... | collective-permute-start | bytes 7077896 | tf_op jit(solution)/shard_map/ppermute | solution.py:936
  419.4 7.0 %collective-permute-start.9 = (bf16[1,2,2,192,16,128]{5,4,3,2,1,0:T(8,128)(2,1)}, bf16[1,2,2,192,16,128]{5,4,3,2,1,0:T(8,128)(2,1)}, u32[]{:S(2)}, u32[]{:S(2)}) collective-permute-start(bf16[1,2,2,192,16,128]{5,4,3,2,1,0:T(8,128)(2,1)} %bitcast.46), channel_id=1, source_target_pairs={{0,1},{1,0},{2,3},{3,2},{4,5},{5,4},{6,7},{7,6},{8,9},{9,8},{10,11... | collective-permute-start | bytes 9437192 | tf_op jit(solution)/shard_map/ppermute | solution.py:936
  420.8 28.2 %collective-permute-start.12 = (bf16[3,96,16,128]{3,2,1,0:T(8,128)(2,1)S(1)}, bf16[3,96,16,128]{3,2,1,0:T(8,128)(2,1)}, u32[]{:S(2)}, u32[]{:S(2)}) collective-permute-start(bf16[3,96,16,128]{3,2,1,0:T(8,128)(2,1)S(1)} %copy-done.5), channel_id=1, source_target_pairs={{0,4},{1,5},{2,6},{3,7},{4,0},{5,1},{6,2},{7,3},{8,12},{9,13},{10,... | collective-permute-start | bytes 3538952 | tf_op jit(solution)/shard_map/ppermute | solution.py:936
  421.1 27.9 %collective-permute-start.13 = (bf16[3,96,16,128]{3,2,1,0:T(8,128)(2,1)}, bf16[3,96,16,128]{3,2,1,0:T(8,128)(2,1)}, u32[]{:S(2)}, u32[]{:S(2)}) collective-permute-start(bf16[3,96,16,128]{3,2,1,0:T(8,128)(2,1)} %get-tuple-element.77), channel_id=1, source_target_pairs={{0,2},{1,3},{2,0},{3,1},{4,6},{5,7},{6,4},{7,5},{8,10},{9,11},{10,... | collective-permute-start | bytes 3538952 | tf_op jit(solution)/shard_map/ppermute | solution.py:936
  432.2 33.3 %collective-permute-start.10 = (bf16[1,2,96,16,128]{4,3,2,1,0:T(8,128)(2,1)}, bf16[1,2,96,16,128]{4,3,2,1,0:T(8,128)(2,1)S(1)}, u32[]{:S(2)}, u32[]{:S(2)}) collective-permute-start(bf16[1,2,96,16,128]{4,3,2,1,0:T(8,128)(2,1)} %get-tuple-element.70.refs_7_), channel_id=1, source_target_pairs={{0,2},{1,3},{2,0},{3,1},{4,6},{5,7},{6,4},{7,5},{8,10},{9,11},{10,... | collective-permute-start | bytes 2359304 | tf_op jit(solution)/shard_map/ppermute | solution.py:936
  432.6 33.0 %collective-permute-start.11 = (bf16[1,2,96,16,128]{4,3,2,1,0:T(8,128)(2,1)}, bf16[1,2,96,16,128]{4,3,2,1,0:T(8,128)(2,1)}, u32[]{:S(2)}, u32[]{:S(2)}) collective-permute-start(bf16[1,2,96,16,128]{4,3,2,1,0:T(8,128)(2,1)} %get-tuple-element.74), channel_id=1, source_target_pairs={{0,4},{1,5},{2,6},{3,7},{4,0},{5,1},{6,2},{7,3},{8,12},{9,13},{10,... | collective-permute-start | bytes 2359304 | tf_op jit(solution)/shard_map/ppermute | solution.py:936
  454.4 19.3 %collective-permute-start.18 = (bf16[192,16,128]{2,1,0:T(8,128)(2,1)}, bf16[192,16,128]{2,1,0:T(8,128)(2,1)}, u32[]{:S(2)}, u32[]{:S(2)}) collective-permute-start(bf16[192,16,128]{2,1,0:T(8,128)(2,1)} %get-tuple-element.84), channel_id=1, source_target_pairs={{0,8},{1,9},{2,10},{3,11},{4,12},{5,13},{6,14},{7,15}} | collective-permute-start | bytes 2359304 | tf_op jit(solution)/shard_map/ppermute | solution.py:1047
  456.7 29.5 %collective-permute-start.21 = (bf16[192,16,128]{2,1,0:T(8,128)(2,1)}, bf16[192,16,128]{2,1,0:T(8,128)(2,1)}, u32[]{:S(2)}, u32[]{:S(2)}) collective-permute-start(bf16[192,16,128]{2,1,0:T(8,128)(2,1)} %get-tuple-element.78.refs_5_), channel_id=1, source_target_pairs={{24,16},{25,17},{26,18},{27,19},{28,20},{29,21},{30,22},{31,23}} | collective-permute-start | bytes 2359304 | tf_op jit(solution)/shard_map/ppermute | solution.py:1047
  470.4 10.0 %collective-permute-start.14 = (bf16[1,96,16,128]{3,2,1,0:T(8,128)(2,1)}, bf16[1,96,16,128]{3,2,1,0:T(8,128)(2,1)}, u32[]{:S(2)}, u32[]{:S(2)}) collective-permute-start(bf16[1,96,16,128]{3,2,1,0:T(8,128)(2,1)} %get-tuple-element.80), channel_id=1, source_target_pairs={{0,4},{1,5},{2,6},{3,7},{4,0},{5,1},{6,2},{7,3},{8,12},{9,13},{10,... | collective-permute-start | bytes 1179656 | tf_op jit(solution)/shard_map/ppermute | solution.py:936
  471.5 9.6 %collective-permute-start.15 = (bf16[1,96,16,128]{3,2,1,0:T(8,128)(2,1)}, bf16[1,96,16,128]{3,2,1,0:T(8,128)(2,1)}, u32[]{:S(2)}, u32[]{:S(2)}) collective-permute-start(bf16[1,96,16,128]{3,2,1,0:T(8,128)(2,1)} %get-tuple-element.82), channel_id=1, source_target_pairs={{0,2},{1,3},{2,0},{3,1},{4,6},{5,7},{6,4},{7,5},{8,10},{9,11},{10,... | collective-permute-start | bytes 1179656 | tf_op jit(solution)/shard_map/ppermute | solution.py:936
  472.0 13.4 %collective-permute-start.23 = (f32[7,4096]{1,0:T(8,128)S(1)}, f32[7,4096]{1,0:T(8,128)S(1)}, u32[]{:S(2)}, u32[]{:S(2)}) collective-permute-start(f32[7,4096]{1,0:T(8,128)S(1)} %broadcast_multiply_fusion), channel_id=1, source_target_pairs={{0,1},{1,0},{2,3},{3,2},{4,5},{5,4},{6,7},{7,6},{8,9},{9,8},{10,11... | collective-permute-start | bytes 344072 | tf_op jit(solution)/shard_map/ppermute | solution.py:936
  476.1 16.9 %collective-permute-start.19 = (bf16[192,16,128]{2,1,0:T(8,128)(2,1)}, bf16[192,16,128]{2,1,0:T(8,128)(2,1)}, u32[]{:S(2)}, u32[]{:S(2)}) collective-permute-start(bf16[192,16,128]{2,1,0:T(8,128)(2,1)} %add_convert_fusion.2), channel_id=1, source_target_pairs={{0,8},{1,9},{2,10},{3,11},{4,12},{5,13},{6,14},{7,15},{8,16},{9,17... | collective-permute-start | bytes 2359304 | tf_op jit(solution)/shard_map/ppermute | solution.py:1047
  484.1 20.0 %collective-permute-start.16 = (bf16[192,16,128]{2,1,0:T(8,128)(2,1)}, bf16[192,16,128]{2,1,0:T(8,128)(2,1)S(1)}, u32[]{:S(2)}, u32[]{:S(2)}) collective-permute-start(bf16[192,16,128]{2,1,0:T(8,128)(2,1)} %line_sum.3), channel_id=1, source_target_pairs={{24,16},{25,17},{26,18},{27,19},{28,20},{29,21},{30,22},{31,23},{8... | collective-permute-start | bytes 2359304 | tf_op jit(solution)/shard_map/ppermute | solution.py:1047
  485.5 18.7 %copy-start.4 = (bf16[192,16,128]{2,1,0:T(8,128)(2,1)S(1)}, bf16[192,16,128]{2,1,0:T(8,128)(2,1)}, u32[]{:S(2)}) copy-start(bf16[192,16,128]{2,1,0:T(8,128)(2,1)} %line_sum.3) | copy-start | bytes 2359300
  485.5 21.0 %collective-permute-start.24 = (f32[7,4096]{1,0:T(8,128)S(1)}, f32[7,4096]{1,0:T(8,128)S(1)}, u32[]{:S(2)}, u32[]{:S(2)}) collective-permute-start(f32[7,4096]{1,0:T(8,128)S(1)} %fusion.4), channel_id=1, source_target_pairs={{0,2},{1,3},{2,0},{3,1},{4,6},{5,7},{6,4},{7,5},{8,10},{9,11},{10,... | collective-permute-start | bytes 344072 | tf_op jit(solution)/shard_map/ppermute | solution.py:936
  496.4 30.1 %collective-permute-start.20 = (bf16[192,16,128]{2,1,0:T(8,128)(2,1)}, bf16[192,16,128]{2,1,0:T(8,128)(2,1)}, u32[]{:S(2)}, u32[]{:S(2)}) collective-permute-start(bf16[192,16,128]{2,1,0:T(8,128)(2,1)} %get-tuple-element.91), channel_id=1, source_target_pairs={{0,8},{1,9},{2,10},{3,11},{4,12},{5,13},{6,14},{7,15},{8,16},{9,17... | collective-permute-start | bytes 2359304 | tf_op jit(solution)/shard_map/ppermute | solution.py:1047
  502.5 40.4 %copy-start.2 = (bf16[192,16,128]{2,1,0:T(8,128)(2,1)S(1)}, bf16[192,16,128]{2,1,0:T(8,128)(2,1)}, u32[]{:S(2)}) copy-start(bf16[192,16,128]{2,1,0:T(8,128)(2,1)} %get-tuple-element.84) | copy-start | bytes 2359300
  502.5 23.9 %collective-permute-start.22 = (bf16[192,16,128]{2,1,0:T(8,128)(2,1)}, bf16[192,16,128]{2,1,0:T(8,128)(2,1)}, u32[]{:S(2)}, u32[]{:S(2)}) collective-permute-start(bf16[192,16,128]{2,1,0:T(8,128)(2,1)} %get-tuple-element.92), channel_id=1, source_target_pairs={{24,16},{25,17},{26,18},{27,19},{28,20},{29,21},{30,22},{31,23},{1... | collective-permute-start | bytes 2359304 | tf_op jit(solution)/shard_map/ppermute | solution.py:1047
  505.3 37.7 %collective-permute-start.17 = (bf16[192,16,128]{2,1,0:T(8,128)(2,1)}, bf16[192,16,128]{2,1,0:T(8,128)(2,1)}, u32[]{:S(2)}, u32[]{:S(2)}) collective-permute-start(bf16[192,16,128]{2,1,0:T(8,128)(2,1)} %add_convert_fusion.3), channel_id=1, source_target_pairs={{16,0},{17,1},{18,2},{19,3},{20,4},{21,5},{22,6},{23,7}} | collective-permute-start | bytes 2359304 | tf_op jit(solution)/shard_map/ppermute | solution.py:1047
  506.7 4.0 collective-permute-start.25
  510.7 8.7 %collective-permute-start.26 = (f32[7,4096]{1,0:T(8,128)S(1)}, f32[7,4096]{1,0:T(8,128)S(1)}, u32[]{:S(2)}, u32[]{:S(2)}) collective-permute-start(f32[7,4096]{1,0:T(8,128)S(1)} %add.121), channel_id=1, source_target_pairs={{0,8},{1,9},{2,10},{3,11},{4,12},{5,13},{6,14},{7,15},{8,0},{9,1},... | collective-permute-start | bytes 344072 | tf_op jit(solution)/shard_map/ppermute | solution.py:936
  519.4 37.1 %collective-permute-start.27 = (f32[7,4096]{1,0:T(8,128)S(1)}, f32[7,4096]{1,0:T(8,128)S(1)}, u32[]{:S(2)}, u32[]{:S(2)}) collective-permute-start(f32[7,4096]{1,0:T(8,128)S(1)} %add.122), channel_id=1, source_target_pairs={{0,16},{1,17},{2,18},{3,19},{4,20},{5,21},{6,22},{7,23},{8,24},{9,... | collective-permute-start | bytes 344072 | tf_op jit(solution)/shard_map/ppermute | solution.py:936
  550.6 9.7 %collective-permute-start.28 = (f32[28672]{0:T(1024)S(1)}, f32[28672]{0:T(1024)S(1)}, u32[]{:S(2)}, u32[]{:S(2)}) collective-permute-start(f32[28672]{0:T(1024)S(1)} %slice_bitcast_fusion), channel_id=1, source_target_pairs={{1,0},{2,1},{3,2},{4,3},{5,4},{6,5},{7,6},{8,7},{9,8},{10,9},{11,1... | collective-permute-start | bytes 344072 | tf_op jit(solution)/shard_map/ppermute | solution.py:1013
  (10 other events, 80.8 us)
Sparse Core Ops, SparseCore 0:
  20.4 159.2 all-gather.1
